TPU v7x, 32 devices: a whole 2x2x4 slice. The times are simulated.
32 devices in a mesh: group: 2 (over y), member: 16 (over z, x, core).
Axes of the slice: x: 2, y: 2, z: 4, core: 2. Of those that a mesh axis runs over, the one named last changes fastest.
Arguments:
- rows: float32 [16384, 1024], P(('group', 'member'))
- old_list: int32 [16384], P(('group', 'member')), may hold values from 0 to 63
- old_centroids: float32 [64, 1024], replicated, may hold values from -6 to 6
- dest_device: int32 [16384, 1], P(('group', 'member')), may hold values from 0 to 31; in each aligned block of 512 rows (0 to 511, 512 to 1023, ...) at most 32 rows name the same one
- new_local: int32 [16384], P(('group', 'member')), may hold values from 0 to 1
- centroids: float32 [4, 1024], P('group'), may hold values from -6 to 6
Outputs:
- whitened: float32 [32768, 1024], P(('group', 'member'))
- factors: float32 [4, 1024, 1024], P('group')
Inputs may be any that keep to these rules, and one draw needn't show every extreme that they name: `dest_device`: among the rows of one device, no destination is named by more than 32 rows, a bound that some block reaches.
All inputs are finite; a program needn't handle non-finite values.
Results may differ from a plain program's by a relative error of at most 0.0003.
Values sent between devices are 32-bit elements; how exact they have to be, the bound alone decides.
No kernel may reach another device: no remote copies, remote signals or barrier semaphores. Data moves between devices by JAX's collectives and lax.ppermute only.
A program may use at most 128 MiB of HBM per device.

v0:
```python
import jax
import jax.numpy as jnp
from jax import lax
from jax.sharding import PartitionSpec as P

ridge = 0.1


def on_device(rows, old_list, old_centroids, dest_device, new_local, centroids):
    n_group = lax.axis_size("group")
    n_member = lax.axis_size("member")
    devices = n_group * n_member
    row_dev = rows.shape[0]
    width = rows.shape[1]
    capacity = max(2, 2 * row_dev // devices)
    old_hot = (
        old_list[:, None] == jnp.arange(old_centroids.shape[0], dtype=jnp.int32)[None, :]
    ).astype(jnp.float32)
    vectors = rows + jnp.dot(old_hot, old_centroids, precision=lax.Precision.HIGHEST)
    dest = dest_device[:, 0]
    onehot = (dest[:, None] == jnp.arange(devices, dtype=jnp.int32)[None, :]).astype(jnp.int32)
    ranks = jnp.sum(jnp.cumsum(onehot, axis=0) * onehot, axis=1) - 1
    position = dest * capacity + ranks
    outgoing = jnp.zeros((devices * capacity, width), jnp.float32).at[position].set(vectors)
    out_tags = jnp.zeros((devices * capacity,), jnp.int32).at[position].set(new_local + 1)
    arrived, in_tags = (
        lax.all_to_all(
            outgoing.reshape(devices, capacity, width),
            ("group", "member"),
            split_axis=0,
            concat_axis=0,
            tiled=True,
        ),
        lax.all_to_all(
            out_tags.reshape(devices, capacity),
            ("group", "member"),
            split_axis=0,
            concat_axis=0,
            tiled=True,
        ),
    )
    flat = arrived.reshape(devices * capacity, width)
    flat_tags = in_tags.reshape(-1)
    lists = centroids.shape[0]
    select = (flat_tags[:, None] == jnp.arange(1, lists + 1, dtype=jnp.int32)[None, :]).astype(
        jnp.float32
    )
    residual = jnp.where(
        flat_tags[:, None] > 0,
        flat - jnp.dot(select, centroids, precision=lax.Precision.HIGHEST),
        0.0,
    )
    partial_grams = []
    for j in range(lists):
        masked = residual * select[:, j : j + 1]
        partial_grams.append(
            lax.dot_general(
                masked, masked, (((0,), (0,)), ((), ())), precision=lax.Precision.HIGHEST
            )
        )
    stacked = jnp.stack(partial_grams)
    local_counts = jnp.sum(select, axis=0)
    identity = ridge * jnp.eye(width, dtype=jnp.float32)
    summed, counts = lax.psum((stacked, local_counts), "member")
    covs = summed / jnp.maximum(counts, 1.0)[:, None, None] + identity[None]
    factors = jax.vmap(jnp.linalg.cholesky)(covs)
    result = jnp.zeros_like(residual)
    for j in range(lists):
        solved = jax.scipy.linalg.solve_triangular(factors[j], residual.T, lower=True).T
        result = result + select[:, j : j + 1] * solved
    return (result, factors)


def solution(mesh):
    return jax.shard_map(
        on_device,
        mesh=mesh,
        in_specs=(
            P(("group", "member"), None),
            P(("group", "member")),
            P(),
            P(("group", "member"), None),
            P(("group", "member")),
            P("group", None),
        ),
        out_specs=(P(("group", "member"), None), P("group", None, None)),
        check_vma=False,
    )
```

profile of v0, /device:TPU:0, one launch (start us, length us, event | category | flops | bytes accessed | tf_op | source)
XLA Modules:
  0.0 1048.0 jit_solution(9774520813117248683)
XLA Ops:
  14.6 7.3 all-to-all-start
  23.7 5.7 scatter_custom_fusion.1
  29.4 6.0 all-to-all-start.1
  37.3 93.2 %all-to-all-done.1 = f32[32,32,1024]{2,1,0:T(8,128)} async-done(((f32[32,32,1024]{2,1,0:T(8,128)}), f32[32,32,1024]{2,1,0:T(8,128)}, u32[]{:S(2)}, u32[]{:S(2)}) %all-to-all-start.1) | async-done | bytes 4194336 | tf_op jit(solution)/shard_map/all_to_all | solution.py:27
  130.5 4.9 fusion.3
  135.4 16.0 %fusion.9 = f32[1,1024,1024]{1,2,0:T(8,128)S(1)} fusion(f32[1024,1024]{1,0:T(8,128)S(1)} %fusion.3, f32[1024]{0:T(1024)S(1)} %bitcast.236), kind=kOutput, calls=%fused_computation.25 | convolution fusion | flops 12885950464 | bytes 8392704 | tf_op jit(solution)/shard_map/dot_general | solution.py:57
  151.4 16.1 %fusion.12 = f32[1,1024,1024]{1,2,0:T(8,128)S(1)} fusion(f32[1024,1024]{1,0:T(8,128)S(1)} %fusion.3, f32[1024]{0:T(1024)S(1)} %bitcast.238), kind=kOutput, calls=%fused_computation.26 | convolution fusion | flops 12885950464 | bytes 8392704 | tf_op jit(solution)/shard_map/dot_general | solution.py:57
  167.5 4.2 pad_maximum_fusion
  175.3 5.4 copy.50
  180.6 31.6 %psum.15 = f32[2]{0:T(128)S(1)} all-reduce(f32[2]{0:T(128)S(1)} %fusion.159), channel_id=1, replica_groups=mesh['group'=2,'member'=16] {'member'}, use_global_device_ids=true, to_apply=%region_7.8 | all-reduce | flops 2 | bytes 16 | tf_op jit(solution)/shard_map/psum | solution.py:64
  212.2 126.9 %all-reduce.3.cloned.1.call-done = f32[2,1024,1024]{1,2,0:T(8,128)} async-done(((f32[2,1024,1024]{1,2,0:T(8,128)}), f32[2,1024,1024]{1,2,0:T(8,128)}) %all-reduce.3.cloned.1.call-update) | async-done | bytes 8388624 | tf_op jit(solution)/shard_map/psum | solution.py:64
  339.1 10.6 %divide_add_fusion = f32[2,1024,1024]{1,2,0:T(8,128)} fusion(f32[2,1024,1024]{1,2,0:T(8,128)} %all-reduce.3.cloned.1.call-done, f32[1024,1024]{0,1:T(8,128)} %copy.50, f32[2]{0:T(128)S(1)} %broadcast_maximum_fusion), kind=kLoop, calls=%fused_computation.10 | loop fusion | flops 4194304 | bytes 20971528 | tf_op jit(solution)/shard_map/add | solution.py:65
  349.7 8.7 copy.51
  358.4 8.4 fusion
  370.0 23.5 %custom-call.70 = f32[2,128,128]{2,1,0:T(8,128)S(1)} custom-call(f32[2,128,128]{2,1,0:T(8,128)S(1)} %cholesky.578), custom_call_target="Cholesky" | custom-call | tf_op jit(solution)/shard_map/vmap(jit(cholesky))/cholesky | solution.py:66
  393.5 19.7 %custom-call.71 = f32[2,1,128,128]{2,3,1,0:T(8,128)S(1)} custom-call(f32[2,1,128,128]{3,2,1,0:T(8,128)S(1)} %select_bitcast_fusion.6), custom_call_target="InvertDiagBlocksLowerTriangular" | custom-call | tf_op jit(solution)/shard_map/vmap(jit(cholesky))/cholesky | solution.py:66
  413.2 4.5 cholesky.253
  422.8 23.6 %custom-call.72 = f32[2,128,128]{2,1,0:T(8,128)S(1)} custom-call(f32[2,128,128]{2,1,0:T(8,128)S(1)} %cholesky.582), custom_call_target="Cholesky" | custom-call | tf_op jit(solution)/shard_map/vmap(jit(cholesky))/cholesky | solution.py:66
  447.1 19.7 %custom-call.73 = f32[2,1,128,128]{2,3,1,0:T(8,128)S(1)} custom-call(f32[2,1,128,128]{3,2,1,0:T(8,128)S(1)} %get-tuple-element.116), custom_call_target="InvertDiagBlocksLowerTriangular" | custom-call | tf_op jit(solution)/shard_map/vmap(jit(cholesky))/cholesky | solution.py:66
  471.7 23.7 %custom-call.74 = f32[2,128,128]{2,1,0:T(8,128)S(1)} custom-call(f32[2,128,128]{2,1,0:T(8,128)S(1)} %cholesky.587), custom_call_target="Cholesky" | custom-call | tf_op jit(solution)/shard_map/vmap(jit(cholesky))/cholesky | solution.py:66
  496.0 19.7 %custom-call.75 = f32[2,1,128,128]{2,3,1,0:T(8,128)S(1)} custom-call(f32[2,1,128,128]{3,2,1,0:T(8,128)S(1)} %get-tuple-element.114), custom_call_target="InvertDiagBlocksLowerTriangular" | custom-call | tf_op jit(solution)/shard_map/vmap(jit(cholesky))/cholesky | solution.py:66
  520.9 23.9 %custom-call.76 = f32[2,128,128]{2,1,0:T(8,128)S(1)} custom-call(f32[2,128,128]{2,1,0:T(8,128)S(1)} %cholesky.592), custom_call_target="Cholesky" | custom-call | tf_op jit(solution)/shard_map/vmap(jit(cholesky))/cholesky | solution.py:66
  545.4 19.7 %custom-call.77 = f32[2,1,128,128]{2,3,1,0:T(8,128)S(1)} custom-call(f32[2,1,128,128]{3,2,1,0:T(8,128)S(1)} %get-tuple-element.112), custom_call_target="InvertDiagBlocksLowerTriangular" | custom-call | tf_op jit(solution)/shard_map/vmap(jit(cholesky))/cholesky | solution.py:66
  566.5 3.8 fusion.76
  570.3 23.5 %custom-call.78 = f32[2,128,128]{2,1,0:T(8,128)S(1)} custom-call(f32[2,128,128]{2,1,0:T(8,128)S(1)} %cholesky.597), custom_call_target="Cholesky" | custom-call | tf_op jit(solution)/shard_map/vmap(jit(cholesky))/cholesky | solution.py:66
  594.4 19.8 %custom-call.79 = f32[2,1,128,128]{2,3,1,0:T(8,128)S(1)} custom-call(f32[2,1,128,128]{3,2,1,0:T(8,128)S(1)} %get-tuple-element.110), custom_call_target="InvertDiagBlocksLowerTriangular" | custom-call | tf_op jit(solution)/shard_map/vmap(jit(cholesky))/cholesky | solution.py:66
  619.1 23.5 %custom-call.80 = f32[2,128,128]{2,1,0:T(8,128)S(1)} custom-call(f32[2,128,128]{2,1,0:T(8,128)S(1)} %cholesky.602), custom_call_target="Cholesky" | custom-call | tf_op jit(solution)/shard_map/vmap(jit(cholesky))/cholesky | solution.py:66
  643.2 19.9 %custom-call.81 = f32[2,1,128,128]{2,3,1,0:T(8,128)S(1)} custom-call(f32[2,1,128,128]{3,2,1,0:T(8,128)S(1)} %get-tuple-element.108), custom_call_target="InvertDiagBlocksLowerTriangular" | custom-call | tf_op jit(solution)/shard_map/vmap(jit(cholesky))/cholesky | solution.py:66
  667.4 23.5 %custom-call.82 = f32[2,128,128]{2,1,0:T(8,128)S(1)} custom-call(f32[2,128,128]{2,1,0:T(8,128)S(1)} %cholesky.607), custom_call_target="Cholesky" | custom-call | tf_op jit(solution)/shard_map/vmap(jit(cholesky))/cholesky | solution.py:66
  691.5 19.7 %custom-call.83 = f32[2,1,128,128]{2,3,1,0:T(8,128)S(1)} custom-call(f32[2,1,128,128]{3,2,1,0:T(8,128)S(1)} %get-tuple-element.106), custom_call_target="InvertDiagBlocksLowerTriangular" | custom-call | tf_op jit(solution)/shard_map/vmap(jit(cholesky))/cholesky | solution.py:66
  714.7 23.9 %custom-call.84 = f32[2,128,128]{2,1,0:T(8,128)S(1)} custom-call(f32[2,128,128]{2,1,0:T(8,128)S(1)} %convolution_subtract_fusion.11), custom_call_target="Cholesky" | custom-call | tf_op jit(solution)/shard_map/vmap(jit(cholesky))/cholesky | solution.py:66
  739.9 4.7 select_select_fusion
  744.7 4.6 fusion.2
  750.6 22.5 %while.4 = (s32[]{:T(128)}, f32[1024,1024]{1,0:T(8,128)}, s32[8,2]{0,1:T(2,128)S(1)}, f32[8,128,128]{2,1,0:T(8,128)S(1)}, s32[]{:T(128)}) while((s32[]{:T(128)}, f32[1024,1024]{1,0:T(8,128)}, s32[8,2]{0,1:T(2,128)S(1)}, f32[8,128,128]{2,1,0:T(8,128)S(1)}, s32[]{:T(128)}) %tuple.110), condition=%wide.while_cond, body=%wide.while_body.sunk | while | flops 2 | bytes 131181 | solution.py:69
  773.1 78.8 %custom-call.86 = f32[8,128,128]{1,2,0:T(8,128)S(1)} custom-call(f32[8,128,128]{2,1,0:T(8,128)S(1)} %get-tuple-element.17), custom_call_target="InvertDiagBlocksLowerTriangular" | custom-call | tf_op jit(solution)/shard_map/jit(_solve_triangular)/triangular_solve | solution.py:69
  860.2 3.7 fusion.67
  864.7 4.5 fusion.73
  870.3 5.4 convolution_subtract_fusion.6
  876.4 6.1 convolution_subtract_fusion.4
  883.2 7.7 convolution_subtract_fusion.9
  890.9 22.8 %while.5 = (s32[]{:T(128)}, f32[1024,1024]{1,0:T(8,128)}, s32[8,2]{0,1:T(2,128)S(1)}, f32[8,128,128]{2,1,0:T(8,128)S(1)}, s32[]{:T(128)}) while((s32[]{:T(128)}, f32[1024,1024]{1,0:T(8,128)}, s32[8,2]{0,1:T(2,128)S(1)}, f32[8,128,128]{2,1,0:T(8,128)S(1)}, s32[]{:T(128)}) %tuple.115), condition=%wide.while_cond.clone, body=%wide.while_body.clone.sunk | while | flops 2 | bytes 131181 | solution.py:69
  913.8 78.6 %custom-call.87 = f32[8,128,128]{1,2,0:T(8,128)S(1)} custom-call(f32[8,128,128]{2,1,0:T(8,128)S(1)} %get-tuple-element.18), custom_call_target="InvertDiagBlocksLowerTriangular" | custom-call | tf_op jit(solution)/shard_map/jit(_solve_triangular)/triangular_solve | solution.py:69
  1000.7 3.7 fusion.64
  1005.2 4.5 fusion.70
  1010.8 5.4 convolution_subtract_fusion.5
  1016.9 6.1 convolution_subtract_fusion.3
  1023.7 7.6 convolution_subtract_fusion.7
  1035.6 5.3 copy.80
  (154 shorter events, 126.0 us)
Async XLA Ops:
  7.2 14.8 %copy-start = (f32[64,1024]{1,0:T(8,128)S(1)}, f32[64,1024]{1,0:T(8,128)}, u32[]{:S(2)}) copy-start(f32[64,1024]{1,0:T(8,128)} %param.10) | copy-start | bytes 786436
  14.6 14.8 %all-to-all-start = ((s32[32,1,32]{2,1,0:T(1,128)}), s32[32,1,32]{2,1,0:T(1,128)S(1)}, u32[]{:S(2)}, u32[]{:S(2)}) async-start(s32[32,1,32]{2,1,0:T(1,128)} %all_to_all.9), calls=%async_computation | async-start | bytes 32768 | tf_op jit(solution)/shard_map/all_to_all | solution.py:34
  29.4 101.1 %copy-start.9 = (f32[2,1024]{1,0:T(2,128)S(1)}, f32[2,1024]{1,0:T(2,128)}, u32[]{:S(2)}) copy-start(f32[2,1024]{1,0:T(2,128)} %param.13) | copy-start | bytes 24580
  29.4 101.1 %all-to-all-start.1 = ((f32[32,32,1024]{2,1,0:T(8,128)}), f32[32,32,1024]{2,1,0:T(8,128)}, u32[]{:S(2)}, u32[]{:S(2)}) async-start(f32[32,32,1024]{2,1,0:T(8,128)} %bitcast.233), calls=%async_computation.1 | async-start | bytes 8388608 | tf_op jit(solution)/shard_map/all_to_all | solution.py:27
  35.4 303.7 %all-reduce.3.cloned.1.call-start = ((), (), s32[]{:S(2)}) async-start(), calls=%async_computation.2 | async-start | bytes 16777216 | tf_op jit(solution)/shard_map/psum | solution.py:64
  135.4 16.0 %copy-start.3 = (f32[1024,1024]{1,0:T(8,128)}, f32[1024,1024]{1,0:T(8,128)S(1)}, u32[]{:S(2)}) copy-start(f32[1024,1024]{1,0:T(8,128)S(1)} %fusion.3) | copy-start | bytes 12582916
  366.8 3.2 copy-start.6
  744.7 5.9 copy-start.2
  851.9 4.8 copy-start.4
  883.2 7.7 copy-start.7
  992.4 4.8 copy-start.5
  1023.0 8.3 copy-start.8
  1032.7 8.3 copy-start.1
Sparse Core Ops, SparseCore 0:
  171.9 167.1 all-reduce.2
where the time goes:
time: 1050 us
  other arithmetic  539 us (51%)
  waiting for transfers between devices  220 us (21%)
  matrix products  151 us (14%)
  local copies, waits for them, and re-layouts  77.5 us (7%)
  blocking collectives  31.6 us (3%)
  between operations  14.9 us (1%)
  starting transfers between devices  13.8 us (1%)
    another operation x30, other arithmetic, on_device(): factors = jax.vmap(jnp.linalg.cholesky)(covs)  332 us
    another operation x5, other arithmetic, on_device(): jax.scipy.linalg.solve_triangular(factors[j], residual.T, lower=True)  162 us
    psum x1, waiting for transfers between devices, on_device(): summed, counts = lax.psum((stacked, local_counts), 'member')  127 us
    all_to_all x1, waiting for transfers between devices, on_device(): lax.all_to_all(outgoing.reshape(devices, capacity, width), ('group', 'mem...  93.2 us
    another operation x30, matrix products, on_device(): jax.scipy.linalg.solve_triangular(factors[j], residual.T, lower=True)  79 us
    another operation x51, local copies, waits for them, and re-layouts, on_device(): jax.scipy.linalg.solve_triangular(factors[j], residual.T, lower=True)  45.1 us
    another operation x14, matrix products, on_device(): factors = jax.vmap(jnp.linalg.cholesky)(covs)  32.9 us
    dot_general x2, matrix products, on_device(): lax.dot_general(masked, masked, (((0,), (0,)), ((), ())), precision=lax.P...  32.1 us
  transfers between devices with their start and end apart: 3, of which 2 were waited for; matrix products, arithmetic and copies ran while one was open for 2% of the time, Pallas kernels for 0%

commit v1 on v0

v1 whole, which is shorter than its diff:
```python
import jax
import jax.numpy as jnp
from jax import lax
from jax.experimental import pallas as pl
from jax.experimental.pallas import tpu as pltpu
from jax.sharding import PartitionSpec as P

ridge = 0.1
f32 = jnp.float32
bf16 = jnp.bfloat16
BL = 128
SUB = 8


def split(x):
    hi = x.astype(bf16)
    return hi, (x - hi.astype(f32)).astype(bf16)


def dot_nt(a, b):
    return lax.dot_general(a, b, (((1,), (1,)), ((), ())), preferred_element_type=f32)


def dot_nn(a, b):
    return lax.dot_general(a, b, (((1,), (0,)), ((), ())), preferred_element_type=f32)


def blocks(n):
    nb = n // BL
    return [(i, j) for j in range(nb) for i in range(j, nb)]


def gram_body(rel, res_ref, code_ref, out_ref, th_ref, tl_ref, h_ref, l_ref):
    g = pl.program_id(0)
    rows, n = res_ref.shape

    @pl.when(g == 0)
    def _():
        for j in range(0, n, BL):
            x = res_ref[:, j : j + BL]
            hi, lo = split(x)
            h_ref[:, j : j + BL] = hi
            l_ref[:, j : j + BL] = lo
            xt = x.T
            hi, lo = split(xt)
            th_ref[j : j + BL, :] = hi
            tl_ref[j : j + BL, :] = lo

    mask = code_ref[...] == 2 * g + rel
    place = {b: p for p, b in enumerate(blocks(n))}
    for j in range(0, n, 2 * BL):
        mh = jnp.where(mask, h_ref[:, j : j + 2 * BL], jnp.zeros((), bf16))
        ml = jnp.where(mask, l_ref[:, j : j + 2 * BL], jnp.zeros((), bf16))
        th = th_ref[j:n, :]
        tl = tl_ref[j:n, :]
        prod = dot_nn(th, mh) + (dot_nn(th, ml) + dot_nn(tl, mh))
        for i in range(j, n, BL):
            for c in (j, j + BL):
                if i >= c:
                    p = place[(i // BL, c // BL)]
                    out_ref[0, p * BL : (p + 1) * BL, :] = prod[i - j : i - j + BL, c - j : c - j + BL]


def gram(res, code, n_group, rel):
    rows, n = res.shape
    size = len(blocks(n)) * BL
    return pl.pallas_call(
        lambda *refs: gram_body(rel, *refs),
        grid=(n_group,),
        in_specs=[
            pl.BlockSpec((rows, n), lambda g: (0, 0)),
            pl.BlockSpec((rows, 1), lambda g: (0, 0)),
        ],
        out_specs=pl.BlockSpec((1, size, BL), lambda g: (g, 0, 0)),
        out_shape=jax.ShapeDtypeStruct((n_group, size, BL), f32),
        scratch_shapes=[
            pltpu.VMEM((n, rows), bf16),
            pltpu.VMEM((n, rows), bf16),
            pltpu.VMEM((rows, n), bf16),
            pltpu.VMEM((rows, n), bf16),
        ],
        compiler_params=pltpu.CompilerParams(vmem_limit_bytes=40 << 20),
        cost_estimate=pl.CostEstimate(
            flops=3 * n_group * rows * n * n, bytes_accessed=4 * (rows * n + n_group * size * BL), transcendentals=0
        ),
        name="gram",
    )(res, code)


def diag_group(b, tt, s):
    lane = lax.broadcasted_iota(jnp.int32, (SUB, BL), 1)
    sub = lax.broadcasted_iota(jnp.int32, (SUB, BL), 0)
    base = SUB * s
    rows = [jnp.broadcast_to(b[base + t : base + t + 1, :], (SUB, BL)) for t in range(SUB)]
    schur = {}
    for i in range(SUB):
        for u in range(i + 1):
            schur[i, u] = jnp.broadcast_to(rows[i][:, base + u : base + u + 1], (SUB, BL))
    panel = (lane >= base) & (lane < base + SUB)
    fwd = [jnp.where(panel, jnp.where(lane == base + t, 1.0, 0.0), rows[t]) for t in range(SUB)]
    pivot, inv, mult = [], [], {}
    for t in range(SUB):
        pivot.append(schur[t, t])
        inv.append(1.0 / schur[t, t])
        for i in range(t + 1, SUB):
            mult[i, t] = schur[i, t] * inv[t]
        for u in range(t + 1, SUB):
            for i in range(u, SUB):
                schur[i, u] = schur[i, u] - mult[u, t] * schur[i, t]
        for i in range(t + 1, SUB):
            fwd[i] = fwd[i] - mult[i, t] * fwd[t]
    back = [None] * SUB
    for t in reversed(range(SUB)):
        w = fwd[t] * inv[t]
        for i in range(SUB - 1, t, -1):
            w = w - mult[i, t] * back[i]
        back[t] = w
    for g in range(s + 1, BL // SUB):
        x = b[SUB * g : SUB * g + SUB, :]
        even, odd = 0.0, 0.0
        for u in range(0, SUB, 2):
            even = even + jnp.broadcast_to(x[:, base + u : base + u + 1], (SUB, BL)) * back[u]
            odd = odd + jnp.broadcast_to(x[:, base + u + 1 : base + u + 2], (SUB, BL)) * back[u + 1]
        b[SUB * g : SUB * g + SUB, :] = jnp.where(panel, 0.0, x) - (even + odd)
    out = jnp.zeros((SUB, BL), f32)
    for t in range(SUB):
        row = jnp.where(lane <= base + t, fwd[t] * lax.rsqrt(pivot[t]), 0.0)
        out = jnp.where(sub == t, row, out)
    tt[base : base + SUB, :] = out


def chol_body(n, scale_ref, pa_ref, pb_ref, out_ref, w_ref, b_ref, t_ref, h1_ref, h2_ref):
    nb = n // BL
    order = blocks(n)
    place = {b: p for p, b in enumerate(order)}
    half = len(order) // 2
    scale = scale_ref[0]
    row = lax.broadcasted_iota(jnp.int32, (BL, BL), 0)
    col = lax.broadcasted_iota(jnp.int32, (BL, BL), 1)
    for p, (i, j) in enumerate(order):
        src, q = (pa_ref, p) if p < half else (pb_ref, p - half)
        x = src[q * BL : (q + 1) * BL, :] * scale
        if i == j:
            x = x + jnp.where(row == col, ridge, 0.0)
        w_ref[i * BL : (i + 1) * BL, j * BL : (j + 1) * BL] = x

    @pl.loop(0, nb)
    def _(k):
        o = pl.multiple_of(k * BL, BL)
        b_ref[...] = w_ref[pl.ds(o, BL), pl.ds(o, BL)]
        for s in range(BL // SUB):
            diag_group(b_ref, t_ref, s)
        out_ref[pl.ds(pl.multiple_of((len(order) + k) * BL, BL), BL), :] = t_ref[...]
        for kk in range(nb):

            @pl.when(k == kk)
            def _():
                c = kk * BL
                th, tl = split(t_ref[...])
                tcat = jnp.concatenate([th, tl, th, tl], axis=1)
                for i in range(c, n, BL):
                    ah, al = split(w_ref[i : i + BL, c : c + BL])
                    x = dot_nt(jnp.concatenate([ah, ah, al, al], axis=1), tcat)
                    if i == c:
                        x = jnp.where(row >= col, x, 0.0)
                    p = place[(i // BL, kk)]
                    out_ref[p * BL : (p + 1) * BL, :] = x
                    if i > c:
                        xh, xl = split(x)
                        h1_ref[i : i + BL, :] = jnp.concatenate([xh, xh, xl, xl], axis=1)
                        h2_ref[i : i + BL, :] = jnp.concatenate([xh, xl, xh, xl], axis=1)
                j = c + BL
                while j < n:
                    wide = BL if (j // BL) % 2 == 1 else 2 * BL
                    w_ref[j:n, j : j + wide] = w_ref[j:n, j : j + wide] - dot_nt(
                        h1_ref[j:n, :], h2_ref[j : j + wide, :]
                    )
                    j += wide


def chol(pa, pb, scale, n):
    nb = n // BL
    size = len(blocks(n)) * BL
    return pl.pallas_call(
        lambda *refs: chol_body(n, *refs),
        in_specs=[
            pl.BlockSpec(memory_space=pltpu.SMEM),
            pl.BlockSpec(memory_space=pltpu.VMEM),
            pl.BlockSpec(memory_space=pltpu.VMEM),
        ],
        out_specs=pl.BlockSpec(memory_space=pltpu.VMEM),
        out_shape=jax.ShapeDtypeStruct((size + n, BL), f32),
        scratch_shapes=[
            pltpu.VMEM((n, n), f32),
            pltpu.VMEM((BL, BL), f32),
            pltpu.VMEM((BL, BL), f32),
            pltpu.VMEM((n, 4 * BL), bf16),
            pltpu.VMEM((n, 4 * BL), bf16),
        ],
        compiler_params=pltpu.CompilerParams(vmem_limit_bytes=40 << 20),
        cost_estimate=pl.CostEstimate(flops=40 * n * n * n, bytes_accessed=8 * size * BL, transcendentals=0),
        name="chol",
    )(scale, pa, pb)


def whiten_body(n, mine_ref, res_ref, tag_ref, own_ref, other_ref, out_ref, fac_ref, lh_ref, ll_ref, th_ref, tl_ref, wh_ref, wl_ref):
    step = pl.program_id(0)
    order = blocks(n)
    nb = n // BL
    mine = mine_ref[0]

    @pl.when(step == 0)
    def _():
        for src, slot, dst in ((own_ref, 0, mine), (other_ref, 1, 1 - mine)):
            fac_ref[dst] = jnp.zeros((n, n), f32)
            for p, (i, j) in enumerate(order):
                x = src[p * BL : (p + 1) * BL, :]
                fac_ref[dst, i * BL : (i + 1) * BL, j * BL : (j + 1) * BL] = x
                hi, lo = split(x)
                lh_ref[slot, i * BL : (i + 1) * BL, j * BL : (j + 1) * BL] = hi
                ll_ref[slot, i * BL : (i + 1) * BL, j * BL : (j + 1) * BL] = lo
            hi, lo = split(src[len(order) * BL :, :])
            th_ref[slot] = hi
            tl_ref[slot] = lo

    tag = tag_ref[...]
    for slot in range(2):
        which = mine if slot == 0 else 1 - mine
        mask = tag == which + 1
        for k in range(nb):
            c = k * BL
            acc = jnp.where(mask, res_ref[:, c : c + BL], 0.0)
            if k:
                lh = lh_ref[slot, c : c + BL, :c]
                ll = ll_ref[slot, c : c + BL, :c]
                wh = wh_ref[:, :c]
                wl = wl_ref[:, :c]
                acc = acc - (dot_nt(wh, lh) + (dot_nt(wh, ll) + dot_nt(wl, lh)))
            ah, al = split(acc)
            th = th_ref[slot, c : c + BL, :]
            tl = tl_ref[slot, c : c + BL, :]
            x = dot_nt(ah, th) + (dot_nt(ah, tl) + dot_nt(al, th))
            hi, lo = split(x)
            wh_ref[:, c : c + BL] = hi
            wl_ref[:, c : c + BL] = lo
            if slot == 0:
                out_ref[:, c : c + BL] = x
            else:
                out_ref[:, c : c + BL] = jnp.where(mask, x, out_ref[:, c : c + BL])


def whiten(res, tags, own, other, mine, tile):
    rows, n = res.shape
    size = own.shape[0]
    whole = lambda s: (0, 0)
    return pl.pallas_call(
        lambda *refs: whiten_body(n, *refs),
        grid=(rows // tile,),
        in_specs=[
            pl.BlockSpec(memory_space=pltpu.SMEM),
            pl.BlockSpec((tile, n), lambda s: (s, 0)),
            pl.BlockSpec((tile, 1), lambda s: (s, 0)),
            pl.BlockSpec((size, BL), whole),
            pl.BlockSpec((size, BL), whole),
        ],
        out_specs=[
            pl.BlockSpec((tile, n), lambda s: (s, 0)),
            pl.BlockSpec((2, n, n), lambda s: (0, 0, 0)),
        ],
        out_shape=[jax.ShapeDtypeStruct((rows, n), f32), jax.ShapeDtypeStruct((2, n, n), f32)],
        scratch_shapes=[
            pltpu.VMEM((2, n, n), bf16),
            pltpu.VMEM((2, n, n), bf16),
            pltpu.VMEM((2, n, BL), bf16),
            pltpu.VMEM((2, n, BL), bf16),
            pltpu.VMEM((tile, n), bf16),
            pltpu.VMEM((tile, n), bf16),
        ],
        compiler_params=pltpu.CompilerParams(vmem_limit_bytes=56 << 20),
        cost_estimate=pl.CostEstimate(flops=12 * rows * n * n, bytes_accessed=16 * n * n, transcendentals=0),
        name="whiten",
    )(mine, res, tags, own, other)


def flip(x, axis, bit):
    size = lax.axis_size(axis)
    return lax.ppermute(x, axis, [(i, i ^ (1 << bit)) for i in range(size)])


def bit_of(axis, bit):
    return (lax.axis_index(axis) >> bit) & 1


def halve(x, axis, bit, dim):
    b = bit_of(axis, bit)
    got = flip(lax.dynamic_slice_in_dim(x, 1 - b, 1, dim), axis, bit)
    return lax.dynamic_slice_in_dim(x, b, 1, dim) + got


def double(x, axis, bit, dim):
    got = flip(x, axis, bit)
    low = bit_of(axis, bit) == 0
    return jnp.where(low, jnp.concatenate([x, got], dim), jnp.concatenate([got, x], dim))


def sum_and_share(part, n_group, n_member):
    gbits = n_group.bit_length() - 1
    mbits = n_member.bit_length() - 1
    rows = part.shape[1]
    shape = (2,) * gbits + (2,) * (mbits - 1)
    ghalf = [("group", b, gbits - 1 - b) for b in range(gbits)]
    mhalf = [("member", b, gbits + b - 1) for b in range(1, mbits)]
    plans = [ghalf + mhalf, mhalf[:1] + ghalf + mhalf[1:]]
    gathers = [mhalf[::-1], mhalf[:1] + mhalf[:0:-1]]
    parts = [
        part[:, c * (rows // 2) : (c + 1) * (rows // 2)].reshape(shape + (rows >> mbits, BL)) for c in range(2)
    ]
    for step in range(gbits + mbits - 1):
        parts = [halve(parts[c], *plans[c][step]) for c in range(2)]
    for step in range(mbits - 1):
        parts = [double(parts[c], *gathers[c][step]) for c in range(2)]
    return [p.reshape(rows // 2, BL) for p in parts]


def on_device(rows, old_list, old_centroids, dest_device, new_local, centroids):
    n_group = lax.axis_size("group")
    n_member = lax.axis_size("member")
    devices = n_group * n_member
    row_dev, width = rows.shape
    lists = centroids.shape[0]
    capacity = max(2, 2 * row_dev // devices)
    group = lax.axis_index("group")
    core = lax.axis_index("member") & 1

    every = jnp.zeros((n_group,) + centroids.shape, f32)
    for shift in range(n_group):
        got = centroids
        if shift:
            got = lax.ppermute(centroids, "group", [(i, (i + shift) % n_group) for i in range(n_group)])
        every = lax.dynamic_update_index_in_dim(every, got, (group - shift) % n_group, 0)
    every = every.reshape(n_group * lists, width)

    dest = dest_device[:, 0]
    new_list = (dest // n_member) * lists + new_local
    old_hot = (old_list[:, None] == jnp.arange(old_centroids.shape[0], dtype=jnp.int32)[None, :]).astype(f32)
    new_hot = (new_list[:, None] == jnp.arange(n_group * lists, dtype=jnp.int32)[None, :]).astype(f32)
    vectors = rows + jnp.dot(old_hot, old_centroids, precision=lax.Precision.HIGHEST)
    residual = vectors - jnp.dot(new_hot, every, precision=lax.Precision.HIGHEST)

    onehot = (dest[:, None] == jnp.arange(devices, dtype=jnp.int32)[None, :]).astype(jnp.int32)
    ranks = jnp.sum(jnp.cumsum(onehot, axis=0) * onehot, axis=1) - 1
    position = dest * capacity + ranks
    outgoing = jnp.zeros((devices * capacity, width), f32).at[position].set(residual)
    out_tags = jnp.zeros((devices * capacity,), jnp.int32).at[position].set(new_local + 1)
    sent = jnp.sum(new_hot, axis=0).astype(jnp.int32).reshape(n_group, lists)
    info = jnp.concatenate(
        [out_tags.reshape(devices, capacity), jnp.repeat(sent, n_member, axis=0)], axis=1
    )
    axes = ("group", "member")
    info = lax.all_to_all(info.reshape(devices, 1, -1), axes, split_axis=0, concat_axis=0, tiled=True)[:, 0]
    arrived = lax.all_to_all(
        outgoing.reshape(devices, capacity, width), axes, split_axis=0, concat_axis=0, tiled=True
    ).reshape(devices * capacity, width)
    tags = info[:, :capacity].reshape(-1, 1)
    counts = jnp.sum(info[:, capacity:], axis=0).astype(f32)

    code = ((dest // n_member) * 2 + (new_local ^ core))[:, None]
    away = gram(residual, code, n_group, 1)
    part = gram(residual, code, n_group, 0) + flip(away, "member", 0)
    pa, pb = sum_and_share(part, n_group, n_member)
    count = lax.dynamic_index_in_dim(counts, core, 0, keepdims=True)
    own = chol(pa, pb, 1.0 / jnp.maximum(count, 1.0), width)
    other = flip(own, "member", 0)
    result, factors = whiten(arrived, tags, own, other, core.reshape(1), min(256, devices * capacity))
    return (result, factors)


def solution(mesh):
    return jax.shard_map(
        on_device,
        mesh=mesh,
        in_specs=(
            P(("group", "member"), None),
            P(("group", "member")),
            P(),
            P(("group", "member"), None),
            P(("group", "member")),
            P("group", None),
        ),
        out_specs=(P(("group", "member"), None), P("group", None, None)),
        check_vma=False,
    )
```

time: 1050 us -> 302 us (0.29)
  other arithmetic: 539 us -> 12 us
  matrix products: 151 us -> 6.35 us
  Pallas kernels: 0 us -> 94.3 us
  waiting for transfers between devices: 220 us -> 140 us
  local copies, waits for them, and re-layouts: 77.5 us -> 19.6 us
  blocking collectives: 31.6 us -> 0 us
  starting transfers between devices: 13.8 us -> 27.5 us
  between operations: 14.9 us -> 1.68 us
    another operation x38 -> x2, other arithmetic: 500 us -> 1.2 us  [the longest x30 332 us: on_device(): factors = jax.vmap(jnp.linalg.cholesky)(covs)]
    ppermute x0 -> x17, waiting for transfers between devices: none -> 133 us  [the longest x16 133 us: flip(): return lax.ppermute(x, axis, [(i, i ^ 1 << bit) for i in range(size)])]
    psum x1 -> x0, waiting for transfers between devices: 127 us -> none  [on_device(): summed, counts = lax.psum((stacked, local_counts), 'member')]
    another operation x44 -> x0, matrix products: 112 us -> none  [the longest x30 79 us: on_device(): jax.scipy.linalg.solve_triangular(factors[j], residual.T, lower=True)]
    pallas_call x0 -> x4, Pallas kernels: none -> 94.3 us  [the longest x1 42.3 us: chol(): pl.pallas_call(lambda *refs: chol_body(n, *refs), in_specs=[pl.BlockSpec(...]
    all_to_all x2, waiting for transfers between devices: 93.2 us -> 6.78 us  [the longest x1 6.78 us: on_device(): lax.all_to_all(info.reshape(devices, 1, -1), axes, split_axis=0, concat_a...]
    another operation x61 -> x1, local copies, waits for them, and re-layouts: 49.9 us -> 0.01 us  [the longest x51 45.1 us: on_device(): jax.scipy.linalg.solve_triangular(factors[j], residual.T, lower=True)]
    dot_general x3 -> x1, matrix products: 37 us -> 3.33 us  [on_device(): jnp.dot(new_hot, every, precision=lax.Precision.HIGHEST)]
  transfers between devices with their start and end apart: 3 -> 19, of which waited for: 2 -> 15; matrix products, arithmetic and copies ran while one was open for 2% -> 9% of each run, Pallas kernels for 0% -> 16%
where the time goes in v1:
time: 302 us; the launch traced here: 301 us
  waiting for transfers between devices  140 us (46%)
  Pallas kernels  94.3 us (31%)
  starting transfers between devices  27.5 us (9%)
  local copies, waits for them, and re-layouts  19.6 us (6%)
  other arithmetic  12 us (4%)
  matrix products  6.35 us (2%)
    ppermute x16, waiting for transfers between devices, flip(): return lax.ppermute(x, axis, [(i, i ^ 1 << bit) for i in range(size)])  133 us
    pallas_call x1, Pallas kernels, chol(): pl.pallas_call(lambda *refs: chol_body(n, *refs), in_specs=[pl.BlockSpec(...  42.3 us
    pallas_call x1, Pallas kernels, whiten(): pl.pallas_call(lambda *refs: whiten_body(n, *refs), grid=(rows // tile,),...  39.8 us
    ppermute x16, starting transfers between devices, flip(): return lax.ppermute(x, axis, [(i, i ^ 1 << bit) for i in range(size)])  16 us
    pallas_call x2, Pallas kernels, gram(): pl.pallas_call(lambda *refs: gram_body(rel, *refs), grid=(n_group,), in_s...  12.2 us
    all_to_all x1, waiting for transfers between devices, on_device(): lax.all_to_all(info.reshape(devices, 1, -1), axes, split_axis=0, concat_a...  6.78 us
  transfers between devices with their start and end apart: 19, of which 15 were waited for; matrix products, arithmetic and copies ran while one was open for 9% of the time, Pallas kernels for 16%

profile of v1, /device:TPU:0, one launch (start us, length us, event | category | flops | bytes accessed | tf_op | source)
XLA Modules:
  0.0 301.2 jit_solution(417232774222212390)
XLA Ops:
  0.7 3.1 %collective-permute-start = (f32[2,1024]{1,0:T(2,128)}, f32[2,1024]{1,0:T(2,128)S(1)}, u32[]{:S(2)}, u32[]{:S(2)}) collective-permute-start(f32[2,1024]{1,0:T(2,128)} %param.11), channel_id=1, source_target_pairs={{0,16},{16,0},{1,17},{17,1},{2,18},{18,2},{3,19},{19,3},{4,20},{20... | collective-permute-start | bytes 24584 | tf_op jit(solution)/shard_map/ppermute | solution.py:339
  3.7 0.7 bitcast_dynamic-update-slice_fusion.1
  4.5 3.0 %fusion.4 = f32[512,1024]{1,0:T(8,128)} fusion(f32[64,1024]{1,0:T(8,128)S(1)} %copy-done, s32[512]{0:T(512)} %param.7), kind=kOutput, calls=%fused_computation.22 | convolution fusion | flops 402685952 | bytes 2361344 | tf_op jit(solution)/shard_map/dot_general | solution.py:347
  7.7 3.3 %add_subtract_fusion.refs_0_ = f32[512,1024]{1,0:T(8,128)S(1)} fusion(f32[512,1024]{1,0:T(8,128)} %param.6, f32[512,1024]{1,0:T(8,128)} %fusion.4, f32[4,1024]{1,0:T(4,128)S(1)} %reshape.654, s32[512]{0:T(512)S(1)} %get-tuple-element.5), kind=kOutput, calls=%fused_computation.2 | convolution fusion | flops 26216448 | bytes 6309888 | tf_op jit(solution)/shard_map/dot_general | solution.py:348
  11.1 6.8 %gram.3 = f32[2,4608,128]{2,1,0:T(8,128)} custom-call(f32[512,1024]{1,0:T(8,128)S(1)} %add_subtract_fusion.refs_0_, s32[512,1]{1,0:T(8,128)S(1)} %copy.25.refs_1_), custom_call_target="tpu_custom_call" | custom-call | flops 3221225472 | bytes 6815744 | tf_op jit(solution)/shard_map/gram/pallas_call | solution.py:67
  17.9 5.4 %gram.2 = f32[2,4608,128]{2,1,0:T(8,128)S(1)} custom-call(f32[512,1024]{1,0:T(8,128)S(1)} %add_subtract_fusion.refs_0_, s32[512,1]{1,0:T(8,128)S(1)} %copy.25.refs_1_), custom_call_target="tpu_custom_call" | custom-call | flops 3221225472 | bytes 6815744 | tf_op jit(solution)/shard_map/gram/pallas_call | solution.py:67
  23.3 2.9 collective-permute-done.1
  26.1 2.8 add.124
  28.9 2.5 fusion.16
  31.4 1.3 constant_dynamic-slice_fusion.3
  32.8 1.6 collective-permute-start.9
  34.3 2.4 constant_dynamic-slice_fusion.7
  37.5 1.2 reduce-window.6
  39.0 22.0 %collective-permute-done.9 = f32[2,1,2,2,288,128]{5,4,3,2,1,0:T(8,128)} collective-permute-done((f32[2,1,2,2,288,128]{5,4,3,2,1,0:T(8,128)S(1)}, f32[2,1,2,2,288,128]{5,4,3,2,1,0:T(8,128)}, u32[]{:S(2)}, u32[]{:S(2)}) %collective-permute-start.9) | collective-permute-done | bytes 1179680 | tf_op jit(solution)/shard_map/ppermute | solution.py:287
  61.0 1.7 dynamic-slice_add_fusion
  62.7 0.9 constant_dynamic-slice_fusion.2
  63.9 0.9 collective-permute-done.2
  64.8 1.5 dynamic-slice_add_fusion.1
  66.2 1.0 copy-done.4
  67.2 0.9 constant_dynamic-slice_fusion.6
  68.1 0.8 collective-permute-start.3
  68.9 2.4 scatter_custom_fusion.1
  71.5 7.0 %collective-permute-done.10 = f32[1,1,2,2,288,128]{5,4,3,2,1,0:T(8,128)} collective-permute-done((f32[1,1,2,2,288,128]{5,4,3,2,1,0:T(8,128)}, f32[1,1,2,2,288,128]{5,4,3,2,1,0:T(8,128)}, u32[]{:S(2)}, u32[]{:S(2)}) %collective-permute-start.10) | collective-permute-done | bytes 589856 | tf_op jit(solution)/shard_map/ppermute | solution.py:287
  78.4 1.1 dynamic-slice_add_fusion.2
  79.6 1.6 collective-permute-start.11
  81.2 1.4 collective-permute-done.3
  82.6 1.1 dynamic-slice_add_fusion.3
  83.8 1.6 collective-permute-start.4
  85.5 5.5 %collective-permute-done.11 = f32[1,1,1,2,288,128]{5,4,3,2,1,0:T(8,128)S(1)} collective-permute-done((f32[1,1,1,2,288,128]{5,4,3,2,1,0:T(8,128)S(1)}, f32[1,1,1,2,288,128]{5,4,3,2,1,0:T(8,128)S(1)}, u32[]{:S(2)}, u32[]{:S(2)}) %collective-permute-start.11) | collective-permute-done | bytes 294944 | tf_op jit(solution)/shard_map/ppermute | solution.py:287
  91.0 1.7 collective-permute-start.12
  92.8 2.1 collective-permute-done.4
  95.0 2.6 collective-permute-start.5
  97.6 5.7 %collective-permute-done.12 = f32[1,1,1,1,288,128]{5,4,3,2,1,0:T(8,128)S(1)} collective-permute-done((f32[1,1,1,1,288,128]{5,4,3,2,1,0:T(8,128)S(1)}, f32[1,1,1,1,288,128]{5,4,3,2,1,0:T(8,128)S(1)}, u32[]{:S(2)}, u32[]{:S(2)}) %collective-permute-start.12) | collective-permute-done | bytes 147488 | tf_op jit(solution)/shard_map/ppermute | solution.py:287
  103.4 1.7 collective-permute-start.13
  105.4 3.1 %collective-permute-done.13 = f32[1,1,1,1,288,128]{5,4,3,2,1,0:T(8,128)S(1)} collective-permute-done((f32[1,1,1,1,288,128]{5,4,3,2,1,0:T(8,128)S(1)}, f32[1,1,1,1,288,128]{5,4,3,2,1,0:T(8,128)S(1)}, u32[]{:S(2)}, u32[]{:S(2)}) %collective-permute-start.13) | collective-permute-done | bytes 147488 | tf_op jit(solution)/shard_map/ppermute | solution.py:287
  109.4 4.8 %all-to-all-start.1 = ((s32[32,1,34]{2,1,0:T(1,128)}), s32[32,1,34]{2,1,0:T(1,128)S(1)}, u32[]{:S(2)}, u32[]{:S(2)}) async-start(s32[32,1,34]{2,1,0:T(1,128)} %bitcast.11), calls=%async_computation.1 | async-start | bytes 32768 | tf_op jit(solution)/shard_map/all_to_all | solution.py:360
  114.2 4.5 %scatter_custom_fusion = f32[1024,1024]{1,0:T(8,128)} fusion(s32[512]{0:T(512)S(1)} %bitcast.65, f32[512,1024]{1,0:T(8,128)S(1)} %add_subtract_fusion.refs_0_, f32[]{:T(128)} %constant.68.clone.1), kind=kCustom, calls=%fused_computation.3 | custom fusion | bytes 4194308 | tf_op jit(solution)/shard_map/scatter | solution.py:353
  118.7 1.9 collective-permute-done.6
  120.7 6.8 %all-to-all-done.1 = s32[32,1,34]{2,1,0:T(1,128)S(1)} async-done(((s32[32,1,34]{2,1,0:T(1,128)}), s32[32,1,34]{2,1,0:T(1,128)S(1)}, u32[]{:S(2)}, u32[]{:S(2)}) %all-to-all-start.1) | async-done | bytes 4384 | tf_op jit(solution)/shard_map/all_to_all | solution.py:360
  127.5 3.6 %all-to-all-start = ((f32[32,32,1024]{2,1,0:T(8,128)}), f32[32,32,1024]{2,1,0:T(8,128)}, u32[]{:S(2)}, u32[]{:S(2)}) async-start(f32[32,32,1024]{2,1,0:T(8,128)} %bitcast.49), calls=%async_computation | async-start | bytes 8388608 | tf_op jit(solution)/shard_map/all_to_all | solution.py:361
  131.2 1.7 collective-permute-start.15
  132.9 1.1 maximum_select_fusion.2
  134.0 1.5 collective-permute-start.8
  137.0 76.5 %collective-permute-done.15 = f32[1,2,1,2,288,128]{5,4,3,2,1,0:T(8,128)S(1)} collective-permute-done((f32[1,2,1,2,288,128]{5,4,3,2,1,0:T(8,128)S(1)}, f32[1,2,1,2,288,128]{5,4,3,2,1,0:T(8,128)S(1)}, u32[]{:S(2)}, u32[]{:S(2)}) %collective-permute-start.15) | collective-permute-done | bytes 589856 | tf_op jit(solution)/shard_map/ppermute | solution.py:287
  213.6 42.3 %chol.1.refs_3_ = f32[5632,128]{1,0:T(8,128)S(1)} custom-call(f32[1]{0:T(128)S(6)} %div.21.refs_0_, f32[2304,128]{1,0:T(8,128)S(1)} %bitcast.48, f32[2304,128]{1,0:T(8,128)S(1)} %bitcast.47), custom_call_target="tpu_custom_call" | custom-call | flops 42949672960 | bytes 4718592 | tf_op jit(solution)/shard_map/chol/pallas_call | solution.py:184
  256.0 1.7 reshape.679.refs_2_
  257.7 3.7 %collective-permute-done.16.refs_4_ = f32[5632,128]{1,0:T(8,128)} collective-permute-done((f32[5632,128]{1,0:T(8,128)S(1)}, f32[5632,128]{1,0:T(8,128)}, u32[]{:S(2)}, u32[]{:S(2)}) %collective-permute-start.16) | collective-permute-done | bytes 2883616 | tf_op jit(solution)/shard_map/ppermute | solution.py:287
  261.4 39.8 %whiten.1 = (f32[1024,1024]{1,0:T(8,128)}, f32[2,1024,1024]{2,1,0:T(8,128)}) custom-call(s32[1]{0:T(128)} %bitcast.refs_0_, f32[1024,1024]{1,0:T(8,128)} %bitcast.9.refs_1_, s32[1024,1]{1,0:T(8,128)} %reshape.679.refs_2_, f32[5632,128]{1,0:T(8,128)} %copy-done.2, f32[5632,128]{1,0:T(8,128)} %collective-permute-done.16.refs_4_), custom_call_target="tpu_custom_call" | custom-call | flops 12884901888 | bytes 16777216 | tf_op jit(solution)/shard_map/whiten/pallas_call | solution.py:256
  (64 shorter events, 4.2 us)
Async XLA Ops:
  0.6 3.8 %copy-start = (f32[64,1024]{1,0:T(8,128)S(1)}, f32[64,1024]{1,0:T(8,128)}, u32[]{:S(2)}) copy-start(f32[64,1024]{1,0:T(8,128)} %param.8) | copy-start | bytes 786436
  0.6 6.8 %copy-start.6 = (s32[512,1]{0,1:T(1,128)S(1)}, s32[512,1]{0,1:T(1,128)}, u32[]{:S(2)}) copy-start(s32[512,1]{0,1:T(1,128)} %param.9) | copy-start | bytes 6148
  0.7 6.8 %copy-start.7 = (s32[512]{0:T(512)S(1)}, s32[512]{0:T(512)}, u32[]{:S(2)}) copy-start(s32[512]{0:T(512)} %param.10) | copy-start | bytes 6148
  0.7 7.0 %collective-permute-start = (f32[2,1024]{1,0:T(2,128)}, f32[2,1024]{1,0:T(2,128)S(1)}, u32[]{:S(2)}, u32[]{:S(2)}) collective-permute-start(f32[2,1024]{1,0:T(2,128)} %param.11), channel_id=1, source_target_pairs={{0,16},{16,0},{1,17},{17,1},{2,18},{18,2},{3,19},{19,3},{4,20},{20... | collective-permute-start | bytes 24584 | tf_op jit(solution)/shard_map/ppermute | solution.py:339
  17.9 8.3 %collective-permute-start.1 = (f32[2,4608,128]{2,1,0:T(8,128)}, f32[2,4608,128]{2,1,0:T(8,128)}, u32[]{:S(2)}, u32[]{:S(2)}) collective-permute-start(f32[2,4608,128]{2,1,0:T(8,128)} %gram.3), channel_id=1, source_target_pairs={{0,1},{1,0},{2,3},{3,2},{4,5},{5,4},{6,7},{7,6},{8,9},{9,8},{10,11... | collective-permute-start | bytes 14155784 | tf_op jit(solution)/shard_map/ppermute | solution.py:287
  32.8 28.2 %collective-permute-start.9 = (f32[2,1,2,2,288,128]{5,4,3,2,1,0:T(8,128)S(1)}, f32[2,1,2,2,288,128]{5,4,3,2,1,0:T(8,128)}, u32[]{:S(2)}, u32[]{:S(2)}) collective-permute-start(f32[2,1,2,2,288,128]{5,4,3,2,1,0:T(8,128)S(1)} %constant_dynamic-slice_fusion.3), channel_id=1, source_target_pairs={{0,2},{1,3},{2,0},{3,1},{4,6},{5,7},{6,4},{7,5},{8,10},{9,11},{10,... | collective-permute-start | bytes 3538952 | tf_op jit(solution)/shard_map/ppermute | solution.py:287
  36.7 28.0 %collective-permute-start.2 = (f32[1,2,2,2,288,128]{5,4,3,2,1,0:T(8,128)}, f32[1,2,2,2,288,128]{5,4,3,2,1,0:T(8,128)}, u32[]{:S(2)}, u32[]{:S(2)}) collective-permute-start(f32[1,2,2,2,288,128]{5,4,3,2,1,0:T(8,128)} %constant_dynamic-slice_fusion.7), channel_id=1, source_target_pairs={{0,16},{16,0},{1,17},{17,1},{2,18},{18,2},{3,19},{19,3},{4,20},{20... | collective-permute-start | bytes 3538952 | tf_op jit(solution)/shard_map/ppermute | solution.py:287
  39.0 25.8 %copy-start.3 = (f32[2,2304,128]{2,1,0:T(8,128)S(1)}, f32[2,2304,128]{2,1,0:T(8,128)}, u32[]{:S(2)}) copy-start(f32[2,2304,128]{2,1,0:T(8,128)} %get-tuple-element.3) | copy-start | bytes 7077892
  63.6 14.8 %collective-permute-start.10 = (f32[1,1,2,2,288,128]{5,4,3,2,1,0:T(8,128)}, f32[1,1,2,2,288,128]{5,4,3,2,1,0:T(8,128)}, u32[]{:S(2)}, u32[]{:S(2)}) collective-permute-start(f32[1,1,2,2,288,128]{5,4,3,2,1,0:T(8,128)} %constant_dynamic-slice_fusion.2), channel_id=1, source_target_pairs={{0,16},{16,0},{1,17},{17,1},{2,18},{18,2},{3,19},{19,3},{4,20},{20... | collective-permute-start | bytes 1769480 | tf_op jit(solution)/shard_map/ppermute | solution.py:287
  66.2 1.0 copy-start.4
  68.1 14.5 %collective-permute-start.3 = (f32[1,1,2,2,288,128]{5,4,3,2,1,0:T(8,128)}, f32[1,1,2,2,288,128]{5,4,3,2,1,0:T(8,128)}, u32[]{:S(2)}, u32[]{:S(2)}) collective-permute-start(f32[1,1,2,2,288,128]{5,4,3,2,1,0:T(8,128)} %constant_dynamic-slice_fusion.6), channel_id=1, source_target_pairs={{0,2},{1,3},{2,0},{3,1},{4,6},{5,7},{6,4},{7,5},{8,10},{9,11},{10,... | collective-permute-start | bytes 1769480 | tf_op jit(solution)/shard_map/ppermute | solution.py:287
  71.4 11.2 %copy-start.5 = (f32[1,2,2,2,288,128]{5,4,3,2,1,0:T(8,128)S(1)}, f32[1,2,2,2,288,128]{5,4,3,2,1,0:T(8,128)}, u32[]{:S(2)}) copy-start(f32[1,2,2,2,288,128]{5,4,3,2,1,0:T(8,128)} %copy-done.4) | copy-start | bytes 3538948
  79.6 11.4 %collective-permute-start.11 = (f32[1,1,1,2,288,128]{5,4,3,2,1,0:T(8,128)S(1)}, f32[1,1,1,2,288,128]{5,4,3,2,1,0:T(8,128)S(1)}, u32[]{:S(2)}, u32[]{:S(2)}) collective-permute-start(f32[1,1,1,2,288,128]{5,4,3,2,1,0:T(8,128)S(1)} %constant_dynamic-slice_fusion.1), channel_id=1, source_target_pairs={{0,4},{1,5},{2,6},{3,7},{4,0},{5,1},{6,2},{7,3},{8,12},{9,13},{10,... | collective-permute-start | bytes 884744 | tf_op jit(solution)/shard_map/ppermute | solution.py:287
  83.8 11.1 %collective-permute-start.4 = (f32[1,1,1,2,288,128]{5,4,3,2,1,0:T(8,128)S(1)}, f32[1,1,1,2,288,128]{5,4,3,2,1,0:T(8,128)S(1)}, u32[]{:S(2)}, u32[]{:S(2)}) collective-permute-start(f32[1,1,1,2,288,128]{5,4,3,2,1,0:T(8,128)S(1)} %constant_dynamic-slice_fusion.5), channel_id=1, source_target_pairs={{0,4},{1,5},{2,6},{3,7},{4,0},{5,1},{6,2},{7,3},{8,12},{9,13},{10,... | collective-permute-start | bytes 884744 | tf_op jit(solution)/shard_map/ppermute | solution.py:287
  91.0 12.3 %collective-permute-start.12 = (f32[1,1,1,1,288,128]{5,4,3,2,1,0:T(8,128)S(1)}, f32[1,1,1,1,288,128]{5,4,3,2,1,0:T(8,128)S(1)}, u32[]{:S(2)}, u32[]{:S(2)}) collective-permute-start(f32[1,1,1,1,288,128]{5,4,3,2,1,0:T(8,128)S(1)} %constant_dynamic-slice_fusion), channel_id=1, source_target_pairs={{0,8},{1,9},{2,10},{3,11},{4,12},{5,13},{6,14},{7,15},{8,0},{9,1},... | collective-permute-start | bytes 442376 | tf_op jit(solution)/shard_map/ppermute | solution.py:287
  95.0 10.4 %collective-permute-start.5 = (f32[1,1,1,1,288,128]{5,4,3,2,1,0:T(8,128)S(1)}, f32[1,1,1,1,288,128]{5,4,3,2,1,0:T(8,128)S(1)}, u32[]{:S(2)}, u32[]{:S(2)}) collective-permute-start(f32[1,1,1,1,288,128]{5,4,3,2,1,0:T(8,128)S(1)} %constant_dynamic-slice_fusion.4), channel_id=1, source_target_pairs={{0,8},{1,9},{2,10},{3,11},{4,12},{5,13},{6,14},{7,15},{8,0},{9,1},... | collective-permute-start | bytes 442376 | tf_op jit(solution)/shard_map/ppermute | solution.py:287
  103.4 5.2 %collective-permute-start.13 = (f32[1,1,1,1,288,128]{5,4,3,2,1,0:T(8,128)S(1)}, f32[1,1,1,1,288,128]{5,4,3,2,1,0:T(8,128)S(1)}, u32[]{:S(2)}, u32[]{:S(2)}) collective-permute-start(f32[1,1,1,1,288,128]{5,4,3,2,1,0:T(8,128)S(1)} %dynamic-slice_add_fusion.6), channel_id=1, source_target_pairs={{0,2},{1,3},{2,0},{3,1},{4,6},{5,7},{6,4},{7,5},{8,10},{9,11},{10,... | collective-permute-start | bytes 442376 | tf_op jit(solution)/shard_map/ppermute | solution.py:287
  105.3 15.3 %collective-permute-start.6 = (f32[1,1,1,1,288,128]{5,4,3,2,1,0:T(8,128)S(1)}, f32[1,1,1,1,288,128]{5,4,3,2,1,0:T(8,128)S(1)}, u32[]{:S(2)}, u32[]{:S(2)}) collective-permute-start(f32[1,1,1,1,288,128]{5,4,3,2,1,0:T(8,128)S(1)} %dynamic-slice_add_fusion.7), channel_id=1, source_target_pairs={{0,8},{1,9},{2,10},{3,11},{4,12},{5,13},{6,14},{7,15},{8,0},{9,1},... | collective-permute-start | bytes 442376 | tf_op jit(solution)/shard_map/ppermute | solution.py:287
  108.6 22.5 %collective-permute-start.14 = (f32[1,2,1,1,288,128]{5,4,3,2,1,0:T(8,128)S(1)}, f32[1,2,1,1,288,128]{5,4,3,2,1,0:T(8,128)S(1)}, u32[]{:S(2)}, u32[]{:S(2)}) collective-permute-start(f32[1,2,1,1,288,128]{5,4,3,2,1,0:T(8,128)S(1)} %maximum_select_fusion.7), channel_id=1, source_target_pairs={{0,8},{1,9},{2,10},{3,11},{4,12},{5,13},{6,14},{7,15},{8,0},{9,1},... | collective-permute-start | bytes 884744 | tf_op jit(solution)/shard_map/ppermute | solution.py:287
  109.4 18.1 %all-to-all-start.1 = ((s32[32,1,34]{2,1,0:T(1,128)}), s32[32,1,34]{2,1,0:T(1,128)S(1)}, u32[]{:S(2)}, u32[]{:S(2)}) async-start(s32[32,1,34]{2,1,0:T(1,128)} %bitcast.11), calls=%async_computation.1 | async-start | bytes 32768 | tf_op jit(solution)/shard_map/all_to_all | solution.py:360
  120.6 12.3 %collective-permute-start.7 = (f32[1,1,1,2,288,128]{5,4,3,2,1,0:T(8,128)S(1)}, f32[1,1,1,2,288,128]{5,4,3,2,1,0:T(8,128)}, u32[]{:S(2)}, u32[]{:S(2)}) collective-permute-start(f32[1,1,1,2,288,128]{5,4,3,2,1,0:T(8,128)S(1)} %maximum_select_fusion.5), channel_id=1, source_target_pairs={{0,4},{1,5},{2,6},{3,7},{4,0},{5,1},{6,2},{7,3},{8,12},{9,13},{10,... | collective-permute-start | bytes 884744 | tf_op jit(solution)/shard_map/ppermute | solution.py:287
  127.5 130.2 %all-to-all-start = ((f32[32,32,1024]{2,1,0:T(8,128)}), f32[32,32,1024]{2,1,0:T(8,128)}, u32[]{:S(2)}, u32[]{:S(2)}) async-start(f32[32,32,1024]{2,1,0:T(8,128)} %bitcast.49), calls=%async_computation | async-start | bytes 8388608 | tf_op jit(solution)/shard_map/all_to_all | solution.py:361
  131.2 82.3 %collective-permute-start.15 = (f32[1,2,1,2,288,128]{5,4,3,2,1,0:T(8,128)S(1)}, f32[1,2,1,2,288,128]{5,4,3,2,1,0:T(8,128)S(1)}, u32[]{:S(2)}, u32[]{:S(2)}) collective-permute-start(f32[1,2,1,2,288,128]{5,4,3,2,1,0:T(8,128)S(1)} %maximum_select_fusion.3), channel_id=1, source_target_pairs={{0,4},{1,5},{2,6},{3,7},{4,0},{5,1},{6,2},{7,3},{8,12},{9,13},{10,... | collective-permute-start | bytes 1769480 | tf_op jit(solution)/shard_map/ppermute | solution.py:287
  134.0 79.5 %collective-permute-start.8 = (f32[1,1,2,2,288,128]{5,4,3,2,1,0:T(8,128)S(1)}, f32[1,1,2,2,288,128]{5,4,3,2,1,0:T(8,128)S(1)}, u32[]{:S(2)}, u32[]{:S(2)}) collective-permute-start(f32[1,1,2,2,288,128]{5,4,3,2,1,0:T(8,128)S(1)} %maximum_select_fusion.2), channel_id=1, source_target_pairs={{0,2},{1,3},{2,0},{3,1},{4,6},{5,7},{6,4},{7,5},{8,10},{9,11},{10,... | collective-permute-start | bytes 1769480 | tf_op jit(solution)/shard_map/ppermute | solution.py:287
  255.9 5.5 %copy-start.2 = (f32[5632,128]{1,0:T(8,128)}, f32[5632,128]{1,0:T(8,128)S(1)}, u32[]{:S(2)}) copy-start(f32[5632,128]{1,0:T(8,128)S(1)} %chol.1.refs_3_) | copy-start | bytes 8650756
  255.9 5.5 %collective-permute-start.16 = (f32[5632,128]{1,0:T(8,128)S(1)}, f32[5632,128]{1,0:T(8,128)}, u32[]{:S(2)}, u32[]{:S(2)}) collective-permute-start(f32[5632,128]{1,0:T(8,128)S(1)} %chol.1.refs_3_), channel_id=1, source_target_pairs={{0,1},{1,0},{2,3},{3,2},{4,5},{5,4},{6,7},{7,6},{8,9},{9,8},{10,11... | collective-permute-start | bytes 8650760 | tf_op jit(solution)/shard_map/ppermute | solution.py:287
  261.4 39.8 %copy-start.1 = (f32[64,1024]{1,0:T(8,128)S(1)}, f32[64,1024]{1,0:T(8,128)}, u32[]{:S(2)}) copy-start(f32[64,1024]{1,0:T(8,128)} %param.8) | copy-start | bytes 786436

commit v2 on v1

--- a/solution.py
+++ b/solution.py
@@ -5,6 +5,7 @@
 from jax.experimental.pallas import tpu as pltpu
 from jax.sharding import PartitionSpec as P
 
+
 ridge = 0.1
 f32 = jnp.float32
 bf16 = jnp.bfloat16
@@ -25,6 +26,12 @@
     return lax.dot_general(a, b, (((1,), (0,)), ((), ())), preferred_element_type=f32)
 
 
+def dot3(a, b):
+    ah, al = split(a)
+    bh, bl = split(b)
+    return dot_nn(ah, bh) + (dot_nn(ah, bl) + dot_nn(al, bh))
+
+
 def blocks(n):
     nb = n // BL
     return [(i, j) for j in range(nb) for i in range(j, nb)]
@@ -32,7 +39,7 @@
 
 def gram_body(rel, res_ref, code_ref, out_ref, th_ref, tl_ref, h_ref, l_ref):
     g = pl.program_id(0)
-    rows, n = res_ref.shape
+    _, n = res_ref.shape
 
     @pl.when(g == 0)
     def _():
@@ -156,6 +163,12 @@
             @pl.when(k == kk)
             def _():
                 c = kk * BL
+                if kk % 2:
+                    p = place[(kk, kk - 1)] * BL
+                    q = (len(order) + kk - 1) * BL
+                    x = dot3(out_ref[p : p + BL, :], out_ref[q : q + BL, :])
+                    q = (len(order) + nb + kk // 2) * BL
+                    out_ref[q : q + BL, :] = -dot3(t_ref[...], x)
                 th, tl = split(t_ref[...])
                 tcat = jnp.concatenate([th, tl, th, tl], axis=1)
                 for i in range(c, n, BL):
@@ -179,7 +192,6 @@
 
 
 def chol(pa, pb, scale, n):
-    nb = n // BL
     size = len(blocks(n)) * BL
     return pl.pallas_call(
         lambda *refs: chol_body(n, *refs),
@@ -189,7 +201,7 @@
             pl.BlockSpec(memory_space=pltpu.VMEM),
         ],
         out_specs=pl.BlockSpec(memory_space=pltpu.VMEM),
-        out_shape=jax.ShapeDtypeStruct((size + n, BL), f32),
+        out_shape=jax.ShapeDtypeStruct((size + n + n // 2, BL), f32),
         scratch_shapes=[
             pltpu.VMEM((n, n), f32),
             pltpu.VMEM((BL, BL), f32),
@@ -203,83 +215,114 @@
     )(scale, pa, pb)
 
 
-def whiten_body(n, mine_ref, res_ref, tag_ref, own_ref, other_ref, out_ref, fac_ref, lh_ref, ll_ref, th_ref, tl_ref, wh_ref, wl_ref):
-    step = pl.program_id(0)
+def whiten_body(n, chunks, *refs):
+    mine_ref, own_ref, other_ref = refs[:3]
+    res_refs = refs[3 : 3 + chunks]
+    tag_refs = refs[3 + chunks : 3 + 2 * chunks]
+    out_ref, fac_ref, f_ref, o_ref, lh_ref, ll_ref, th_ref, tl_ref, wh_ref, wl_ref, sem = refs[3 + 2 * chunks :]
     order = blocks(n)
     nb = n // BL
+    wide = 2 * BL
     mine = mine_ref[0]
-
-    @pl.when(step == 0)
-    def _():
-        for src, slot, dst in ((own_ref, 0, mine), (other_ref, 1, 1 - mine)):
-            fac_ref[dst] = jnp.zeros((n, n), f32)
-            for p, (i, j) in enumerate(order):
-                x = src[p * BL : (p + 1) * BL, :]
-                fac_ref[dst, i * BL : (i + 1) * BL, j * BL : (j + 1) * BL] = x
-                hi, lo = split(x)
-                lh_ref[slot, i * BL : (i + 1) * BL, j * BL : (j + 1) * BL] = hi
-                ll_ref[slot, i * BL : (i + 1) * BL, j * BL : (j + 1) * BL] = lo
-            hi, lo = split(src[len(order) * BL :, :])
-            th_ref[slot] = hi
-            tl_ref[slot] = lo
-
-    tag = tag_ref[...]
-    for slot in range(2):
-        which = mine if slot == 0 else 1 - mine
-        mask = tag == which + 1
+    sources, part, _ = res_refs[0].shape
+    rows = sources * part
+    copies = []
+
+    for slot, (src, dst) in enumerate(((own_ref, mine), (other_ref, 1 - mine))):
+        f_ref[slot] = jnp.zeros((n, n), f32)
+        for p, (i, j) in enumerate(order):
+            x = src[p * BL : (p + 1) * BL, :]
+            f_ref[slot, i * BL : (i + 1) * BL, j * BL : (j + 1) * BL] = x
+            hi, lo = split(x)
+            lh_ref[slot, i * BL : (i + 1) * BL, j * BL : (j + 1) * BL] = hi
+            ll_ref[slot, i * BL : (i + 1) * BL, j * BL : (j + 1) * BL] = lo
+        copies.append(pltpu.make_async_copy(f_ref.at[slot], fac_ref.at[dst], sem.at[slot]))
+        copies[-1].start()
         for k in range(nb):
-            c = k * BL
-            acc = jnp.where(mask, res_ref[:, c : c + BL], 0.0)
-            if k:
-                lh = lh_ref[slot, c : c + BL, :c]
-                ll = ll_ref[slot, c : c + BL, :c]
-                wh = wh_ref[:, :c]
-                wl = wl_ref[:, :c]
-                acc = acc - (dot_nt(wh, lh) + (dot_nt(wh, ll) + dot_nt(wl, lh)))
-            ah, al = split(acc)
-            th = th_ref[slot, c : c + BL, :]
-            tl = tl_ref[slot, c : c + BL, :]
+            p = (len(order) + k) * BL
+            c = (k % 2) * BL
+            hi, lo = split(src[p : p + BL, :])
+            th_ref[slot, k * BL : (k + 1) * BL, c : c + BL] = hi
+            tl_ref[slot, k * BL : (k + 1) * BL, c : c + BL] = lo
+            if k % 2:
+                p = (len(order) + nb + k // 2) * BL
+                hi, lo = split(src[p : p + BL, :])
+            else:
+                hi = lo = jnp.zeros((BL, BL), bf16)
+            th_ref[slot, k * BL : (k + 1) * BL, BL - c : wide - c] = hi
+            tl_ref[slot, k * BL : (k + 1) * BL, BL - c : wide - c] = lo
+
+    for c in range(0, n, wide):
+        for slot in range(2):
+            which = mine if slot == 0 else 1 - mine
+            prod = None
+            if c:
+                lh = lh_ref[slot, c : c + wide, :c]
+                ll = ll_ref[slot, c : c + wide, :c]
+                wh = wh_ref[slot, :, :c]
+                wl = wl_ref[slot, :, :c]
+                prod = dot_nt(wh, lh) + (dot_nt(wh, ll) + dot_nt(wl, lh))
+            accs = []
+            for q in range(chunks):
+                x = res_refs[q][:, :, c : c + wide].reshape(rows, wide)
+                x = jnp.where(tag_refs[q][...] == which + 1, x, 0.0)
+                if prod is not None:
+                    x = x - prod[q * rows : (q + 1) * rows]
+                accs.append(x)
+            ah, al = split(jnp.concatenate(accs, axis=0) if chunks > 1 else accs[0])
+            th = th_ref[slot, c : c + wide, :]
+            tl = tl_ref[slot, c : c + wide, :]
             x = dot_nt(ah, th) + (dot_nt(ah, tl) + dot_nt(al, th))
             hi, lo = split(x)
-            wh_ref[:, c : c + BL] = hi
-            wl_ref[:, c : c + BL] = lo
-            if slot == 0:
-                out_ref[:, c : c + BL] = x
-            else:
-                out_ref[:, c : c + BL] = jnp.where(mask, x, out_ref[:, c : c + BL])
-
-
-def whiten(res, tags, own, other, mine, tile):
-    rows, n = res.shape
-    size = own.shape[0]
-    whole = lambda s: (0, 0)
+            wh_ref[slot, :, c : c + wide] = hi
+            wl_ref[slot, :, c : c + wide] = lo
+            for q in range(chunks):
+                y = x[q * rows : (q + 1) * rows].reshape(sources, part, wide)
+                if slot:
+                    y = y + o_ref[q, :, :, c : c + wide]
+                o_ref[q, :, :, c : c + wide] = y
+        for q in range(chunks):
+            copies.append(
+                pltpu.make_async_copy(
+                    o_ref.at[q, :, :, pl.ds(c, wide)],
+                    out_ref.at[:, pl.ds(q * part, part), pl.ds(c, wide)],
+                    sem.at[2 + (c // wide) * chunks + q],
+                )
+            )
+            copies[-1].start()
+    for copy in copies:
+        copy.wait()
+
+
+def whiten(res, tags, own, other, mine):
+    chunks = len(res)
+    sources, part, n = res[0].shape
+    rows = chunks * sources * part
+    vmem = pl.BlockSpec(memory_space=pltpu.VMEM)
+    hbm = pl.BlockSpec(memory_space=pl.ANY)
     return pl.pallas_call(
-        lambda *refs: whiten_body(n, *refs),
-        grid=(rows // tile,),
-        in_specs=[
-            pl.BlockSpec(memory_space=pltpu.SMEM),
-            pl.BlockSpec((tile, n), lambda s: (s, 0)),
-            pl.BlockSpec((tile, 1), lambda s: (s, 0)),
-            pl.BlockSpec((size, BL), whole),
-            pl.BlockSpec((size, BL), whole),
-        ],
-        out_specs=[
-            pl.BlockSpec((tile, n), lambda s: (s, 0)),
-            pl.BlockSpec((2, n, n), lambda s: (0, 0, 0)),
-        ],
-        out_shape=[jax.ShapeDtypeStruct((rows, n), f32), jax.ShapeDtypeStruct((2, n, n), f32)],
+        lambda *refs: whiten_body(n, chunks, *refs),
+        in_specs=[pl.BlockSpec(memory_space=pltpu.SMEM)] + [vmem] * (2 + 2 * chunks),
+        out_specs=[hbm, hbm],
+        out_shape=[
+            jax.ShapeDtypeStruct((sources, chunks * part, n), f32),
+            jax.ShapeDtypeStruct((2, n, n), f32),
+        ],
         scratch_shapes=[
+            pltpu.VMEM((2, n, n), f32),
+            pltpu.VMEM((chunks, sources, part, n), f32),
             pltpu.VMEM((2, n, n), bf16),
             pltpu.VMEM((2, n, n), bf16),
-            pltpu.VMEM((2, n, BL), bf16),
-            pltpu.VMEM((2, n, BL), bf16),
-            pltpu.VMEM((tile, n), bf16),
-            pltpu.VMEM((tile, n), bf16),
-        ],
-        compiler_params=pltpu.CompilerParams(vmem_limit_bytes=56 << 20),
+            pltpu.VMEM((2, n, 2 * BL), bf16),
+            pltpu.VMEM((2, n, 2 * BL), bf16),
+            pltpu.VMEM((2, rows, n), bf16),
+            pltpu.VMEM((2, rows, n), bf16),
+            pltpu.SemaphoreType.DMA((2 + chunks * (n // (2 * BL)),)),
+        ],
+        compiler_params=pltpu.CompilerParams(vmem_limit_bytes=58 << 20),
         cost_estimate=pl.CostEstimate(flops=12 * rows * n * n, bytes_accessed=16 * n * n, transcendentals=0),
         name="whiten",
-    )(mine, res, tags, own, other)
+    )(mine, own, other, *res, *tags)
 
 
 def flip(x, axis, bit):
@@ -322,6 +365,10 @@
     return [p.reshape(rows // 2, BL) for p in parts]
 
 
+def to_owners(x):
+    return lax.all_to_all(x, ("group", "member"), split_axis=0, concat_axis=0, tiled=True)
+
+
 def on_device(rows, old_list, old_centroids, dest_device, new_local, centroids):
     n_group = lax.axis_size("group")
     n_member = lax.axis_size("member")
@@ -350,29 +397,36 @@
     onehot = (dest[:, None] == jnp.arange(devices, dtype=jnp.int32)[None, :]).astype(jnp.int32)
     ranks = jnp.sum(jnp.cumsum(onehot, axis=0) * onehot, axis=1) - 1
     position = dest * capacity + ranks
-    outgoing = jnp.zeros((devices * capacity, width), f32).at[position].set(residual)
+    chunk = capacity // 2 if capacity % (2 * SUB) == 0 else capacity
+    slot_of = (ranks // chunk) * devices * chunk + dest * chunk + ranks % chunk
+    outgoing = jnp.zeros((devices * capacity, width), f32).at[slot_of].set(residual)
+    outgoing = outgoing.reshape(capacity // chunk, devices, chunk, width)
     out_tags = jnp.zeros((devices * capacity,), jnp.int32).at[position].set(new_local + 1)
     sent = jnp.sum(new_hot, axis=0).astype(jnp.int32).reshape(n_group, lists)
     info = jnp.concatenate(
         [out_tags.reshape(devices, capacity), jnp.repeat(sent, n_member, axis=0)], axis=1
-    )
-    axes = ("group", "member")
-    info = lax.all_to_all(info.reshape(devices, 1, -1), axes, split_axis=0, concat_axis=0, tiled=True)[:, 0]
-    arrived = lax.all_to_all(
-        outgoing.reshape(devices, capacity, width), axes, split_axis=0, concat_axis=0, tiled=True
-    ).reshape(devices * capacity, width)
-    tags = info[:, :capacity].reshape(-1, 1)
-    counts = jnp.sum(info[:, capacity:], axis=0).astype(f32)
-
+    ).reshape(devices, 1, -1)
+
+    first = to_owners(outgoing[0])
     code = ((dest // n_member) * 2 + (new_local ^ core))[:, None]
     away = gram(residual, code, n_group, 1)
-    part = gram(residual, code, n_group, 0) + flip(away, "member", 0)
+    part = gram(residual, code, n_group, 0)
+    part = part + flip(away, "member", 0)
+    info, first = lax.optimization_barrier((info, first))
+    info = to_owners(info)[:, 0]
     pa, pb = sum_and_share(part, n_group, n_member)
+    arrived = [first]
+    for later in outgoing[1:]:
+        later, info, pa, pb = lax.optimization_barrier((later, info, pa, pb))
+        arrived.append(to_owners(later))
+    tags = [info[:, c : c + chunk].reshape(-1, 1) for c in range(0, capacity, chunk)]
+    counts = jnp.sum(info[:, capacity:], axis=0).astype(f32)
     count = lax.dynamic_index_in_dim(counts, core, 0, keepdims=True)
-    own = chol(pa, pb, 1.0 / jnp.maximum(count, 1.0), width)
+    scale = 1.0 / jnp.maximum(count, 1.0)
+    own = chol(pa, pb, scale, width)
     other = flip(own, "member", 0)
-    result, factors = whiten(arrived, tags, own, other, core.reshape(1), min(256, devices * capacity))
-    return (result, factors)
+    result, factors = whiten(arrived, tags, own, other, core.reshape(1))
+    return (result.reshape(devices * capacity, width), factors)
 
 
 def solution(mesh):

time: 302 us -> 253 us (0.84)
  waiting for transfers between devices: 140 us -> 98.9 us
  Pallas kernels: 94.3 us -> 79.5 us
  local copies, waits for them, and re-layouts: 19.6 us -> 24.2 us
    ppermute x16, waiting for transfers between devices: 133 us -> 98.9 us  [flip(): return lax.ppermute(x, axis, [(i, i ^ 1 << bit) for i in range(size)])]
    pallas_call x1, Pallas kernels: 39.8 us -> 22.6 us  [whiten(): pl.pallas_call(lambda *refs: whiten_body(n, chunks, *refs), in_specs=[pl....]
    all_to_all x2 -> x3, waiting for transfers between devices: 6.78 us -> 0.01 us  [to_owners(): lax.all_to_all(x, ('group', 'member'), split_axis=0, concat_axis=0, tiled...]
    slice x1 -> x3, local copies, waits for them, and re-layouts: 0.22 us -> 5.13 us  [the longest x1 4.85 us: on_device(): first = to_owners(outgoing[0])]
    all_to_all x2 -> x3, starting transfers between devices: 8.41 us -> 11.8 us  [to_owners(): lax.all_to_all(x, ('group', 'member'), split_axis=0, concat_axis=0, tiled...]
  transfers between devices with their start and end apart: 19 -> 20, of which waited for: 15 -> 13; matrix products, arithmetic and copies ran while one was open for 9% -> 12% of each run, Pallas kernels for 16% -> 20%
where the time goes in v2:
time: 253 us; the launch traced here: 252 us
  waiting for transfers between devices  98.9 us (39%)
  Pallas kernels  79.5 us (31%)
  starting transfers between devices  28.5 us (11%)
  local copies, waits for them, and re-layouts  24.2 us (10%)
  other arithmetic  13.1 us (5%)
  matrix products  6.35 us (3%)
    ppermute x16, waiting for transfers between devices, flip(): return lax.ppermute(x, axis, [(i, i ^ 1 << bit) for i in range(size)])  98.9 us
    pallas_call x1, Pallas kernels, chol(): pl.pallas_call(lambda *refs: chol_body(n, *refs), in_specs=[pl.BlockSpec(...  44.8 us
    pallas_call x1, Pallas kernels, whiten(): pl.pallas_call(lambda *refs: whiten_body(n, chunks, *refs), in_specs=[pl....  22.6 us
    ppermute x16, starting transfers between devices, flip(): return lax.ppermute(x, axis, [(i, i ^ 1 << bit) for i in range(size)])  13.6 us
    pallas_call x2, Pallas kernels, gram(): pl.pallas_call(lambda *refs: gram_body(rel, *refs), grid=(n_group,), in_s...  12.2 us
    all_to_all x3, starting transfers between devices, to_owners(): lax.all_to_all(x, ('group', 'member'), split_axis=0, concat_axis=0, tiled...  11.8 us
    add x8, other arithmetic, halve(): return lax.dynamic_slice_in_dim(x, b, 1, dim) + got  5.2 us
  transfers between devices with their start and end apart: 20, of which 13 were waited for; matrix products, arithmetic and copies ran while one was open for 12% of the time, Pallas kernels for 20%

profile of v2, /device:TPU:0, one launch (start us, length us, event | category | flops | bytes accessed | tf_op | source)
XLA Modules:
  0.0 252.4 jit_solution(9440605483233303445)
XLA Ops:
  0.7 3.1 %collective-permute-start = (f32[2,1024]{1,0:T(2,128)}, f32[2,1024]{1,0:T(2,128)S(1)}, u32[]{:S(2)}, u32[]{:S(2)}) collective-permute-start(f32[2,1024]{1,0:T(2,128)} %param.11), channel_id=1, source_target_pairs={{0,16},{16,0},{1,17},{17,1},{2,18},{18,2},{3,19},{19,3},{4,20},{20... | collective-permute-start | bytes 24584 | tf_op jit(solution)/shard_map/ppermute | solution.py:386
  3.7 0.7 bitcast_dynamic-update-slice_fusion.1
  4.5 3.0 %fusion.4 = f32[512,1024]{1,0:T(8,128)} fusion(f32[64,1024]{1,0:T(8,128)S(1)} %copy-done, s32[512]{0:T(512)} %param.7), kind=kOutput, calls=%fused_computation.22 | convolution fusion | flops 402685952 | bytes 2361344 | tf_op jit(solution)/shard_map/dot_general | solution.py:394
  7.7 3.3 %add_subtract_fusion.refs_0_ = f32[512,1024]{1,0:T(8,128)S(1)} fusion(f32[512,1024]{1,0:T(8,128)} %param.6, f32[512,1024]{1,0:T(8,128)} %fusion.4, f32[4,1024]{1,0:T(4,128)S(1)} %reshape.733, s32[512]{0:T(512)S(1)} %get-tuple-element.25), kind=kOutput, calls=%fused_computation.2 | convolution fusion | flops 26216448 | bytes 6309888 | tf_op jit(solution)/shard_map/dot_general | solution.py:395
  11.1 6.8 %gram.3 = f32[2,4608,128]{2,1,0:T(8,128)} custom-call(f32[512,1024]{1,0:T(8,128)S(1)} %add_subtract_fusion.refs_0_, s32[512,1]{1,0:T(8,128)S(1)} %copy.27.refs_1_), custom_call_target="tpu_custom_call" | custom-call | flops 3221225472 | bytes 6815744 | tf_op jit(solution)/shard_map/gram/pallas_call | solution.py:74
  17.9 1.2 reduce-window.6
  19.1 5.4 %gram.2 = f32[2,4608,128]{2,1,0:T(8,128)S(1)} custom-call(f32[512,1024]{1,0:T(8,128)S(1)} %add_subtract_fusion.refs_0_, s32[512,1]{1,0:T(8,128)S(1)} %copy.27.refs_1_), custom_call_target="tpu_custom_call" | custom-call | flops 3221225472 | bytes 6815744 | tf_op jit(solution)/shard_map/gram/pallas_call | solution.py:74
  24.5 1.7 collective-permute-done.1
  26.1 2.8 %add.166 = f32[2,4608,128]{2,1,0:T(8,128)S(1)} add(f32[2,4608,128]{2,1,0:T(8,128)S(1)} %gram.2, f32[2,4608,128]{2,1,0:T(8,128)} %collective-permute-done.1) | non-fusion elementwise | flops 1179648 | bytes 14155776 | tf_op jit(solution)/shard_map/add | solution.py:414
  28.9 1.7 fusion.17
  30.7 1.5 copy-done.3
  32.1 1.2 constant_dynamic-slice_fusion.3
  33.3 1.5 collective-permute-start.9
  35.1 2.4 constant_dynamic-slice_fusion.7
  38.1 4.5 %scatter_custom_fusion = f32[1024,1024]{1,0:T(8,128)} fusion(s32[512]{0:T(512)S(1)} %bitcast.69, f32[512,1024]{1,0:T(8,128)S(1)} %add_subtract_fusion.refs_0_, f32[]{:T(128)} %constant.89.clone.1), kind=kCustom, calls=%fused_computation.3 | custom fusion | bytes 4194308 | tf_op jit(solution)/shard_map/scatter | solution.py:402
  42.6 4.8 %fusion.18 = (f32[512,1024]{1,0:T(8,128)}, f32[512,1024]{1,0:T(8,128)}) fusion(f32[1024,1024]{1,0:T(8,128)} %scatter_custom_fusion), kind=kLoop, calls=%fused_computation.72 | loop fusion | bytes 8388608 | tf_op jit(solution)/shard_map/slice | solution.py:410
  47.4 5.2 %all-to-all-start = ((f32[32,16,1024]{2,1,0:T(8,128)}), f32[32,16,1024]{2,1,0:T(8,128)}, u32[]{:S(2)}, u32[]{:S(2)}) async-start(f32[32,16,1024]{2,1,0:T(8,128)} %bitcast.55), calls=%async_computation | async-start | bytes 4194304 | tf_op jit(solution)/shard_map/all_to_all | solution.py:369
  52.7 16.4 %collective-permute-done.9 = f32[2,1,2,2,288,128]{5,4,3,2,1,0:T(8,128)} collective-permute-done((f32[2,1,2,2,288,128]{5,4,3,2,1,0:T(8,128)}, f32[2,1,2,2,288,128]{5,4,3,2,1,0:T(8,128)}, u32[]{:S(2)}, u32[]{:S(2)}) %collective-permute-start.9) | collective-permute-done | bytes 1179680 | tf_op jit(solution)/shard_map/ppermute | solution.py:330
  69.0 1.4 dynamic-slice_add_fusion
  70.6 10.2 %collective-permute-done.2 = f32[1,2,2,2,288,128]{5,4,3,2,1,0:T(8,128)} collective-permute-done((f32[1,2,2,2,288,128]{5,4,3,2,1,0:T(8,128)}, f32[1,2,2,2,288,128]{5,4,3,2,1,0:T(8,128)}, u32[]{:S(2)}, u32[]{:S(2)}) %collective-permute-start.2) | collective-permute-done | bytes 1179680 | tf_op jit(solution)/shard_map/ppermute | solution.py:330
  80.8 1.5 dynamic-slice_add_fusion.1
  82.5 16.7 %collective-permute-done.10 = f32[1,1,2,2,288,128]{5,4,3,2,1,0:T(8,128)S(1)} collective-permute-done((f32[1,1,2,2,288,128]{5,4,3,2,1,0:T(8,128)S(1)}, f32[1,1,2,2,288,128]{5,4,3,2,1,0:T(8,128)S(1)}, u32[]{:S(2)}, u32[]{:S(2)}) %collective-permute-start.10) | collective-permute-done | bytes 589856 | tf_op jit(solution)/shard_map/ppermute | solution.py:330
  99.2 1.1 dynamic-slice_add_fusion.2
  100.4 3.0 %collective-permute-start.11 = (f32[1,1,1,2,288,128]{5,4,3,2,1,0:T(8,128)S(1)}, f32[1,1,1,2,288,128]{5,4,3,2,1,0:T(8,128)S(1)}, u32[]{:S(2)}, u32[]{:S(2)}) collective-permute-start(f32[1,1,1,2,288,128]{5,4,3,2,1,0:T(8,128)S(1)} %constant_dynamic-slice_fusion.1), channel_id=1, source_target_pairs={{0,4},{1,5},{2,6},{3,7},{4,0},{5,1},{6,2},{7,3},{8,12},{9,13},{10,... | collective-permute-start | bytes 884744 | tf_op jit(solution)/shard_map/ppermute | solution.py:330
  103.4 1.1 dynamic-slice_add_fusion.3
  104.7 6.6 %collective-permute-done.11 = f32[1,1,1,2,288,128]{5,4,3,2,1,0:T(8,128)S(1)} collective-permute-done((f32[1,1,1,2,288,128]{5,4,3,2,1,0:T(8,128)S(1)}, f32[1,1,1,2,288,128]{5,4,3,2,1,0:T(8,128)S(1)}, u32[]{:S(2)}, u32[]{:S(2)}) %collective-permute-start.11) | collective-permute-done | bytes 294944 | tf_op jit(solution)/shard_map/ppermute | solution.py:330
  111.3 3.1 %collective-permute-start.12 = (f32[1,1,1,1,288,128]{5,4,3,2,1,0:T(8,128)S(1)}, f32[1,1,1,1,288,128]{5,4,3,2,1,0:T(8,128)S(1)}, u32[]{:S(2)}, u32[]{:S(2)}) collective-permute-start(f32[1,1,1,1,288,128]{5,4,3,2,1,0:T(8,128)S(1)} %constant_dynamic-slice_fusion), channel_id=1, source_target_pairs={{0,8},{1,9},{2,10},{3,11},{4,12},{5,13},{6,14},{7,15},{8,0},{9,1},... | collective-permute-start | bytes 442376 | tf_op jit(solution)/shard_map/ppermute | solution.py:330
  114.4 4.7 %collective-permute-done.4 = f32[1,1,1,2,288,128]{5,4,3,2,1,0:T(8,128)S(1)} collective-permute-done((f32[1,1,1,2,288,128]{5,4,3,2,1,0:T(8,128)S(1)}, f32[1,1,1,2,288,128]{5,4,3,2,1,0:T(8,128)S(1)}, u32[]{:S(2)}, u32[]{:S(2)}) %collective-permute-start.4) | collective-permute-done | bytes 294944 | tf_op jit(solution)/shard_map/ppermute | solution.py:330
  119.2 1.2 collective-permute-start.5
  121.0 6.5 %collective-permute-done.5 = f32[1,1,1,1,288,128]{5,4,3,2,1,0:T(8,128)S(1)} collective-permute-done((f32[1,1,1,1,288,128]{5,4,3,2,1,0:T(8,128)S(1)}, f32[1,1,1,1,288,128]{5,4,3,2,1,0:T(8,128)S(1)}, u32[]{:S(2)}, u32[]{:S(2)}) %collective-permute-start.5) | collective-permute-done | bytes 147488 | tf_op jit(solution)/shard_map/ppermute | solution.py:330
  127.7 3.0 %collective-permute-start.14 = (f32[1,2,1,1,288,128]{5,4,3,2,1,0:T(8,128)S(1)}, f32[1,2,1,1,288,128]{5,4,3,2,1,0:T(8,128)S(1)}, u32[]{:S(2)}, u32[]{:S(2)}) collective-permute-start(f32[1,2,1,1,288,128]{5,4,3,2,1,0:T(8,128)S(1)} %maximum_select_fusion.7), channel_id=1, source_target_pairs={{0,8},{1,9},{2,10},{3,11},{4,12},{5,13},{6,14},{7,15},{8,0},{9,1},... | collective-permute-start | bytes 884744 | tf_op jit(solution)/shard_map/ppermute | solution.py:330
  130.6 12.3 %collective-permute-done.6 = f32[1,1,1,1,288,128]{5,4,3,2,1,0:T(8,128)S(1)} collective-permute-done((f32[1,1,1,1,288,128]{5,4,3,2,1,0:T(8,128)S(1)}, f32[1,1,1,1,288,128]{5,4,3,2,1,0:T(8,128)S(1)}, u32[]{:S(2)}, u32[]{:S(2)}) %collective-permute-start.6) | collective-permute-done | bytes 147488 | tf_op jit(solution)/shard_map/ppermute | solution.py:330
  143.0 6.2 %collective-permute-done.14 = f32[1,2,1,1,288,128]{5,4,3,2,1,0:T(8,128)S(1)} collective-permute-done((f32[1,2,1,1,288,128]{5,4,3,2,1,0:T(8,128)S(1)}, f32[1,2,1,1,288,128]{5,4,3,2,1,0:T(8,128)S(1)}, u32[]{:S(2)}, u32[]{:S(2)}) %collective-permute-start.14) | collective-permute-done | bytes 294944 | tf_op jit(solution)/shard_map/ppermute | solution.py:330
  149.4 6.2 %collective-permute-done.7 = f32[1,1,1,2,288,128]{5,4,3,2,1,0:T(8,128)S(1)} collective-permute-done((f32[1,1,1,2,288,128]{5,4,3,2,1,0:T(8,128)S(1)}, f32[1,1,1,2,288,128]{5,4,3,2,1,0:T(8,128)S(1)}, u32[]{:S(2)}, u32[]{:S(2)}) %collective-permute-start.7) | collective-permute-done | bytes 294944 | tf_op jit(solution)/shard_map/ppermute | solution.py:330
  155.9 2.4 scatter_custom_fusion.1
  158.4 0.7 pad_add_fusion
  159.1 3.1 %all-to-all-start.1 = ((s32[32,1,34]{2,1,0:T(1,128)}), s32[32,1,34]{2,1,0:T(1,128)S(1)}, u32[]{:S(2)}, u32[]{:S(2)}) async-start(s32[32,1,34]{2,1,0:T(1,128)} %bitcast.11), calls=%async_computation.1 | async-start | bytes 32768 | tf_op jit(solution)/shard_map/all_to_all | solution.py:369
  162.1 6.2 %collective-permute-done.15 = f32[1,2,1,2,288,128]{5,4,3,2,1,0:T(8,128)} collective-permute-done((f32[1,2,1,2,288,128]{5,4,3,2,1,0:T(8,128)S(1)}, f32[1,2,1,2,288,128]{5,4,3,2,1,0:T(8,128)}, u32[]{:S(2)}, u32[]{:S(2)}) %collective-permute-start.15) | collective-permute-done | bytes 589856 | tf_op jit(solution)/shard_map/ppermute | solution.py:330
  168.4 1.3 maximum_select_fusion.1
  169.7 1.3 collective-permute-done.8
  171.0 1.3 maximum_select_fusion
  173.8 3.5 %all-to-all-start.2 = ((f32[32,16,1024]{2,1,0:T(8,128)}), f32[32,16,1024]{2,1,0:T(8,128)}, u32[]{:S(2)}, u32[]{:S(2)}) async-start(f32[32,16,1024]{2,1,0:T(8,128)} %bitcast.54), calls=%async_computation.2 | async-start | bytes 4194304 | tf_op jit(solution)/shard_map/all_to_all | solution.py:369
  177.3 44.8 %chol.1.refs_1_ = f32[6144,128]{1,0:T(8,128)} custom-call(f32[1]{0:T(128)S(6)} %div.35.refs_0_, f32[2304,128]{1,0:T(8,128)S(1)} %bitcast.49, f32[2304,128]{1,0:T(8,128)S(1)} %bitcast.48), custom_call_target="tpu_custom_call" | custom-call | flops 42949672960 | bytes 4718592 | tf_op jit(solution)/shard_map/chol/pallas_call | solution.py:196
  222.1 0.9 reshape.759.refs_6_
  223.0 0.9 reshape.758.refs_5_
  223.9 4.0 %collective-permute-done.16.refs_2_ = f32[6144,128]{1,0:T(8,128)S(1)} collective-permute-done((f32[6144,128]{1,0:T(8,128)}, f32[6144,128]{1,0:T(8,128)S(1)}, u32[]{:S(2)}, u32[]{:S(2)}) %collective-permute-start.16) | collective-permute-done | bytes 3145760 | tf_op jit(solution)/shard_map/ppermute | solution.py:330
  227.9 1.7 copy-done.8
  229.6 22.6 %whiten.1 = (f32[32,32,1024]{2,1,0:T(8,128)}, f32[2,1024,1024]{2,1,0:T(8,128)}) custom-call(s32[1]{0:T(128)} %bitcast.refs_0_, f32[6144,128]{1,0:T(8,128)} %chol.1.refs_1_, f32[6144,128]{1,0:T(8,128)} %copy-done.8, f32[32,16,1024]{2,1,0:T(8,128)} %all-to-all-done.refs_3_, f32[32,16,1024]{2,1,0:T(8,128)} %all-to-all-done.2.refs_4_, ...), custom_call_target="tpu_custom_call" | custom-call | flops 12884901888 | bytes 16777216 | tf_op jit(solution)/shard_map/whiten/pallas_call | solution.py:303
  (71 shorter events, 4.0 us)
Async XLA Ops:
  0.6 3.8 %copy-start = (f32[64,1024]{1,0:T(8,128)S(1)}, f32[64,1024]{1,0:T(8,128)}, u32[]{:S(2)}) copy-start(f32[64,1024]{1,0:T(8,128)} %param.8) | copy-start | bytes 786436
  0.6 6.8 %copy-start.6 = (s32[512,1]{0,1:T(1,128)S(1)}, s32[512,1]{0,1:T(1,128)}, u32[]{:S(2)}) copy-start(s32[512,1]{0,1:T(1,128)} %param.9) | copy-start | bytes 6148
  0.7 6.8 %copy-start.7 = (s32[512]{0:T(512)S(1)}, s32[512]{0:T(512)}, u32[]{:S(2)}) copy-start(s32[512]{0:T(512)} %param.10) | copy-start | bytes 6148
  0.7 7.0 %collective-permute-start = (f32[2,1024]{1,0:T(2,128)}, f32[2,1024]{1,0:T(2,128)S(1)}, u32[]{:S(2)}, u32[]{:S(2)}) collective-permute-start(f32[2,1024]{1,0:T(2,128)} %param.11), channel_id=1, source_target_pairs={{0,16},{16,0},{1,17},{17,1},{2,18},{18,2},{3,19},{19,3},{4,20},{20... | collective-permute-start | bytes 24584 | tf_op jit(solution)/shard_map/ppermute | solution.py:386
  17.9 8.3 %collective-permute-start.1 = (f32[2,4608,128]{2,1,0:T(8,128)}, f32[2,4608,128]{2,1,0:T(8,128)}, u32[]{:S(2)}, u32[]{:S(2)}) collective-permute-start(f32[2,4608,128]{2,1,0:T(8,128)} %gram.3), channel_id=1, source_target_pairs={{0,1},{1,0},{2,3},{3,2},{4,5},{5,4},{6,7},{7,6},{8,9},{9,8},{10,11... | collective-permute-start | bytes 14155784 | tf_op jit(solution)/shard_map/ppermute | solution.py:330
  30.7 1.5 copy-start.3
  33.3 35.7 %collective-permute-start.9 = (f32[2,1,2,2,288,128]{5,4,3,2,1,0:T(8,128)}, f32[2,1,2,2,288,128]{5,4,3,2,1,0:T(8,128)}, u32[]{:S(2)}, u32[]{:S(2)}) collective-permute-start(f32[2,1,2,2,288,128]{5,4,3,2,1,0:T(8,128)} %constant_dynamic-slice_fusion.3), channel_id=1, source_target_pairs={{0,2},{1,3},{2,0},{3,1},{4,6},{5,7},{6,4},{7,5},{8,10},{9,11},{10,... | collective-permute-start | bytes 3538952 | tf_op jit(solution)/shard_map/ppermute | solution.py:330
  37.6 43.2 %collective-permute-start.2 = (f32[1,2,2,2,288,128]{5,4,3,2,1,0:T(8,128)}, f32[1,2,2,2,288,128]{5,4,3,2,1,0:T(8,128)}, u32[]{:S(2)}, u32[]{:S(2)}) collective-permute-start(f32[1,2,2,2,288,128]{5,4,3,2,1,0:T(8,128)} %constant_dynamic-slice_fusion.7), channel_id=1, source_target_pairs={{0,16},{16,0},{1,17},{17,1},{2,18},{18,2},{3,19},{19,3},{4,20},{20... | collective-permute-start | bytes 3538952 | tf_op jit(solution)/shard_map/ppermute | solution.py:330
  47.4 21.6 %copy-start.4 = (f32[2,2304,128]{2,1,0:T(8,128)S(1)}, f32[2,2304,128]{2,1,0:T(8,128)}, u32[]{:S(2)}) copy-start(f32[2,2304,128]{2,1,0:T(8,128)} %copy-done.3) | copy-start | bytes 7077892
  47.4 111.6 %all-to-all-start = ((f32[32,16,1024]{2,1,0:T(8,128)}), f32[32,16,1024]{2,1,0:T(8,128)}, u32[]{:S(2)}, u32[]{:S(2)}) async-start(f32[32,16,1024]{2,1,0:T(8,128)} %bitcast.55), calls=%async_computation | async-start | bytes 4194304 | tf_op jit(solution)/shard_map/all_to_all | solution.py:369
  52.7 28.1 %copy-start.2 = (f32[2,2304,128]{2,1,0:T(8,128)S(1)}, f32[2,2304,128]{2,1,0:T(8,128)}, u32[]{:S(2)}) copy-start(f32[2,2304,128]{2,1,0:T(8,128)} %get-tuple-element.19) | copy-start | bytes 7077892
  70.4 11.8 %copy-start.5 = (f32[2,1,2,2,288,128]{5,4,3,2,1,0:T(8,128)}, f32[2,1,2,2,288,128]{5,4,3,2,1,0:T(8,128)S(1)}, u32[]{:S(2)}) copy-start(f32[2,1,2,2,288,128]{5,4,3,2,1,0:T(8,128)S(1)} %dynamic-slice_add_fusion) | copy-start | bytes 3538948
  70.5 28.7 %collective-permute-start.10 = (f32[1,1,2,2,288,128]{5,4,3,2,1,0:T(8,128)S(1)}, f32[1,1,2,2,288,128]{5,4,3,2,1,0:T(8,128)S(1)}, u32[]{:S(2)}, u32[]{:S(2)}) collective-permute-start(f32[1,1,2,2,288,128]{5,4,3,2,1,0:T(8,128)S(1)} %constant_dynamic-slice_fusion.2), channel_id=1, source_target_pairs={{0,16},{16,0},{1,17},{17,1},{2,18},{18,2},{3,19},{19,3},{4,20},{20... | collective-permute-start | bytes 1769480 | tf_op jit(solution)/shard_map/ppermute | solution.py:330
  82.3 21.1 %collective-permute-start.3 = (f32[1,1,2,2,288,128]{5,4,3,2,1,0:T(8,128)S(1)}, f32[1,1,2,2,288,128]{5,4,3,2,1,0:T(8,128)}, u32[]{:S(2)}, u32[]{:S(2)}) collective-permute-start(f32[1,1,2,2,288,128]{5,4,3,2,1,0:T(8,128)S(1)} %constant_dynamic-slice_fusion.6), channel_id=1, source_target_pairs={{0,2},{1,3},{2,0},{3,1},{4,6},{5,7},{6,4},{7,5},{8,10},{9,11},{10,... | collective-permute-start | bytes 1769480 | tf_op jit(solution)/shard_map/ppermute | solution.py:330
  100.4 10.9 %collective-permute-start.11 = (f32[1,1,1,2,288,128]{5,4,3,2,1,0:T(8,128)S(1)}, f32[1,1,1,2,288,128]{5,4,3,2,1,0:T(8,128)S(1)}, u32[]{:S(2)}, u32[]{:S(2)}) collective-permute-start(f32[1,1,1,2,288,128]{5,4,3,2,1,0:T(8,128)S(1)} %constant_dynamic-slice_fusion.1), channel_id=1, source_target_pairs={{0,4},{1,5},{2,6},{3,7},{4,0},{5,1},{6,2},{7,3},{8,12},{9,13},{10,... | collective-permute-start | bytes 884744 | tf_op jit(solution)/shard_map/ppermute | solution.py:330
  104.6 14.6 %collective-permute-start.4 = (f32[1,1,1,2,288,128]{5,4,3,2,1,0:T(8,128)S(1)}, f32[1,1,1,2,288,128]{5,4,3,2,1,0:T(8,128)S(1)}, u32[]{:S(2)}, u32[]{:S(2)}) collective-permute-start(f32[1,1,1,2,288,128]{5,4,3,2,1,0:T(8,128)S(1)} %constant_dynamic-slice_fusion.5), channel_id=1, source_target_pairs={{0,4},{1,5},{2,6},{3,7},{4,0},{5,1},{6,2},{7,3},{8,12},{9,13},{10,... | collective-permute-start | bytes 884744 | tf_op jit(solution)/shard_map/ppermute | solution.py:330
  111.3 9.1 %collective-permute-start.12 = (f32[1,1,1,1,288,128]{5,4,3,2,1,0:T(8,128)S(1)}, f32[1,1,1,1,288,128]{5,4,3,2,1,0:T(8,128)S(1)}, u32[]{:S(2)}, u32[]{:S(2)}) collective-permute-start(f32[1,1,1,1,288,128]{5,4,3,2,1,0:T(8,128)S(1)} %constant_dynamic-slice_fusion), channel_id=1, source_target_pairs={{0,8},{1,9},{2,10},{3,11},{4,12},{5,13},{6,14},{7,15},{8,0},{9,1},... | collective-permute-start | bytes 442376 | tf_op jit(solution)/shard_map/ppermute | solution.py:330
  119.2 8.3 %collective-permute-start.5 = (f32[1,1,1,1,288,128]{5,4,3,2,1,0:T(8,128)S(1)}, f32[1,1,1,1,288,128]{5,4,3,2,1,0:T(8,128)S(1)}, u32[]{:S(2)}, u32[]{:S(2)}) collective-permute-start(f32[1,1,1,1,288,128]{5,4,3,2,1,0:T(8,128)S(1)} %constant_dynamic-slice_fusion.4), channel_id=1, source_target_pairs={{0,8},{1,9},{2,10},{3,11},{4,12},{5,13},{6,14},{7,15},{8,0},{9,1},... | collective-permute-start | bytes 442376 | tf_op jit(solution)/shard_map/ppermute | solution.py:330
  120.4 7.2 %collective-permute-start.13 = (f32[1,1,1,1,288,128]{5,4,3,2,1,0:T(8,128)S(1)}, f32[1,1,1,1,288,128]{5,4,3,2,1,0:T(8,128)S(1)}, u32[]{:S(2)}, u32[]{:S(2)}) collective-permute-start(f32[1,1,1,1,288,128]{5,4,3,2,1,0:T(8,128)S(1)} %dynamic-slice_add_fusion.6), channel_id=1, source_target_pairs={{0,2},{1,3},{2,0},{3,1},{4,6},{5,7},{6,4},{7,5},{8,10},{9,11},{10,... | collective-permute-start | bytes 442376 | tf_op jit(solution)/shard_map/ppermute | solution.py:330
  127.5 15.3 %collective-permute-start.6 = (f32[1,1,1,1,288,128]{5,4,3,2,1,0:T(8,128)S(1)}, f32[1,1,1,1,288,128]{5,4,3,2,1,0:T(8,128)S(1)}, u32[]{:S(2)}, u32[]{:S(2)}) collective-permute-start(f32[1,1,1,1,288,128]{5,4,3,2,1,0:T(8,128)S(1)} %dynamic-slice_add_fusion.7), channel_id=1, source_target_pairs={{0,8},{1,9},{2,10},{3,11},{4,12},{5,13},{6,14},{7,15},{8,0},{9,1},... | collective-permute-start | bytes 442376 | tf_op jit(solution)/shard_map/ppermute | solution.py:330
  127.7 21.5 %collective-permute-start.14 = (f32[1,2,1,1,288,128]{5,4,3,2,1,0:T(8,128)S(1)}, f32[1,2,1,1,288,128]{5,4,3,2,1,0:T(8,128)S(1)}, u32[]{:S(2)}, u32[]{:S(2)}) collective-permute-start(f32[1,2,1,1,288,128]{5,4,3,2,1,0:T(8,128)S(1)} %maximum_select_fusion.7), channel_id=1, source_target_pairs={{0,8},{1,9},{2,10},{3,11},{4,12},{5,13},{6,14},{7,15},{8,0},{9,1},... | collective-permute-start | bytes 884744 | tf_op jit(solution)/shard_map/ppermute | solution.py:330
  142.9 12.6 %collective-permute-start.7 = (f32[1,1,1,2,288,128]{5,4,3,2,1,0:T(8,128)S(1)}, f32[1,1,1,2,288,128]{5,4,3,2,1,0:T(8,128)S(1)}, u32[]{:S(2)}, u32[]{:S(2)}) collective-permute-start(f32[1,1,1,2,288,128]{5,4,3,2,1,0:T(8,128)S(1)} %maximum_select_fusion.5), channel_id=1, source_target_pairs={{0,4},{1,5},{2,6},{3,7},{4,0},{5,1},{6,2},{7,3},{8,12},{9,13},{10,... | collective-permute-start | bytes 884744 | tf_op jit(solution)/shard_map/ppermute | solution.py:330
  149.2 19.1 %collective-permute-start.15 = (f32[1,2,1,2,288,128]{5,4,3,2,1,0:T(8,128)S(1)}, f32[1,2,1,2,288,128]{5,4,3,2,1,0:T(8,128)}, u32[]{:S(2)}, u32[]{:S(2)}) collective-permute-start(f32[1,2,1,2,288,128]{5,4,3,2,1,0:T(8,128)S(1)} %maximum_select_fusion.3), channel_id=1, source_target_pairs={{0,4},{1,5},{2,6},{3,7},{4,0},{5,1},{6,2},{7,3},{8,12},{9,13},{10,... | collective-permute-start | bytes 1769480 | tf_op jit(solution)/shard_map/ppermute | solution.py:330
  155.6 15.5 %collective-permute-start.8 = (f32[1,1,2,2,288,128]{5,4,3,2,1,0:T(8,128)S(1)}, f32[1,1,2,2,288,128]{5,4,3,2,1,0:T(8,128)}, u32[]{:S(2)}, u32[]{:S(2)}) collective-permute-start(f32[1,1,2,2,288,128]{5,4,3,2,1,0:T(8,128)S(1)} %maximum_select_fusion.2), channel_id=1, source_target_pairs={{0,2},{1,3},{2,0},{3,1},{4,6},{5,7},{6,4},{7,5},{8,10},{9,11},{10,... | collective-permute-start | bytes 1769480 | tf_op jit(solution)/shard_map/ppermute | solution.py:330
  159.1 13.3 %all-to-all-start.1 = ((s32[32,1,34]{2,1,0:T(1,128)}), s32[32,1,34]{2,1,0:T(1,128)S(1)}, u32[]{:S(2)}, u32[]{:S(2)}) async-start(s32[32,1,34]{2,1,0:T(1,128)} %bitcast.11), calls=%async_computation.1 | async-start | bytes 32768 | tf_op jit(solution)/shard_map/all_to_all | solution.py:369
  173.8 54.1 %all-to-all-start.2 = ((f32[32,16,1024]{2,1,0:T(8,128)}), f32[32,16,1024]{2,1,0:T(8,128)}, u32[]{:S(2)}, u32[]{:S(2)}) async-start(f32[32,16,1024]{2,1,0:T(8,128)} %bitcast.54), calls=%async_computation.2 | async-start | bytes 4194304 | tf_op jit(solution)/shard_map/all_to_all | solution.py:369
  222.0 5.9 %collective-permute-start.16 = (f32[6144,128]{1,0:T(8,128)}, f32[6144,128]{1,0:T(8,128)S(1)}, u32[]{:S(2)}, u32[]{:S(2)}) collective-permute-start(f32[6144,128]{1,0:T(8,128)} %chol.1.refs_1_), channel_id=1, source_target_pairs={{0,1},{1,0},{2,3},{3,2},{4,5},{5,4},{6,7},{7,6},{8,9},{9,8},{10,11... | collective-permute-start | bytes 9437192 | tf_op jit(solution)/shard_map/ppermute | solution.py:330
  227.9 1.7 copy-start.8
  229.6 22.6 %copy-start.1 = (f32[64,1024]{1,0:T(8,128)S(1)}, f32[64,1024]{1,0:T(8,128)}, u32[]{:S(2)}) copy-start(f32[64,1024]{1,0:T(8,128)} %param.8) | copy-start | bytes 786436

commit v3 on v2

--- a/solution.py
+++ b/solution.py
@@ -37,49 +37,149 @@
     return [(i, j) for j in range(nb) for i in range(j, nb)]
 
 
-def gram_body(rel, res_ref, code_ref, out_ref, th_ref, tl_ref, h_ref, l_ref):
+def split3(x):
+    hi = x.astype(bf16)
+    rest = x - hi.astype(f32)
+    mid = rest.astype(bf16)
+    return hi, mid, (rest - mid.astype(f32)).astype(bf16)
+
+
+def table_rows(index, table):
+    count = table.shape[0]
+    hot = (lax.broadcasted_iota(jnp.int32, (count, index.shape[1]), 0) == index).astype(f32)
+    hot = jnp.concatenate([hot] * 3, axis=0).astype(bf16)
+    return lax.dot_general(
+        hot, jnp.concatenate(split3(table), axis=0), (((0,), (0,)), ((), ())), preferred_element_type=f32
+    )
+
+
+def route_body(sizes, ids_ref, rows_ref, old_ref, dest_ref, local_ref, table_ref, *refs):
+    n_group, n_member, capacity, chunk = sizes
+    devices = n_group * n_member
+    chunks = capacity // chunk
+    out_refs = refs[:chunks]
+    vec_ref, info_ref, code_ref, o_ref, sem = refs[chunks:]
+    count, _ = rows_ref.shape
+    group, core = ids_ref[0], ids_ref[1]
+    dest = dest_ref[...]
+    local = local_ref[...]
+    shift = n_member.bit_length() - 1
+    device = lax.broadcasted_iota(jnp.int32, (devices, count), 0)
+    onehot = (device == dest).astype(f32)
+    earlier = lax.broadcasted_iota(jnp.int32, (count, count), 0) < lax.broadcasted_iota(jnp.int32, (count, count), 1)
+    ahead = dot_nn(onehot.astype(bf16), earlier.astype(f32).astype(bf16))
+    rank = jnp.sum(onehot * ahead, axis=0, keepdims=True).astype(jnp.int32)
+    low = chunk.bit_length() - 1
+    place = (rank >> low) * (devices * chunk) + dest * chunk + (rank & (chunk - 1))
+
+    to_group = dest >> shift
+    row = lax.broadcasted_iota(jnp.int32, (SUB, count), 0)
+    code = to_group * 2 + (local ^ core)
+    seen = ((group - to_group) & (n_group - 1)) * 2 + local
+    code_ref[...] = jnp.where(row == 0, code, seen)
+
+    slot = lax.broadcasted_iota(jnp.int32, (BL, count), 0)
+    left = jnp.concatenate(
+        [onehot * (local + 1).astype(f32), ((device >> shift) == to_group).astype(f32)], axis=1
+    )
+    right = jnp.concatenate(
+        [((slot == rank) & (slot < capacity)).astype(f32), ((slot - capacity) == local).astype(f32)], axis=1
+    )
+    info_ref[...] = dot_nt(left.astype(bf16), right.astype(bf16)).astype(jnp.int32)
+
+    vec = rows_ref[...] + table_rows(old_ref[...], table_ref[...])
+    vec_ref[...] = vec
+    hi, mid, lo = split3(vec)
+    copies = []
+    for q in range(chunks):
+        for r in range(0, devices * chunk, 2 * BL):
+            base = q * devices * chunk + r
+            pick = (lax.broadcasted_iota(jnp.int32, (2 * BL, count), 0) + base == place).astype(f32).astype(bf16)
+            o_ref[base : base + 2 * BL, :] = dot_nn(pick, hi) + (dot_nn(pick, mid) + dot_nn(pick, lo))
+            copies.append(
+                pltpu.make_async_copy(
+                    o_ref.at[pl.ds(base, 2 * BL), :], out_refs[q].at[pl.ds(r, 2 * BL), :], sem.at[base // (2 * BL)]
+                )
+            )
+            copies[-1].start()
+    for copy in copies:
+        copy.wait()
+
+
+def route(ids, rows, old, dest, local, table, sizes):
+    n_group, n_member, capacity, chunk = sizes
+    devices = n_group * n_member
+    count, n = rows.shape
+    chunks = capacity // chunk
+    vmem = pl.BlockSpec(memory_space=pltpu.VMEM)
+    return pl.pallas_call(
+        lambda *refs: route_body(sizes, *refs),
+        in_specs=[pl.BlockSpec(memory_space=pltpu.SMEM)] + [vmem] * 5,
+        out_specs=[pl.BlockSpec(memory_space=pl.ANY)] * chunks + [vmem] * 3,
+        out_shape=[jax.ShapeDtypeStruct((devices * chunk, n), f32)] * chunks
+        + [
+            jax.ShapeDtypeStruct((count, n), f32),
+            jax.ShapeDtypeStruct((devices, BL), jnp.int32),
+            jax.ShapeDtypeStruct((SUB, count), jnp.int32),
+        ],
+        scratch_shapes=[
+            pltpu.VMEM((devices * capacity, n), f32),
+            pltpu.SemaphoreType.DMA((devices * capacity // (2 * BL),)),
+        ],
+        compiler_params=pltpu.CompilerParams(vmem_limit_bytes=40 << 20),
+        cost_estimate=pl.CostEstimate(
+            flops=6 * devices * capacity * count * n, bytes_accessed=4 * devices * capacity * n, transcendentals=0
+        ),
+        name="route",
+    )(ids, rows, old, dest, local, table)
+
+
+def gram_body(rel, vec_ref, code_ref, table_ref, a_ref, b_ref, th_ref, tl_ref, h_ref, l_ref):
     g = pl.program_id(0)
-    _, n = res_ref.shape
+    _, n = vec_ref.shape
+    order = blocks(n)
+    half = len(order) // 2
 
     @pl.when(g == 0)
     def _():
+        x = vec_ref[...] - table_rows(code_ref[1:2, :], table_ref[...])
+        hi, lo = split(x)
+        h_ref[...] = hi
+        l_ref[...] = lo
         for j in range(0, n, BL):
-            x = res_ref[:, j : j + BL]
-            hi, lo = split(x)
-            h_ref[:, j : j + BL] = hi
-            l_ref[:, j : j + BL] = lo
-            xt = x.T
-            hi, lo = split(xt)
+            hi, lo = split(x[:, j : j + BL].T)
             th_ref[j : j + BL, :] = hi
             tl_ref[j : j + BL, :] = lo
 
-    mask = code_ref[...] == 2 * g + rel
-    place = {b: p for p, b in enumerate(blocks(n))}
+    mask = (code_ref[0:1, :] == 2 * g + rel).astype(f32).astype(bf16)
+    place = {b: p for p, b in enumerate(order)}
     for j in range(0, n, 2 * BL):
-        mh = jnp.where(mask, h_ref[:, j : j + 2 * BL], jnp.zeros((), bf16))
-        ml = jnp.where(mask, l_ref[:, j : j + 2 * BL], jnp.zeros((), bf16))
-        th = th_ref[j:n, :]
-        tl = tl_ref[j:n, :]
+        mh = h_ref[:, j : j + 2 * BL]
+        ml = l_ref[:, j : j + 2 * BL]
+        th = th_ref[j:n, :] * mask
+        tl = tl_ref[j:n, :] * mask
         prod = dot_nn(th, mh) + (dot_nn(th, ml) + dot_nn(tl, mh))
         for i in range(j, n, BL):
             for c in (j, j + BL):
                 if i >= c:
                     p = place[(i // BL, c // BL)]
-                    out_ref[0, p * BL : (p + 1) * BL, :] = prod[i - j : i - j + BL, c - j : c - j + BL]
-
-
-def gram(res, code, n_group, rel):
-    rows, n = res.shape
-    size = len(blocks(n)) * BL
+                    dst, p = (a_ref, p) if p < half else (b_ref, p - half)
+                    dst[0, p * BL : (p + 1) * BL, :] = prod[i - j : i - j + BL, c - j : c - j + BL]
+
+
+def gram(vec, code, table, n_group, rel):
+    rows, n = vec.shape
+    size = len(blocks(n)) * BL // 2
     return pl.pallas_call(
         lambda *refs: gram_body(rel, *refs),
         grid=(n_group,),
         in_specs=[
             pl.BlockSpec((rows, n), lambda g: (0, 0)),
-            pl.BlockSpec((rows, 1), lambda g: (0, 0)),
-        ],
-        out_specs=pl.BlockSpec((1, size, BL), lambda g: (g, 0, 0)),
-        out_shape=jax.ShapeDtypeStruct((n_group, size, BL), f32),
+            pl.BlockSpec(code.shape, lambda g: (0, 0)),
+            pl.BlockSpec(table.shape, lambda g: (0, 0)),
+        ],
+        out_specs=[pl.BlockSpec((1, size, BL), lambda g: (g, 0, 0))] * 2,
+        out_shape=[jax.ShapeDtypeStruct((n_group, size, BL), f32)] * 2,
         scratch_shapes=[
             pltpu.VMEM((n, rows), bf16),
             pltpu.VMEM((n, rows), bf16),
@@ -88,10 +188,10 @@
         ],
         compiler_params=pltpu.CompilerParams(vmem_limit_bytes=40 << 20),
         cost_estimate=pl.CostEstimate(
-            flops=3 * n_group * rows * n * n, bytes_accessed=4 * (rows * n + n_group * size * BL), transcendentals=0
+            flops=3 * n_group * rows * n * n, bytes_accessed=4 * (rows * n + 2 * n_group * size * BL), transcendentals=0
         ),
         name="gram",
-    )(res, code)
+    )(vec, code, table)
 
 
 def diag_group(b, tt, s):
@@ -216,10 +316,10 @@
 
 
 def whiten_body(n, chunks, *refs):
-    mine_ref, own_ref, other_ref = refs[:3]
-    res_refs = refs[3 : 3 + chunks]
-    tag_refs = refs[3 + chunks : 3 + 2 * chunks]
-    out_ref, fac_ref, f_ref, o_ref, lh_ref, ll_ref, th_ref, tl_ref, wh_ref, wl_ref, sem = refs[3 + 2 * chunks :]
+    mine_ref, cent_ref, own_ref, other_ref = refs[:4]
+    res_refs = refs[4 : 4 + chunks]
+    tag_refs = refs[4 + chunks : 4 + 2 * chunks]
+    out_ref, fac_ref, f_ref, o_ref, lh_ref, ll_ref, th_ref, tl_ref, wh_ref, wl_ref, sem = refs[4 + 2 * chunks :]
     order = blocks(n)
     nb = n // BL
     wide = 2 * BL
@@ -265,7 +365,7 @@
             accs = []
             for q in range(chunks):
                 x = res_refs[q][:, :, c : c + wide].reshape(rows, wide)
-                x = jnp.where(tag_refs[q][...] == which + 1, x, 0.0)
+                x = jnp.where(tag_refs[q][...] == which + 1, x - cent_ref[pl.ds(which, 1), c : c + wide], 0.0)
                 if prod is not None:
                     x = x - prod[q * rows : (q + 1) * rows]
                 accs.append(x)
@@ -294,7 +394,7 @@
         copy.wait()
 
 
-def whiten(res, tags, own, other, mine):
+def whiten(res, tags, own, other, mine, centroids):
     chunks = len(res)
     sources, part, n = res[0].shape
     rows = chunks * sources * part
@@ -302,7 +402,7 @@
     hbm = pl.BlockSpec(memory_space=pl.ANY)
     return pl.pallas_call(
         lambda *refs: whiten_body(n, chunks, *refs),
-        in_specs=[pl.BlockSpec(memory_space=pltpu.SMEM)] + [vmem] * (2 + 2 * chunks),
+        in_specs=[pl.BlockSpec(memory_space=pltpu.SMEM)] + [vmem] * (3 + 2 * chunks),
         out_specs=[hbm, hbm],
         out_shape=[
             jax.ShapeDtypeStruct((sources, chunks * part, n), f32),
@@ -322,7 +422,7 @@
         compiler_params=pltpu.CompilerParams(vmem_limit_bytes=58 << 20),
         cost_estimate=pl.CostEstimate(flops=12 * rows * n * n, bytes_accessed=16 * n * n, transcendentals=0),
         name="whiten",
-    )(mine, own, other, *res, *tags)
+    )(mine, centroids, own, other, *res, *tags)
 
 
 def flip(x, axis, bit):
@@ -346,23 +446,21 @@
     return jnp.where(low, jnp.concatenate([x, got], dim), jnp.concatenate([got, x], dim))
 
 
-def sum_and_share(part, n_group, n_member):
+def sum_and_share(parts, n_group, n_member):
     gbits = n_group.bit_length() - 1
     mbits = n_member.bit_length() - 1
-    rows = part.shape[1]
+    rows = parts[0].shape[1]
     shape = (2,) * gbits + (2,) * (mbits - 1)
     ghalf = [("group", b, gbits - 1 - b) for b in range(gbits)]
     mhalf = [("member", b, gbits + b - 1) for b in range(1, mbits)]
     plans = [ghalf + mhalf, mhalf[:1] + ghalf + mhalf[1:]]
     gathers = [mhalf[::-1], mhalf[:1] + mhalf[:0:-1]]
-    parts = [
-        part[:, c * (rows // 2) : (c + 1) * (rows // 2)].reshape(shape + (rows >> mbits, BL)) for c in range(2)
-    ]
+    parts = [p.reshape(shape + (rows >> (mbits - 1), BL)) for p in parts]
     for step in range(gbits + mbits - 1):
         parts = [halve(parts[c], *plans[c][step]) for c in range(2)]
     for step in range(mbits - 1):
         parts = [double(parts[c], *gathers[c][step]) for c in range(2)]
-    return [p.reshape(rows // 2, BL) for p in parts]
+    return [p.reshape(rows, BL) for p in parts]
 
 
 def to_owners(x):
@@ -379,53 +477,42 @@
     group = lax.axis_index("group")
     core = lax.axis_index("member") & 1
 
-    every = jnp.zeros((n_group,) + centroids.shape, f32)
-    for shift in range(n_group):
-        got = centroids
-        if shift:
-            got = lax.ppermute(centroids, "group", [(i, (i + shift) % n_group) for i in range(n_group)])
-        every = lax.dynamic_update_index_in_dim(every, got, (group - shift) % n_group, 0)
-    every = every.reshape(n_group * lists, width)
-
-    dest = dest_device[:, 0]
-    new_list = (dest // n_member) * lists + new_local
-    old_hot = (old_list[:, None] == jnp.arange(old_centroids.shape[0], dtype=jnp.int32)[None, :]).astype(f32)
-    new_hot = (new_list[:, None] == jnp.arange(n_group * lists, dtype=jnp.int32)[None, :]).astype(f32)
-    vectors = rows + jnp.dot(old_hot, old_centroids, precision=lax.Precision.HIGHEST)
-    residual = vectors - jnp.dot(new_hot, every, precision=lax.Precision.HIGHEST)
-
-    onehot = (dest[:, None] == jnp.arange(devices, dtype=jnp.int32)[None, :]).astype(jnp.int32)
-    ranks = jnp.sum(jnp.cumsum(onehot, axis=0) * onehot, axis=1) - 1
-    position = dest * capacity + ranks
+    seen = [centroids]
+    for shift in range(1, n_group):
+        seen.append(lax.ppermute(centroids, "group", [(i, (i + shift) % n_group) for i in range(n_group)]))
+    spare = -(n_group * lists) % SUB
+    seen = jnp.concatenate(seen + [jnp.zeros((spare, width), f32)] * (spare > 0), axis=0)
+
     chunk = capacity // 2 if capacity % (2 * SUB) == 0 else capacity
-    slot_of = (ranks // chunk) * devices * chunk + dest * chunk + ranks % chunk
-    outgoing = jnp.zeros((devices * capacity, width), f32).at[slot_of].set(residual)
-    outgoing = outgoing.reshape(capacity // chunk, devices, chunk, width)
-    out_tags = jnp.zeros((devices * capacity,), jnp.int32).at[position].set(new_local + 1)
-    sent = jnp.sum(new_hot, axis=0).astype(jnp.int32).reshape(n_group, lists)
-    info = jnp.concatenate(
-        [out_tags.reshape(devices, capacity), jnp.repeat(sent, n_member, axis=0)], axis=1
-    ).reshape(devices, 1, -1)
+    *outgoing, vectors, info, code = route(
+        jnp.stack([group, core]),
+        rows,
+        old_list.reshape(1, -1),
+        dest_device.reshape(1, -1),
+        new_local.reshape(1, -1),
+        old_centroids,
+        (n_group, n_member, capacity, chunk),
+    )
+    outgoing = [x.reshape(devices, chunk, width) for x in outgoing]
 
     first = to_owners(outgoing[0])
-    code = ((dest // n_member) * 2 + (new_local ^ core))[:, None]
-    away = gram(residual, code, n_group, 1)
-    part = gram(residual, code, n_group, 0)
-    part = part + flip(away, "member", 0)
-    info, first = lax.optimization_barrier((info, first))
+    away = gram(vectors, code, seen, n_group, 1)
+    kept = gram(vectors, code, seen, n_group, 0)
+    parts = [k + flip(x, "member", 0) for k, x in zip(kept, away)]
+    info, first = lax.optimization_barrier((info.reshape(devices, 1, BL), first))
     info = to_owners(info)[:, 0]
-    pa, pb = sum_and_share(part, n_group, n_member)
+    pa, pb = sum_and_share(parts, n_group, n_member)
+    tags = [info[:, c : c + chunk].reshape(-1, 1) for c in range(0, capacity, chunk)]
+    counts = jnp.sum(info[:, capacity : capacity + lists], axis=0).astype(f32)
+    count = lax.dynamic_index_in_dim(counts, core, 0, keepdims=True)
+    scale = 1.0 / jnp.maximum(count, 1.0)
     arrived = [first]
     for later in outgoing[1:]:
-        later, info, pa, pb = lax.optimization_barrier((later, info, pa, pb))
+        later, scale, pa, pb = lax.optimization_barrier((later, scale, pa, pb))
         arrived.append(to_owners(later))
-    tags = [info[:, c : c + chunk].reshape(-1, 1) for c in range(0, capacity, chunk)]
-    counts = jnp.sum(info[:, capacity:], axis=0).astype(f32)
-    count = lax.dynamic_index_in_dim(counts, core, 0, keepdims=True)
-    scale = 1.0 / jnp.maximum(count, 1.0)
     own = chol(pa, pb, scale, width)
     other = flip(own, "member", 0)
-    result, factors = whiten(arrived, tags, own, other, core.reshape(1))
+    result, factors = whiten(arrived, tags, own, other, core.reshape(1), centroids)
     return (result.reshape(devices * capacity, width), factors)
 
 

time: 253 us -> 246 us (0.972)
  starting transfers between devices: 28.5 us -> 43.9 us
  local copies, waits for them, and re-layouts: 24.2 us -> 13.8 us
  waiting for transfers between devices: 98.9 us -> 89.6 us
  matrix products: 6.35 us -> 0 us
  Pallas kernels: 79.5 us -> 85.5 us
    ppermute x16 -> x17, waiting for transfers between devices: 98.9 us -> 79.7 us  [flip(): return lax.ppermute(x, axis, [(i, i ^ 1 << bit) for i in range(size)])]
    ppermute x16 -> x17, starting transfers between devices: 13.6 us -> 27 us  [flip(): return lax.ppermute(x, axis, [(i, i ^ 1 << bit) for i in range(size)])]
    all_to_all x3, waiting for transfers between devices: 0.01 us -> 9.95 us  [to_owners(): lax.all_to_all(x, ('group', 'member'), split_axis=0, concat_axis=0, tiled...]
    scatter x2 -> x0, local copies, waits for them, and re-layouts: 6.92 us -> none  [the longest x1 4.48 us: on_device(): jnp.zeros((devices * capacity, width), f32).at[slot_of].set(residual)]
    slice x3 -> x0, local copies, waits for them, and re-layouts: 6.77 us -> none  [the longest x1 4.85 us: on_device(): first = to_owners(outgoing[0])]
    unnamed x18 -> x26, local copies, waits for them, and re-layouts: 3.24 us -> 9.78 us
    dot_general x2 -> x0, matrix products: 6.35 us -> none  [the longest x1 3.33 us: on_device(): jnp.dot(new_hot, every, precision=lax.Precision.HIGHEST)]
    pallas_call x0 -> x1, Pallas kernels: none -> 6.34 us  [route(): pl.pallas_call(lambda *refs: route_body(sizes, *refs), in_specs=[pl.Block...]
  transfers between devices with their start and end apart: 20 -> 21, of which waited for: 13 -> 11; matrix products, arithmetic and copies ran while one was open for 12% -> 6% of each run, Pallas kernels for 20% -> 23%
where the time goes in v3:
time: 246 us
  waiting for transfers between devices  89.6 us (36%)
  Pallas kernels  85.5 us (35%)
  starting transfers between devices  43.9 us (18%)
  local copies, waits for them, and re-layouts  13.8 us (6%)
  other arithmetic  11 us (4%)
    ppermute x17, waiting for transfers between devices, flip(): return lax.ppermute(x, axis, [(i, i ^ 1 << bit) for i in range(size)])  79.7 us
    pallas_call x1, Pallas kernels, chol(): pl.pallas_call(lambda *refs: chol_body(n, *refs), in_specs=[pl.BlockSpec(...  44.7 us
    ppermute x17, starting transfers between devices, flip(): return lax.ppermute(x, axis, [(i, i ^ 1 << bit) for i in range(size)])  27 us
    pallas_call x1, Pallas kernels, whiten(): pl.pallas_call(lambda *refs: whiten_body(n, chunks, *refs), in_specs=[pl....  22.7 us
    all_to_all x3, starting transfers between devices, to_owners(): lax.all_to_all(x, ('group', 'member'), split_axis=0, concat_axis=0, tiled...  13.9 us
    pallas_call x2, Pallas kernels, gram(): pl.pallas_call(lambda *refs: gram_body(rel, *refs), grid=(n_group,), in_s...  11.8 us
    all_to_all x3, waiting for transfers between devices, to_owners(): lax.all_to_all(x, ('group', 'member'), split_axis=0, concat_axis=0, tiled...  9.95 us
    unnamed x26, local copies, waits for them, and re-layouts  9.78 us
  transfers between devices with their start and end apart: 21, of which 11 were waited for; matrix products, arithmetic and copies ran while one was open for 6% of the time, Pallas kernels for 23%

profile of v3, /device:TPU:0, one launch (start us, length us, event | category | flops | bytes accessed | tf_op | source)
XLA Modules:
  0.0 245.5 jit_solution(9905081685027015759)
XLA Ops:
  0.6 3.1 %collective-permute-start = (f32[2,1024]{1,0:T(2,128)}, f32[2,1024]{1,0:T(2,128)S(1)}, u32[]{:S(2)}, u32[]{:S(2)}) collective-permute-start(f32[2,1024]{1,0:T(2,128)} %refs_1_.3), channel_id=1, source_target_pairs={{0,16},{16,0},{1,17},{17,1},{2,18},{18,2},{3,19},{19,3},{4,20},{20... | collective-permute-start | bytes 24584 | tf_op jit(solution)/shard_map/ppermute | solution.py:482
  3.8 1.6 copy-done
  5.4 0.9 copy-done.1
  6.3 0.7 copy-done.2
  7.0 0.7 copy-done.3
  7.7 0.7 copy-done.4
  8.4 6.3 %route.1 = (f32[512,1024]{1,0:T(8,128)}, f32[512,1024]{1,0:T(8,128)}, f32[512,1024]{1,0:T(8,128)S(1)}, s32[32,128]{1,0:T(8,128)}, s32[8,512]{1,0:T(8,128)S(1)}) custom-call(s32[2]{0:T(128)S(1)} %pad_add_fusion.refs_0_, f32[512,1024]{1,0:T(8,128)S(1)} %copy-done, s32[1,512]{1,0:T(1,128)S(1)} %bitcast.25, s32[1,512]{1,0:T(1,128)S(1)} %bitcast.26, ...), custom_call_target="tpu_custom_call" | custom-call | flops 3221225472 | bytes 4194304 | tf_op jit(solution)/shard_map/route/pallas_call | solution.py:115
  14.9 6.4 %gram.3 = (f32[2,2304,128]{2,1,0:T(8,128)}, f32[2,2304,128]{2,1,0:T(8,128)}) custom-call(f32[512,1024]{1,0:T(8,128)S(1)} %get-tuple-element.23.refs_0_, s32[8,512]{1,0:T(8,128)S(1)} %get-tuple-element.24.refs_1_, f32[8,1024]{1,0:T(8,128)S(1)} %maximum_maximum_fusion.refs_2_), custom_call_target="tpu_custom_call" | custom-call | flops 3221225472 | bytes 6815744 | tf_op jit(solution)/shard_map/gram/pallas_call | solution.py:173
  21.8 1.6 copy-done.6
  23.4 5.4 %gram.2 = (f32[2,2304,128]{2,1,0:T(8,128)S(1)}, f32[2,2304,128]{2,1,0:T(8,128)S(1)}) custom-call(f32[512,1024]{1,0:T(8,128)S(1)} %copy-done.6, s32[8,512]{1,0:T(8,128)S(1)} %get-tuple-element.24.refs_1_, f32[8,1024]{1,0:T(8,128)S(1)} %maximum_maximum_fusion.refs_2_), custom_call_target="tpu_custom_call" | custom-call | flops 3221225472 | bytes 6815744 | tf_op jit(solution)/shard_map/gram/pallas_call | solution.py:173
  28.8 1.9 add.71
  30.8 1.3 copy-done.7
  32.1 1.9 add.84
  34.0 1.2 constant_dynamic-slice_fusion.3
  35.8 2.0 collective-permute-start.10
  37.8 5.0 %all-to-all-start = ((f32[32,16,1024]{2,1,0:T(8,128)}), f32[32,16,1024]{2,1,0:T(8,128)}, u32[]{:S(2)}, u32[]{:S(2)}) async-start(f32[32,16,1024]{2,1,0:T(8,128)} %bitcast.7), calls=%async_computation | async-start | bytes 4194304 | tf_op jit(solution)/shard_map/all_to_all | solution.py:467
  42.9 29.4 %collective-permute-done.2 = f32[1,2,2,2,288,128]{5,4,3,2,1,0:T(8,128)} collective-permute-done((f32[1,2,2,2,288,128]{5,4,3,2,1,0:T(8,128)S(1)}, f32[1,2,2,2,288,128]{5,4,3,2,1,0:T(8,128)}, u32[]{:S(2)}, u32[]{:S(2)}) %collective-permute-start.2) | collective-permute-done | bytes 1179680 | tf_op jit(solution)/shard_map/ppermute | solution.py:430
  72.3 1.5 dynamic-slice_add_fusion.1
  73.9 1.6 collective-permute-start.3
  75.4 2.9 %collective-permute-done.10 = f32[2,1,2,2,288,128]{5,4,3,2,1,0:T(8,128)} collective-permute-done((f32[2,1,2,2,288,128]{5,4,3,2,1,0:T(8,128)}, f32[2,1,2,2,288,128]{5,4,3,2,1,0:T(8,128)}, u32[]{:S(2)}, u32[]{:S(2)}) %collective-permute-start.10) | collective-permute-done | bytes 1179680 | tf_op jit(solution)/shard_map/ppermute | solution.py:430
  78.3 1.5 dynamic-slice_add_fusion
  79.8 2.1 collective-permute-start.11
  81.9 17.3 %collective-permute-done.3 = f32[1,1,2,2,288,128]{5,4,3,2,1,0:T(8,128)} collective-permute-done((f32[1,1,2,2,288,128]{5,4,3,2,1,0:T(8,128)S(1)}, f32[1,1,2,2,288,128]{5,4,3,2,1,0:T(8,128)}, u32[]{:S(2)}, u32[]{:S(2)}) %collective-permute-start.3) | collective-permute-done | bytes 589856 | tf_op jit(solution)/shard_map/ppermute | solution.py:430
  99.2 1.1 dynamic-slice_add_fusion.3
  100.4 1.8 collective-permute-start.4
  102.1 1.1 dynamic-slice_add_fusion.2
  103.7 6.6 %collective-permute-done.4 = f32[1,1,1,2,288,128]{5,4,3,2,1,0:T(8,128)S(1)} collective-permute-done((f32[1,1,1,2,288,128]{5,4,3,2,1,0:T(8,128)S(1)}, f32[1,1,1,2,288,128]{5,4,3,2,1,0:T(8,128)S(1)}, u32[]{:S(2)}, u32[]{:S(2)}) %collective-permute-start.4) | collective-permute-done | bytes 294944 | tf_op jit(solution)/shard_map/ppermute | solution.py:430
  110.4 3.3 %collective-permute-start.5 = (f32[1,1,1,1,288,128]{5,4,3,2,1,0:T(8,128)S(1)}, f32[1,1,1,1,288,128]{5,4,3,2,1,0:T(8,128)S(1)}, u32[]{:S(2)}, u32[]{:S(2)}) collective-permute-start(f32[1,1,1,1,288,128]{5,4,3,2,1,0:T(8,128)S(1)} %constant_dynamic-slice_fusion.4), channel_id=1, source_target_pairs={{0,8},{1,9},{2,10},{3,11},{4,12},{5,13},{6,14},{7,15},{8,0},{9,1},... | collective-permute-start | bytes 442376 | tf_op jit(solution)/shard_map/ppermute | solution.py:430
  113.7 3.8 %collective-permute-done.12 = f32[1,1,1,2,288,128]{5,4,3,2,1,0:T(8,128)S(1)} collective-permute-done((f32[1,1,1,2,288,128]{5,4,3,2,1,0:T(8,128)S(1)}, f32[1,1,1,2,288,128]{5,4,3,2,1,0:T(8,128)S(1)}, u32[]{:S(2)}, u32[]{:S(2)}) %collective-permute-start.12) | collective-permute-done | bytes 294944 | tf_op jit(solution)/shard_map/ppermute | solution.py:430
  117.6 1.4 collective-permute-start.13
  119.0 2.2 collective-permute-start.6
  121.2 6.6 %collective-permute-done.13 = f32[1,1,1,1,288,128]{5,4,3,2,1,0:T(8,128)S(1)} collective-permute-done((f32[1,1,1,1,288,128]{5,4,3,2,1,0:T(8,128)S(1)}, f32[1,1,1,1,288,128]{5,4,3,2,1,0:T(8,128)S(1)}, u32[]{:S(2)}, u32[]{:S(2)}) %collective-permute-start.13) | collective-permute-done | bytes 147488 | tf_op jit(solution)/shard_map/ppermute | solution.py:430
  127.9 2.8 %collective-permute-start.14 = (f32[1,1,1,1,288,128]{5,4,3,2,1,0:T(8,128)S(1)}, f32[1,1,1,1,288,128]{5,4,3,2,1,0:T(8,128)S(1)}, u32[]{:S(2)}, u32[]{:S(2)}) collective-permute-start(f32[1,1,1,1,288,128]{5,4,3,2,1,0:T(8,128)S(1)} %dynamic-slice_add_fusion.6), channel_id=1, source_target_pairs={{0,2},{1,3},{2,0},{3,1},{4,6},{5,7},{6,4},{7,5},{8,10},{9,11},{10,... | collective-permute-start | bytes 442376 | tf_op jit(solution)/shard_map/ppermute | solution.py:430
  130.9 3.5 %collective-permute-start.7 = (f32[1,1,1,2,288,128]{5,4,3,2,1,0:T(8,128)S(1)}, f32[1,1,1,2,288,128]{5,4,3,2,1,0:T(8,128)S(1)}, u32[]{:S(2)}, u32[]{:S(2)}) collective-permute-start(f32[1,1,1,2,288,128]{5,4,3,2,1,0:T(8,128)S(1)} %maximum_select_fusion.5), channel_id=1, source_target_pairs={{0,4},{1,5},{2,6},{3,7},{4,0},{5,1},{6,2},{7,3},{8,12},{9,13},{10,... | collective-permute-start | bytes 884744 | tf_op jit(solution)/shard_map/ppermute | solution.py:430
  134.5 3.0 %collective-permute-start.15 = (f32[1,2,1,1,288,128]{5,4,3,2,1,0:T(8,128)S(1)}, f32[1,2,1,1,288,128]{5,4,3,2,1,0:T(8,128)S(1)}, u32[]{:S(2)}, u32[]{:S(2)}) collective-permute-start(f32[1,2,1,1,288,128]{5,4,3,2,1,0:T(8,128)S(1)} %maximum_select_fusion.7), channel_id=1, source_target_pairs={{0,8},{1,9},{2,10},{3,11},{4,12},{5,13},{6,14},{7,15},{8,0},{9,1},... | collective-permute-start | bytes 884744 | tf_op jit(solution)/shard_map/ppermute | solution.py:430
  137.5 8.1 %collective-permute-done.7 = f32[1,1,1,2,288,128]{5,4,3,2,1,0:T(8,128)S(1)} collective-permute-done((f32[1,1,1,2,288,128]{5,4,3,2,1,0:T(8,128)S(1)}, f32[1,1,1,2,288,128]{5,4,3,2,1,0:T(8,128)S(1)}, u32[]{:S(2)}, u32[]{:S(2)}) %collective-permute-start.7) | collective-permute-done | bytes 294944 | tf_op jit(solution)/shard_map/ppermute | solution.py:430
  145.6 1.6 collective-permute-start.8
  147.3 0.8 collective-permute-done.15
  148.8 4.8 %all-to-all-start.1 = ((s32[32,1,128]{2,1,0:T(1,128)}), s32[32,1,128]{2,1,0:T(1,128)S(1)}, u32[]{:S(2)}, u32[]{:S(2)}) async-start(s32[32,1,128]{2,1,0:T(1,128)} %bitcast.8), calls=%async_computation.1 | async-start | bytes 32768 | tf_op jit(solution)/shard_map/all_to_all | solution.py:467
  153.6 9.9 %all-to-all-done.1 = s32[32,1,128]{2,1,0:T(1,128)S(1)} async-done(((s32[32,1,128]{2,1,0:T(1,128)}), s32[32,1,128]{2,1,0:T(1,128)S(1)}, u32[]{:S(2)}, u32[]{:S(2)}) %all-to-all-start.1) | async-done | bytes 16416 | tf_op jit(solution)/shard_map/all_to_all | solution.py:467
  165.0 1.4 maximum_select_fusion.1
  166.4 4.1 %all-to-all-start.2 = ((f32[32,16,1024]{2,1,0:T(8,128)}), f32[32,16,1024]{2,1,0:T(8,128)}, u32[]{:S(2)}, u32[]{:S(2)}) async-start(f32[32,16,1024]{2,1,0:T(8,128)} %bitcast.5), calls=%async_computation.2 | async-start | bytes 4194304 | tf_op jit(solution)/shard_map/all_to_all | solution.py:467
  170.5 44.7 %chol.1.refs_2_ = f32[6144,128]{1,0:T(8,128)} custom-call(f32[1]{0:T(128)S(6)} %div.3.refs_0_, f32[2304,128]{1,0:T(8,128)S(1)} %bitcast.23, f32[2304,128]{1,0:T(8,128)S(1)} %bitcast.24), custom_call_target="tpu_custom_call" | custom-call | flops 42949672960 | bytes 4718592 | tf_op jit(solution)/shard_map/chol/pallas_call | solution.py:296
  215.4 0.9 reshape.641.refs_7_
  216.3 0.9 reshape.640.refs_6_
  217.1 3.8 %collective-permute-done.17.refs_3_ = f32[6144,128]{1,0:T(8,128)S(1)} collective-permute-done((f32[6144,128]{1,0:T(8,128)}, f32[6144,128]{1,0:T(8,128)S(1)}, u32[]{:S(2)}, u32[]{:S(2)}) %collective-permute-start.17) | collective-permute-done | bytes 3145760 | tf_op jit(solution)/shard_map/ppermute | solution.py:430
  221.0 1.7 copy-done.12
  222.7 22.7 %whiten.1 = (f32[32,32,1024]{2,1,0:T(8,128)}, f32[2,1024,1024]{2,1,0:T(8,128)}) custom-call(s32[1]{0:T(128)} %bitcast.refs_0_, f32[2,1024]{1,0:T(2,128)} %refs_1_.3, f32[6144,128]{1,0:T(8,128)} %chol.1.refs_2_, f32[6144,128]{1,0:T(8,128)} %copy-done.12, f32[32,16,1024]{2,1,0:T(8,128)} %all-to-all-done.refs_4_, f32[32,16,1024]{2,1,0:T(8,128)} %all-to-all-done.2.refs_5_, ...), custom_call_target="tpu_custom_call" | custom-call | flops 12884901888 | bytes 16777216 | tf_op jit(solution)/shard_map/whiten/pallas_call | solution.py:403
  (61 shorter events, 4.2 us)
Async XLA Ops:
  0.6 14.2 %collective-permute-start = (f32[2,1024]{1,0:T(2,128)}, f32[2,1024]{1,0:T(2,128)S(1)}, u32[]{:S(2)}, u32[]{:S(2)}) collective-permute-start(f32[2,1024]{1,0:T(2,128)} %refs_1_.3), channel_id=1, source_target_pairs={{0,16},{16,0},{1,17},{17,1},{2,18},{18,2},{3,19},{19,3},{4,20},{20... | collective-permute-start | bytes 24584 | tf_op jit(solution)/shard_map/ppermute | solution.py:482
  3.8 1.6 copy-start
  5.4 0.9 copy-start.1
  6.3 0.7 copy-start.2
  7.0 0.7 copy-start.3
  7.7 0.7 copy-start.4
  8.4 6.4 %copy-start.11 = (f32[2,1024]{1,0:T(2,128)S(1)}, f32[2,1024]{1,0:T(2,128)}, u32[]{:S(2)}) copy-start(f32[2,1024]{1,0:T(2,128)} %refs_1_.3) | copy-start | bytes 24580
  14.7 6.6 %copy-start.5 = (f32[512,1024]{1,0:T(8,128)}, f32[512,1024]{1,0:T(8,128)S(1)}, u32[]{:S(2)}) copy-start(f32[512,1024]{1,0:T(8,128)S(1)} %get-tuple-element.23.refs_0_) | copy-start | bytes 6291460
  21.3 7.5 %collective-permute-start.1 = (f32[2,2304,128]{2,1,0:T(8,128)}, f32[2,2304,128]{2,1,0:T(8,128)}, u32[]{:S(2)}, u32[]{:S(2)}) collective-permute-start(f32[2,2304,128]{2,1,0:T(8,128)} %get-tuple-element.26), channel_id=1, source_target_pairs={{0,1},{1,0},{2,3},{3,2},{4,5},{5,4},{6,7},{7,6},{8,9},{9,8},{10,11... | collective-permute-start | bytes 7077896 | tf_op jit(solution)/shard_map/ppermute | solution.py:430
  21.3 10.8 %collective-permute-start.9 = (f32[2,2304,128]{2,1,0:T(8,128)}, f32[2,2304,128]{2,1,0:T(8,128)}, u32[]{:S(2)}, u32[]{:S(2)}) collective-permute-start(f32[2,2304,128]{2,1,0:T(8,128)} %get-tuple-element.28), channel_id=1, source_target_pairs={{0,1},{1,0},{2,3},{3,2},{4,5},{5,4},{6,7},{7,6},{8,9},{9,8},{10,11... | collective-permute-start | bytes 7077896 | tf_op jit(solution)/shard_map/ppermute | solution.py:430
  21.8 1.6 copy-start.6
  30.7 1.4 copy-start.7
  32.1 40.2 %collective-permute-start.2 = (f32[1,2,2,2,288,128]{5,4,3,2,1,0:T(8,128)S(1)}, f32[1,2,2,2,288,128]{5,4,3,2,1,0:T(8,128)}, u32[]{:S(2)}, u32[]{:S(2)}) collective-permute-start(f32[1,2,2,2,288,128]{5,4,3,2,1,0:T(8,128)S(1)} %constant_dynamic-slice_fusion.7), channel_id=1, source_target_pairs={{0,16},{16,0},{1,17},{17,1},{2,18},{18,2},{3,19},{19,3},{4,20},{20... | collective-permute-start | bytes 3538952 | tf_op jit(solution)/shard_map/ppermute | solution.py:430
  34.0 1.8 copy-start.9
  35.8 42.5 %collective-permute-start.10 = (f32[2,1,2,2,288,128]{5,4,3,2,1,0:T(8,128)}, f32[2,1,2,2,288,128]{5,4,3,2,1,0:T(8,128)}, u32[]{:S(2)}, u32[]{:S(2)}) collective-permute-start(f32[2,1,2,2,288,128]{5,4,3,2,1,0:T(8,128)} %constant_dynamic-slice_fusion.3), channel_id=1, source_target_pairs={{0,2},{1,3},{2,0},{3,1},{4,6},{5,7},{6,4},{7,5},{8,10},{9,11},{10,... | collective-permute-start | bytes 3538952 | tf_op jit(solution)/shard_map/ppermute | solution.py:430
  37.8 34.5 %copy-start.8 = (f32[2,2304,128]{2,1,0:T(8,128)S(1)}, f32[2,2304,128]{2,1,0:T(8,128)}, u32[]{:S(2)}) copy-start(f32[2,2304,128]{2,1,0:T(8,128)} %copy-done.7) | copy-start | bytes 7077892
  37.8 111.0 %all-to-all-start = ((f32[32,16,1024]{2,1,0:T(8,128)}), f32[32,16,1024]{2,1,0:T(8,128)}, u32[]{:S(2)}, u32[]{:S(2)}) async-start(f32[32,16,1024]{2,1,0:T(8,128)} %bitcast.7), calls=%async_computation | async-start | bytes 4194304 | tf_op jit(solution)/shard_map/all_to_all | solution.py:467
  72.3 6.0 %copy-start.10 = (f32[2,2304,128]{2,1,0:T(8,128)S(1)}, f32[2,2304,128]{2,1,0:T(8,128)}, u32[]{:S(2)}) copy-start(f32[2,2304,128]{2,1,0:T(8,128)} %copy-done.9) | copy-start | bytes 7077892
  73.9 25.3 %collective-permute-start.3 = (f32[1,1,2,2,288,128]{5,4,3,2,1,0:T(8,128)S(1)}, f32[1,1,2,2,288,128]{5,4,3,2,1,0:T(8,128)}, u32[]{:S(2)}, u32[]{:S(2)}) collective-permute-start(f32[1,1,2,2,288,128]{5,4,3,2,1,0:T(8,128)S(1)} %constant_dynamic-slice_fusion.6), channel_id=1, source_target_pairs={{0,2},{1,3},{2,0},{3,1},{4,6},{5,7},{6,4},{7,5},{8,10},{9,11},{10,... | collective-permute-start | bytes 1769480 | tf_op jit(solution)/shard_map/ppermute | solution.py:430
  79.8 22.3 %collective-permute-start.11 = (f32[1,1,2,2,288,128]{5,4,3,2,1,0:T(8,128)S(1)}, f32[1,1,2,2,288,128]{5,4,3,2,1,0:T(8,128)}, u32[]{:S(2)}, u32[]{:S(2)}) collective-permute-start(f32[1,1,2,2,288,128]{5,4,3,2,1,0:T(8,128)S(1)} %constant_dynamic-slice_fusion.2), channel_id=1, source_target_pairs={{0,16},{16,0},{1,17},{17,1},{2,18},{18,2},{3,19},{19,3},{4,20},{20... | collective-permute-start | bytes 1769480 | tf_op jit(solution)/shard_map/ppermute | solution.py:430
  100.4 9.9 %collective-permute-start.4 = (f32[1,1,1,2,288,128]{5,4,3,2,1,0:T(8,128)S(1)}, f32[1,1,1,2,288,128]{5,4,3,2,1,0:T(8,128)S(1)}, u32[]{:S(2)}, u32[]{:S(2)}) collective-permute-start(f32[1,1,1,2,288,128]{5,4,3,2,1,0:T(8,128)S(1)} %constant_dynamic-slice_fusion.5), channel_id=1, source_target_pairs={{0,4},{1,5},{2,6},{3,7},{4,0},{5,1},{6,2},{7,3},{8,12},{9,13},{10,... | collective-permute-start | bytes 884744 | tf_op jit(solution)/shard_map/ppermute | solution.py:430
  103.3 14.2 %collective-permute-start.12 = (f32[1,1,1,2,288,128]{5,4,3,2,1,0:T(8,128)S(1)}, f32[1,1,1,2,288,128]{5,4,3,2,1,0:T(8,128)S(1)}, u32[]{:S(2)}, u32[]{:S(2)}) collective-permute-start(f32[1,1,1,2,288,128]{5,4,3,2,1,0:T(8,128)S(1)} %constant_dynamic-slice_fusion.1), channel_id=1, source_target_pairs={{0,4},{1,5},{2,6},{3,7},{4,0},{5,1},{6,2},{7,3},{8,12},{9,13},{10,... | collective-permute-start | bytes 884744 | tf_op jit(solution)/shard_map/ppermute | solution.py:430
  110.4 8.6 %collective-permute-start.5 = (f32[1,1,1,1,288,128]{5,4,3,2,1,0:T(8,128)S(1)}, f32[1,1,1,1,288,128]{5,4,3,2,1,0:T(8,128)S(1)}, u32[]{:S(2)}, u32[]{:S(2)}) collective-permute-start(f32[1,1,1,1,288,128]{5,4,3,2,1,0:T(8,128)S(1)} %constant_dynamic-slice_fusion.4), channel_id=1, source_target_pairs={{0,8},{1,9},{2,10},{3,11},{4,12},{5,13},{6,14},{7,15},{8,0},{9,1},... | collective-permute-start | bytes 442376 | tf_op jit(solution)/shard_map/ppermute | solution.py:430
  117.6 10.3 %collective-permute-start.13 = (f32[1,1,1,1,288,128]{5,4,3,2,1,0:T(8,128)S(1)}, f32[1,1,1,1,288,128]{5,4,3,2,1,0:T(8,128)S(1)}, u32[]{:S(2)}, u32[]{:S(2)}) collective-permute-start(f32[1,1,1,1,288,128]{5,4,3,2,1,0:T(8,128)S(1)} %constant_dynamic-slice_fusion), channel_id=1, source_target_pairs={{0,8},{1,9},{2,10},{3,11},{4,12},{5,13},{6,14},{7,15},{8,0},{9,1},... | collective-permute-start | bytes 442376 | tf_op jit(solution)/shard_map/ppermute | solution.py:430
  119.0 11.9 %collective-permute-start.6 = (f32[1,1,1,1,288,128]{5,4,3,2,1,0:T(8,128)S(1)}, f32[1,1,1,1,288,128]{5,4,3,2,1,0:T(8,128)S(1)}, u32[]{:S(2)}, u32[]{:S(2)}) collective-permute-start(f32[1,1,1,1,288,128]{5,4,3,2,1,0:T(8,128)S(1)} %dynamic-slice_add_fusion.7), channel_id=1, source_target_pairs={{0,8},{1,9},{2,10},{3,11},{4,12},{5,13},{6,14},{7,15},{8,0},{9,1},... | collective-permute-start | bytes 442376 | tf_op jit(solution)/shard_map/ppermute | solution.py:430
  127.9 6.6 %collective-permute-start.14 = (f32[1,1,1,1,288,128]{5,4,3,2,1,0:T(8,128)S(1)}, f32[1,1,1,1,288,128]{5,4,3,2,1,0:T(8,128)S(1)}, u32[]{:S(2)}, u32[]{:S(2)}) collective-permute-start(f32[1,1,1,1,288,128]{5,4,3,2,1,0:T(8,128)S(1)} %dynamic-slice_add_fusion.6), channel_id=1, source_target_pairs={{0,2},{1,3},{2,0},{3,1},{4,6},{5,7},{6,4},{7,5},{8,10},{9,11},{10,... | collective-permute-start | bytes 442376 | tf_op jit(solution)/shard_map/ppermute | solution.py:430
  130.9 14.6 %collective-permute-start.7 = (f32[1,1,1,2,288,128]{5,4,3,2,1,0:T(8,128)S(1)}, f32[1,1,1,2,288,128]{5,4,3,2,1,0:T(8,128)S(1)}, u32[]{:S(2)}, u32[]{:S(2)}) collective-permute-start(f32[1,1,1,2,288,128]{5,4,3,2,1,0:T(8,128)S(1)} %maximum_select_fusion.5), channel_id=1, source_target_pairs={{0,4},{1,5},{2,6},{3,7},{4,0},{5,1},{6,2},{7,3},{8,12},{9,13},{10,... | collective-permute-start | bytes 884744 | tf_op jit(solution)/shard_map/ppermute | solution.py:430
  134.5 13.7 %collective-permute-start.15 = (f32[1,2,1,1,288,128]{5,4,3,2,1,0:T(8,128)S(1)}, f32[1,2,1,1,288,128]{5,4,3,2,1,0:T(8,128)S(1)}, u32[]{:S(2)}, u32[]{:S(2)}) collective-permute-start(f32[1,2,1,1,288,128]{5,4,3,2,1,0:T(8,128)S(1)} %maximum_select_fusion.7), channel_id=1, source_target_pairs={{0,8},{1,9},{2,10},{3,11},{4,12},{5,13},{6,14},{7,15},{8,0},{9,1},... | collective-permute-start | bytes 884744 | tf_op jit(solution)/shard_map/ppermute | solution.py:430
  145.6 19.3 %collective-permute-start.8 = (f32[1,1,2,2,288,128]{5,4,3,2,1,0:T(8,128)S(1)}, f32[1,1,2,2,288,128]{5,4,3,2,1,0:T(8,128)S(1)}, u32[]{:S(2)}, u32[]{:S(2)}) collective-permute-start(f32[1,1,2,2,288,128]{5,4,3,2,1,0:T(8,128)S(1)} %maximum_select_fusion.2), channel_id=1, source_target_pairs={{0,2},{1,3},{2,0},{3,1},{4,6},{5,7},{6,4},{7,5},{8,10},{9,11},{10,... | collective-permute-start | bytes 1769480 | tf_op jit(solution)/shard_map/ppermute | solution.py:430
  148.2 16.8 %collective-permute-start.16 = (f32[1,2,1,2,288,128]{5,4,3,2,1,0:T(8,128)S(1)}, f32[1,2,1,2,288,128]{5,4,3,2,1,0:T(8,128)}, u32[]{:S(2)}, u32[]{:S(2)}) collective-permute-start(f32[1,2,1,2,288,128]{5,4,3,2,1,0:T(8,128)S(1)} %maximum_select_fusion.3), channel_id=1, source_target_pairs={{0,4},{1,5},{2,6},{3,7},{4,0},{5,1},{6,2},{7,3},{8,12},{9,13},{10,... | collective-permute-start | bytes 1769480 | tf_op jit(solution)/shard_map/ppermute | solution.py:430
  148.8 14.7 %all-to-all-start.1 = ((s32[32,1,128]{2,1,0:T(1,128)}), s32[32,1,128]{2,1,0:T(1,128)S(1)}, u32[]{:S(2)}, u32[]{:S(2)}) async-start(s32[32,1,128]{2,1,0:T(1,128)} %bitcast.8), calls=%async_computation.1 | async-start | bytes 32768 | tf_op jit(solution)/shard_map/all_to_all | solution.py:467
  166.4 54.6 %all-to-all-start.2 = ((f32[32,16,1024]{2,1,0:T(8,128)}), f32[32,16,1024]{2,1,0:T(8,128)}, u32[]{:S(2)}, u32[]{:S(2)}) async-start(f32[32,16,1024]{2,1,0:T(8,128)} %bitcast.5), calls=%async_computation.2 | async-start | bytes 4194304 | tf_op jit(solution)/shard_map/all_to_all | solution.py:467
  215.1 5.9 %collective-permute-start.17 = (f32[6144,128]{1,0:T(8,128)}, f32[6144,128]{1,0:T(8,128)S(1)}, u32[]{:S(2)}, u32[]{:S(2)}) collective-permute-start(f32[6144,128]{1,0:T(8,128)} %chol.1.refs_2_), channel_id=1, source_target_pairs={{0,1},{1,0},{2,3},{3,2},{4,5},{5,4},{6,7},{7,6},{8,9},{9,8},{10,11... | collective-permute-start | bytes 9437192 | tf_op jit(solution)/shard_map/ppermute | solution.py:430
  221.0 1.7 copy-start.12

commit v4 on v3

--- a/solution.py
+++ b/solution.py
@@ -11,6 +11,7 @@
 bf16 = jnp.bfloat16
 BL = 128
 SUB = 8
+NEST = 8
 
 
 def split(x):
@@ -53,13 +54,19 @@
     )
 
 
-def route_body(sizes, ids_ref, rows_ref, old_ref, dest_ref, local_ref, table_ref, *refs):
+def route_body(sizes, ids_ref, rows_hbm, old_ref, dest_ref, local_ref, table_hbm, *refs):
     n_group, n_member, capacity, chunk = sizes
     devices = n_group * n_member
     chunks = capacity // chunk
     out_refs = refs[:chunks]
-    vec_ref, info_ref, code_ref, o_ref, sem = refs[chunks:]
+    vec_hbm, info_ref, code_ref, rows_ref, table_ref, vec_ref, o_ref, sem = refs[chunks:]
     count, _ = rows_ref.shape
+    loads = [
+        pltpu.make_async_copy(rows_hbm, rows_ref, sem.at[0]),
+        pltpu.make_async_copy(table_hbm, table_ref, sem.at[1]),
+    ]
+    for copy in loads:
+        copy.start()
     group, core = ids_ref[0], ids_ref[1]
     dest = dest_ref[...]
     local = local_ref[...]
@@ -87,6 +94,8 @@
     )
     info_ref[...] = dot_nt(left.astype(bf16), right.astype(bf16)).astype(jnp.int32)
 
+    for copy in loads:
+        copy.wait()
     vec = rows_ref[...] + table_rows(old_ref[...], table_ref[...])
     vec_ref[...] = vec
     hi, mid, lo = split3(vec)
@@ -98,10 +107,12 @@
             o_ref[base : base + 2 * BL, :] = dot_nn(pick, hi) + (dot_nn(pick, mid) + dot_nn(pick, lo))
             copies.append(
                 pltpu.make_async_copy(
-                    o_ref.at[pl.ds(base, 2 * BL), :], out_refs[q].at[pl.ds(r, 2 * BL), :], sem.at[base // (2 * BL)]
+                    o_ref.at[pl.ds(base, 2 * BL), :], out_refs[q].at[pl.ds(r, 2 * BL), :], sem.at[3 + base // (2 * BL)]
                 )
             )
             copies[-1].start()
+    copies.append(pltpu.make_async_copy(vec_ref, vec_hbm, sem.at[2]))
+    copies[-1].start()
     for copy in copies:
         copy.wait()
 
@@ -112,10 +123,11 @@
     count, n = rows.shape
     chunks = capacity // chunk
     vmem = pl.BlockSpec(memory_space=pltpu.VMEM)
+    hbm = pl.BlockSpec(memory_space=pltpu.HBM)
     return pl.pallas_call(
         lambda *refs: route_body(sizes, *refs),
-        in_specs=[pl.BlockSpec(memory_space=pltpu.SMEM)] + [vmem] * 5,
-        out_specs=[pl.BlockSpec(memory_space=pl.ANY)] * chunks + [vmem] * 3,
+        in_specs=[pl.BlockSpec(memory_space=pltpu.SMEM), hbm, vmem, vmem, vmem, hbm],
+        out_specs=[hbm] * (chunks + 1) + [vmem] * 2,
         out_shape=[jax.ShapeDtypeStruct((devices * chunk, n), f32)] * chunks
         + [
             jax.ShapeDtypeStruct((count, n), f32),
@@ -123,10 +135,12 @@
             jax.ShapeDtypeStruct((SUB, count), jnp.int32),
         ],
         scratch_shapes=[
+            pltpu.VMEM((count, n), f32),
+            pltpu.VMEM(table.shape, f32),
+            pltpu.VMEM((count, n), f32),
             pltpu.VMEM((devices * capacity, n), f32),
-            pltpu.SemaphoreType.DMA((devices * capacity // (2 * BL),)),
-        ],
-        compiler_params=pltpu.CompilerParams(vmem_limit_bytes=40 << 20),
+            pltpu.SemaphoreType.DMA((3 + devices * capacity // (2 * BL),)),
+        ],
         cost_estimate=pl.CostEstimate(
             flops=6 * devices * capacity * count * n, bytes_accessed=4 * devices * capacity * n, transcendentals=0
         ),
@@ -134,9 +148,9 @@
     )(ids, rows, old, dest, local, table)
 
 
-def gram_body(rel, vec_ref, code_ref, table_ref, a_ref, b_ref, th_ref, tl_ref, h_ref, l_ref):
+def gram_body(rel, vec_ref, code_ref, table_ref, a_ref, b_ref, t_ref, h_ref):
     g = pl.program_id(0)
-    _, n = vec_ref.shape
+    rows, n = vec_ref.shape
     order = blocks(n)
     half = len(order) // 2
 
@@ -144,21 +158,18 @@
     def _():
         x = vec_ref[...] - table_rows(code_ref[1:2, :], table_ref[...])
         hi, lo = split(x)
-        h_ref[...] = hi
-        l_ref[...] = lo
+        for at, y in enumerate((hi, lo, hi)):
+            h_ref[at * rows : (at + 1) * rows, :] = y
         for j in range(0, n, BL):
             hi, lo = split(x[:, j : j + BL].T)
-            th_ref[j : j + BL, :] = hi
-            tl_ref[j : j + BL, :] = lo
+            for at, y in enumerate((hi, hi, lo)):
+                t_ref[j : j + BL, at * rows : (at + 1) * rows] = y
 
     mask = (code_ref[0:1, :] == 2 * g + rel).astype(f32).astype(bf16)
+    mask = jnp.concatenate([mask] * 3, axis=1)
     place = {b: p for p, b in enumerate(order)}
     for j in range(0, n, 2 * BL):
-        mh = h_ref[:, j : j + 2 * BL]
-        ml = l_ref[:, j : j + 2 * BL]
-        th = th_ref[j:n, :] * mask
-        tl = tl_ref[j:n, :] * mask
-        prod = dot_nn(th, mh) + (dot_nn(th, ml) + dot_nn(tl, mh))
+        prod = dot_nn(t_ref[j:n, :] * mask, h_ref[:, j : j + 2 * BL])
         for i in range(j, n, BL):
             for c in (j, j + BL):
                 if i >= c:
@@ -181,12 +192,9 @@
         out_specs=[pl.BlockSpec((1, size, BL), lambda g: (g, 0, 0))] * 2,
         out_shape=[jax.ShapeDtypeStruct((n_group, size, BL), f32)] * 2,
         scratch_shapes=[
-            pltpu.VMEM((n, rows), bf16),
-            pltpu.VMEM((n, rows), bf16),
-            pltpu.VMEM((rows, n), bf16),
-            pltpu.VMEM((rows, n), bf16),
-        ],
-        compiler_params=pltpu.CompilerParams(vmem_limit_bytes=40 << 20),
+            pltpu.VMEM((n, 3 * rows), bf16),
+            pltpu.VMEM((3 * rows, n), bf16),
+        ],
         cost_estimate=pl.CostEstimate(
             flops=3 * n_group * rows * n * n, bytes_accessed=4 * (rows * n + 2 * n_group * size * BL), transcendentals=0
         ),
@@ -194,15 +202,21 @@
     )(vec, code, table)
 
 
-def diag_group(b, tt, s):
+def diag_group(b, c, tt, s):
     lane = lax.broadcasted_iota(jnp.int32, (SUB, BL), 1)
     sub = lax.broadcasted_iota(jnp.int32, (SUB, BL), 0)
     base = SUB * s
+
+    def columns(x):
+        return [jnp.broadcast_to(x[:, base + u : base + u + 1], (SUB, BL)) for u in range(SUB)]
+
+    for u, x in enumerate(columns(b[base : base + SUB, :])):
+        c[SUB * u : SUB * u + SUB, :] = x
     rows = [jnp.broadcast_to(b[base + t : base + t + 1, :], (SUB, BL)) for t in range(SUB)]
     schur = {}
     for i in range(SUB):
         for u in range(i + 1):
-            schur[i, u] = jnp.broadcast_to(rows[i][:, base + u : base + u + 1], (SUB, BL))
+            schur[i, u] = jnp.broadcast_to(c[SUB * u + i : SUB * u + i + 1, :], (SUB, BL))
     panel = (lane >= base) & (lane < base + SUB)
     fwd = [jnp.where(panel, jnp.where(lane == base + t, 1.0, 0.0), rows[t]) for t in range(SUB)]
     pivot, inv, mult = [], [], {}
@@ -222,21 +236,46 @@
         for i in range(SUB - 1, t, -1):
             w = w - mult[i, t] * back[i]
         back[t] = w
-    for g in range(s + 1, BL // SUB):
+    first = s - s % NEST
+    for g in [*range(s + 1, first + NEST), *range(first, s)]:
         x = b[SUB * g : SUB * g + SUB, :]
         even, odd = 0.0, 0.0
+        col = columns(x)
         for u in range(0, SUB, 2):
-            even = even + jnp.broadcast_to(x[:, base + u : base + u + 1], (SUB, BL)) * back[u]
-            odd = odd + jnp.broadcast_to(x[:, base + u + 1 : base + u + 2], (SUB, BL)) * back[u + 1]
+            even = even + col[u] * back[u]
+            odd = odd + col[u + 1] * back[u + 1]
         b[SUB * g : SUB * g + SUB, :] = jnp.where(panel, 0.0, x) - (even + odd)
     out = jnp.zeros((SUB, BL), f32)
+    full = jnp.zeros((SUB, BL), f32)
     for t in range(SUB):
         row = jnp.where(lane <= base + t, fwd[t] * lax.rsqrt(pivot[t]), 0.0)
         out = jnp.where(sub == t, row, out)
+        full = jnp.where(sub == t, back[t], full)
+    b[base : base + SUB, :] = full
     tt[base : base + SUB, :] = out
 
 
-def chol_body(n, scale_ref, pa_ref, pb_ref, out_ref, w_ref, b_ref, t_ref, h1_ref, h2_ref):
+def diag_block(b, c, tt):
+    wide = SUB * NEST
+    lane = lax.broadcasted_iota(jnp.int32, (BL, BL), 1)
+    for first in range(0, BL // SUB, NEST):
+        for s in range(first, first + NEST):
+            diag_group(b, c.at[s % 4], tt, s)
+        low, high = SUB * first, SUB * first + wide
+        if high < BL:
+            w = b[low:high, :]
+            pad = [jnp.zeros((low, BL), f32)] * (low > 0) + [w] + [jnp.zeros((BL - high, BL), f32)]
+            wh, wl = split(jnp.concatenate(pad, axis=0))
+            x = b[high:BL, :]
+            xh, xl = split(x)
+            inside = (lane[high:BL] >= low) & (lane[high:BL] < high)
+            prod = dot_nn(
+                jnp.concatenate([xh, xh, xl, xl], axis=1), jnp.concatenate([wh, wl, wh, wl], axis=0)
+            )
+            b[high:BL, :] = jnp.where(inside, 0.0, x) - prod
+
+
+def chol_body(n, scale_ref, pa_ref, pb_ref, out_ref, w_ref, b_ref, c_ref, t_ref, h1_ref, h2_ref):
     nb = n // BL
     order = blocks(n)
     place = {b: p for p, b in enumerate(order)}
@@ -255,8 +294,7 @@
     def _(k):
         o = pl.multiple_of(k * BL, BL)
         b_ref[...] = w_ref[pl.ds(o, BL), pl.ds(o, BL)]
-        for s in range(BL // SUB):
-            diag_group(b_ref, t_ref, s)
+        diag_block(b_ref, c_ref, t_ref)
         out_ref[pl.ds(pl.multiple_of((len(order) + k) * BL, BL), BL), :] = t_ref[...]
         for kk in range(nb):
 
@@ -305,124 +343,152 @@
         scratch_shapes=[
             pltpu.VMEM((n, n), f32),
             pltpu.VMEM((BL, BL), f32),
+            pltpu.VMEM((4, SUB * SUB, BL), f32),
             pltpu.VMEM((BL, BL), f32),
             pltpu.VMEM((n, 4 * BL), bf16),
             pltpu.VMEM((n, 4 * BL), bf16),
         ],
-        compiler_params=pltpu.CompilerParams(vmem_limit_bytes=40 << 20),
         cost_estimate=pl.CostEstimate(flops=40 * n * n * n, bytes_accessed=8 * size * BL, transcendentals=0),
         name="chol",
     )(scale, pa, pb)
 
 
 def whiten_body(n, chunks, *refs):
-    mine_ref, cent_ref, own_ref, other_ref = refs[:4]
-    res_refs = refs[4 : 4 + chunks]
-    tag_refs = refs[4 + chunks : 4 + 2 * chunks]
-    out_ref, fac_ref, f_ref, o_ref, lh_ref, ll_ref, th_ref, tl_ref, wh_ref, wl_ref, sem = refs[4 + 2 * chunks :]
+    mine_ref, cent_ref, info_ref, own_hbm, other_hbm = refs[:5]
+    res_hbm = refs[5 : 5 + chunks]
+    out_ref, fac_ref, p_ref, r_ref, z_ref, o_ref, l_ref, t_ref, w_ref, sem = refs[5 + chunks :]
     order = blocks(n)
+    place = {b: p for p, b in enumerate(order)}
     nb = n // BL
     wide = 2 * BL
     mine = mine_ref[0]
-    sources, part, _ = res_refs[0].shape
+    _, sources, part, _ = r_ref.shape
     rows = sources * part
-    copies = []
-
-    for slot, (src, dst) in enumerate(((own_ref, mine), (other_ref, 1 - mine))):
-        f_ref[slot] = jnp.zeros((n, n), f32)
+    used = [0]
+
+    def copy(src, dst):
+        one = pltpu.make_async_copy(src, dst, sem.at[used[0]])
+        used[0] += 1
+        one.start()
+        return one
+
+    packs = [copy(own_hbm, p_ref.at[0])]
+    moved = [copy(res_hbm[q], r_ref.at[q]) for q in range(chunks)]
+    packs.append(copy(other_hbm, p_ref.at[1]))
+    z_ref[...] = jnp.zeros_like(z_ref)
+
+    low = part.bit_length() - 1
+    row = lax.broadcasted_iota(jnp.int32, (rows, sources), 0)
+    pick = ((row >> low) == lax.broadcasted_iota(jnp.int32, (rows, sources), 1)).astype(f32).astype(bf16)
+    spread = dot_nn(pick, info_ref[...].astype(f32).astype(bf16))
+    k = lax.broadcasted_iota(jnp.int32, (rows, BL), 0) & (part - 1)
+    lane = lax.broadcasted_iota(jnp.int32, (rows, BL), 1)
+    tags = [jnp.sum(jnp.where(lane == k + q * part, spread, 0.0), axis=1, keepdims=True) for q in range(chunks)]
+
+    done = []
+    for slot, dst in enumerate((mine, 1 - mine)):
+        packs[slot].wait()
+        for j in range(nb):
+            p = place[(j, j)] * BL
+            done.append(
+                copy(
+                    p_ref.at[slot, pl.ds(p, n - j * BL), :],
+                    fac_ref.at[dst, pl.ds(j * BL, n - j * BL), pl.ds(j * BL, BL)],
+                )
+            )
+            if j + 1 < nb:
+                rest = n - (j + 1) * BL
+                done.append(
+                    copy(
+                        z_ref.at[:, pl.ds(0, rest)],
+                        fac_ref.at[dst, pl.ds(j * BL, BL), pl.ds((j + 1) * BL, rest)],
+                    )
+                )
         for p, (i, j) in enumerate(order):
-            x = src[p * BL : (p + 1) * BL, :]
-            f_ref[slot, i * BL : (i + 1) * BL, j * BL : (j + 1) * BL] = x
-            hi, lo = split(x)
-            lh_ref[slot, i * BL : (i + 1) * BL, j * BL : (j + 1) * BL] = hi
-            ll_ref[slot, i * BL : (i + 1) * BL, j * BL : (j + 1) * BL] = lo
-        copies.append(pltpu.make_async_copy(f_ref.at[slot], fac_ref.at[dst], sem.at[slot]))
-        copies[-1].start()
+            if i // 2 == j // 2:
+                continue
+            hi, lo = split(p_ref[slot, p * BL : (p + 1) * BL, :])
+            c = (j // 2) * 3 * wide + (j % 2) * BL
+            for at, x in enumerate((hi, hi, lo)):
+                l_ref[slot, i * BL : (i + 1) * BL, c + at * wide : c + at * wide + BL] = x
         for k in range(nb):
             p = (len(order) + k) * BL
             c = (k % 2) * BL
-            hi, lo = split(src[p : p + BL, :])
-            th_ref[slot, k * BL : (k + 1) * BL, c : c + BL] = hi
-            tl_ref[slot, k * BL : (k + 1) * BL, c : c + BL] = lo
+            hi, lo = split(p_ref[slot, p : p + BL, :])
             if k % 2:
                 p = (len(order) + nb + k // 2) * BL
-                hi, lo = split(src[p : p + BL, :])
+                hi2, lo2 = split(p_ref[slot, p : p + BL, :])
             else:
-                hi = lo = jnp.zeros((BL, BL), bf16)
-            th_ref[slot, k * BL : (k + 1) * BL, BL - c : wide - c] = hi
-            tl_ref[slot, k * BL : (k + 1) * BL, BL - c : wide - c] = lo
-
+                hi2 = lo2 = jnp.zeros((BL, BL), bf16)
+            for at, (x, y) in enumerate(((hi, hi2), (hi, hi2), (lo, lo2))):
+                t_ref[slot, k * BL : (k + 1) * BL, at * wide + c : at * wide + c + BL] = x
+                t_ref[slot, k * BL : (k + 1) * BL, at * wide + BL - c : at * wide + wide - c] = y
+
+    for one in moved:
+        one.wait()
     for c in range(0, n, wide):
         for slot in range(2):
             which = mine if slot == 0 else 1 - mine
             prod = None
             if c:
-                lh = lh_ref[slot, c : c + wide, :c]
-                ll = ll_ref[slot, c : c + wide, :c]
-                wh = wh_ref[slot, :, :c]
-                wl = wl_ref[slot, :, :c]
-                prod = dot_nt(wh, lh) + (dot_nt(wh, ll) + dot_nt(wl, lh))
+                prod = dot_nt(w_ref[slot, :, : 3 * c], l_ref[slot, c : c + wide, : 3 * c])
             accs = []
             for q in range(chunks):
-                x = res_refs[q][:, :, c : c + wide].reshape(rows, wide)
-                x = jnp.where(tag_refs[q][...] == which + 1, x - cent_ref[pl.ds(which, 1), c : c + wide], 0.0)
+                x = r_ref[q, :, :, c : c + wide].reshape(rows, wide)
+                x = jnp.where(tags[q] == (which + 1).astype(f32), x - cent_ref[pl.ds(which, 1), c : c + wide], 0.0)
                 if prod is not None:
                     x = x - prod[q * rows : (q + 1) * rows]
                 accs.append(x)
             ah, al = split(jnp.concatenate(accs, axis=0) if chunks > 1 else accs[0])
-            th = th_ref[slot, c : c + wide, :]
-            tl = tl_ref[slot, c : c + wide, :]
-            x = dot_nt(ah, th) + (dot_nt(ah, tl) + dot_nt(al, th))
-            hi, lo = split(x)
-            wh_ref[slot, :, c : c + wide] = hi
-            wl_ref[slot, :, c : c + wide] = lo
+            x = dot_nt(jnp.concatenate([ah, al, ah], axis=1), t_ref[slot, c : c + wide, :])
+            if c + wide < n:
+                hi, lo = split(x)
+                for at, y in enumerate((hi, lo, hi)):
+                    w_ref[slot, :, 3 * c + at * wide : 3 * c + (at + 1) * wide] = y
             for q in range(chunks):
                 y = x[q * rows : (q + 1) * rows].reshape(sources, part, wide)
                 if slot:
                     y = y + o_ref[q, :, :, c : c + wide]
                 o_ref[q, :, :, c : c + wide] = y
         for q in range(chunks):
-            copies.append(
-                pltpu.make_async_copy(
+            done.append(
+                copy(
                     o_ref.at[q, :, :, pl.ds(c, wide)],
                     out_ref.at[:, pl.ds(q * part, part), pl.ds(c, wide)],
-                    sem.at[2 + (c // wide) * chunks + q],
                 )
             )
-            copies[-1].start()
-    for copy in copies:
-        copy.wait()
-
-
-def whiten(res, tags, own, other, mine, centroids):
+    for one in done:
+        one.wait()
+
+
+def whiten(res, info, own, other, mine, centroids):
     chunks = len(res)
     sources, part, n = res[0].shape
     rows = chunks * sources * part
+    nb = n // BL
     vmem = pl.BlockSpec(memory_space=pltpu.VMEM)
-    hbm = pl.BlockSpec(memory_space=pl.ANY)
+    hbm = pl.BlockSpec(memory_space=pltpu.HBM)
     return pl.pallas_call(
         lambda *refs: whiten_body(n, chunks, *refs),
-        in_specs=[pl.BlockSpec(memory_space=pltpu.SMEM)] + [vmem] * (3 + 2 * chunks),
+        in_specs=[pl.BlockSpec(memory_space=pltpu.SMEM), vmem, vmem] + [hbm] * (2 + chunks),
         out_specs=[hbm, hbm],
         out_shape=[
             jax.ShapeDtypeStruct((sources, chunks * part, n), f32),
             jax.ShapeDtypeStruct((2, n, n), f32),
         ],
         scratch_shapes=[
-            pltpu.VMEM((2, n, n), f32),
+            pltpu.VMEM((2,) + own.shape, f32),
             pltpu.VMEM((chunks, sources, part, n), f32),
-            pltpu.VMEM((2, n, n), bf16),
-            pltpu.VMEM((2, n, n), bf16),
-            pltpu.VMEM((2, n, 2 * BL), bf16),
-            pltpu.VMEM((2, n, 2 * BL), bf16),
-            pltpu.VMEM((2, rows, n), bf16),
-            pltpu.VMEM((2, rows, n), bf16),
-            pltpu.SemaphoreType.DMA((2 + chunks * (n // (2 * BL)),)),
-        ],
-        compiler_params=pltpu.CompilerParams(vmem_limit_bytes=58 << 20),
+            pltpu.VMEM((BL, n - BL), f32),
+            pltpu.VMEM((chunks, sources, part, n), f32),
+            pltpu.VMEM((2, n, 3 * (n - 2 * BL)), bf16),
+            pltpu.VMEM((2, n, 6 * BL), bf16),
+            pltpu.VMEM((2, rows, 3 * (n - 2 * BL)), bf16),
+            pltpu.SemaphoreType.DMA((2 + chunks + 2 * (2 * nb - 1) + chunks * (nb // 2),)),
+        ],
         cost_estimate=pl.CostEstimate(flops=12 * rows * n * n, bytes_accessed=16 * n * n, transcendentals=0),
         name="whiten",
-    )(mine, centroids, own, other, *res, *tags)
+    )(mine, centroids, info, own, other, *res)
 
 
 def flip(x, axis, bit):
@@ -434,10 +500,10 @@
     return (lax.axis_index(axis) >> bit) & 1
 
 
-def halve(x, axis, bit, dim):
+def halve(terms, axis, bit, dim):
     b = bit_of(axis, bit)
-    got = flip(lax.dynamic_slice_in_dim(x, 1 - b, 1, dim), axis, bit)
-    return lax.dynamic_slice_in_dim(x, b, 1, dim) + got
+    got = flip(sum(lax.dynamic_slice_in_dim(x, 1 - b, 1, dim) for x in terms), axis, bit)
+    return (sum(lax.dynamic_slice_in_dim(x, b, 1, dim) for x in terms) + got,)
 
 
 def double(x, axis, bit, dim):
@@ -446,19 +512,22 @@
     return jnp.where(low, jnp.concatenate([x, got], dim), jnp.concatenate([got, x], dim))
 
 
-def sum_and_share(parts, n_group, n_member):
+def sum_and_share(parts, n_group, n_member, before_last):
     gbits = n_group.bit_length() - 1
     mbits = n_member.bit_length() - 1
-    rows = parts[0].shape[1]
+    rows = parts[0][0].shape[1]
     shape = (2,) * gbits + (2,) * (mbits - 1)
     ghalf = [("group", b, gbits - 1 - b) for b in range(gbits)]
     mhalf = [("member", b, gbits + b - 1) for b in range(1, mbits)]
     plans = [ghalf + mhalf, mhalf[:1] + ghalf + mhalf[1:]]
     gathers = [mhalf[::-1], mhalf[:1] + mhalf[:0:-1]]
-    parts = [p.reshape(shape + (rows >> (mbits - 1), BL)) for p in parts]
+    parts = [tuple(x.reshape(shape + (rows >> (mbits - 1), BL)) for x in terms) for terms in parts]
     for step in range(gbits + mbits - 1):
         parts = [halve(parts[c], *plans[c][step]) for c in range(2)]
+    parts = [sum(terms) for terms in parts]
     for step in range(mbits - 1):
+        if step == mbits - 2:
+            parts = before_last(parts)
         parts = [double(parts[c], *gathers[c][step]) for c in range(2)]
     return [p.reshape(rows, BL) for p in parts]
 
@@ -498,21 +567,25 @@
     first = to_owners(outgoing[0])
     away = gram(vectors, code, seen, n_group, 1)
     kept = gram(vectors, code, seen, n_group, 0)
-    parts = [k + flip(x, "member", 0) for k, x in zip(kept, away)]
+    parts = [(k, flip(x, "member", 0)) for k, x in zip(kept, away)]
     info, first = lax.optimization_barrier((info.reshape(devices, 1, BL), first))
     info = to_owners(info)[:, 0]
-    pa, pb = sum_and_share(parts, n_group, n_member)
-    tags = [info[:, c : c + chunk].reshape(-1, 1) for c in range(0, capacity, chunk)]
     counts = jnp.sum(info[:, capacity : capacity + lists], axis=0).astype(f32)
     count = lax.dynamic_index_in_dim(counts, core, 0, keepdims=True)
     scale = 1.0 / jnp.maximum(count, 1.0)
     arrived = [first]
-    for later in outgoing[1:]:
-        later, scale, pa, pb = lax.optimization_barrier((later, scale, pa, pb))
-        arrived.append(to_owners(later))
+
+    def before_last(parts):
+        nonlocal scale
+        for later in outgoing[1:]:
+            later, scale, *parts = lax.optimization_barrier((later, scale, *parts))
+            arrived.append(to_owners(later))
+        return parts
+
+    pa, pb = sum_and_share(parts, n_group, n_member, before_last)
     own = chol(pa, pb, scale, width)
     other = flip(own, "member", 0)
-    result, factors = whiten(arrived, tags, own, other, core.reshape(1), centroids)
+    result, factors = whiten(arrived, info, own, other, core.reshape(1), centroids)
     return (result.reshape(devices * capacity, width), factors)
 
 

time: 246 us -> 243 us (0.988)
  the two profiles are of different devices: /device:TPU:0 before, /device:TPU:29 now
where the time goes in v4:
time: 243 us; the launch traced here: 242 us
  waiting for transfers between devices  104 us (43%)
  Pallas kernels  83.8 us (34%)
  starting transfers between devices  31.8 us (13%)
  other arithmetic  18.1 us (7%)
  local copies, waits for them, and re-layouts  2.92 us (1%)
    ppermute x17, waiting for transfers between devices, flip(): return lax.ppermute(x, axis, [(i, i ^ 1 << bit) for i in range(size)])  104 us
    pallas_call x1, Pallas kernels, chol(): pl.pallas_call(lambda *refs: chol_body(n, *refs), in_specs=[pl.BlockSpec(...  35.2 us
    pallas_call x1, Pallas kernels, whiten(): pl.pallas_call(lambda *refs: whiten_body(n, chunks, *refs), in_specs=[pl....  23.8 us
    all_to_all x3, starting transfers between devices, to_owners(): lax.all_to_all(x, ('group', 'member'), split_axis=0, concat_axis=0, tiled...  19.1 us
    pallas_call x2, Pallas kernels, gram(): pl.pallas_call(lambda *refs: gram_body(rel, *refs), grid=(n_group,), in_s...  16.2 us
    ppermute x17, starting transfers between devices, flip(): return lax.ppermute(x, axis, [(i, i ^ 1 << bit) for i in range(size)])  12.5 us
    pallas_call x1, Pallas kernels, route(): pl.pallas_call(lambda *refs: route_body(sizes, *refs), in_specs=[pl.Block...  8.63 us
    add x2, other arithmetic, halve(): sum((lax.dynamic_slice_in_dim(x, 1 - b, 1, dim) for x in terms))  6.05 us
  transfers between devices with their start and end apart: 21, of which 12 were waited for; matrix products, arithmetic and copies ran while one was open for 8% of the time, Pallas kernels for 21%

profile of v4, /device:TPU:29, one launch (start us, length us, event | category | flops | bytes accessed | tf_op | source)
XLA Modules:
  0.0 242.4 jit_solution(6205605401134706592)
XLA Ops:
  0.6 0.3 collective-permute-start
  0.9 0.6 pad_add_fusion.refs_0_
  1.5 8.6 %route.1 = (f32[512,1024]{1,0:T(8,128)}, f32[512,1024]{1,0:T(8,128)}, f32[512,1024]{1,0:T(8,128)}, s32[32,128]{1,0:T(8,128)}, s32[8,512]{1,0:T(8,128)}) custom-call(s32[2]{0:T(128)} %pad_add_fusion.refs_0_, f32[512,1024]{1,0:T(8,128)} %refs_1_.2, s32[1,512]{1,0:T(1,128)} %bitcast.41, s32[1,512]{1,0:T(1,128)} %bitcast.42, s32[1,512]{1,0:T(1,128)} %bitcast.43, ...), custom_call_target="tpu_custom_call" | custom-call | flops 3221225472 | bytes 4194304 | tf_op jit(solution)/shard_map/route/pallas_call | solution.py:127
  10.2 0.1 pad.34.clone
  10.2 0.7 maximum_maximum_fusion.refs_2_
  10.9 8.1 %gram.3 = (f32[2,2304,128]{2,1,0:T(8,128)}, f32[2,2304,128]{2,1,0:T(8,128)}) custom-call(f32[512,1024]{1,0:T(8,128)} %get-tuple-element.23.refs_0_, s32[8,512]{1,0:T(8,128)} %get-tuple-element.24.refs_1_, f32[8,1024]{1,0:T(8,128)} %maximum_maximum_fusion.refs_2_), custom_call_target="tpu_custom_call" | custom-call | flops 3221225472 | bytes 6815744 | tf_op jit(solution)/shard_map/gram/pallas_call | solution.py:184
  19.0 0.9 collective-permute-start.8
  19.9 6.1 %all-to-all-start = ((f32[32,16,1024]{2,1,0:T(8,128)}), f32[32,16,1024]{2,1,0:T(8,128)}, u32[]{:S(2)}, u32[]{:S(2)}) async-start(f32[32,16,1024]{2,1,0:T(8,128)} %bitcast.31), calls=%async_computation | async-start | bytes 4194304 | tf_op jit(solution)/shard_map/all_to_all | solution.py:536
  26.0 8.1 %gram.2 = (f32[2,2304,128]{2,1,0:T(8,128)}, f32[2,2304,128]{2,1,0:T(8,128)}) custom-call(f32[512,1024]{1,0:T(8,128)} %get-tuple-element.23.refs_0_, s32[8,512]{1,0:T(8,128)} %get-tuple-element.24.refs_1_, f32[8,1024]{1,0:T(8,128)} %maximum_maximum_fusion.refs_2_), custom_call_target="tpu_custom_call" | custom-call | flops 3221225472 | bytes 6815744 | tf_op jit(solution)/shard_map/gram/pallas_call | solution.py:184
  34.2 2.8 %dynamic-slice_add_fusion = f32[2,1,2,2,288,128]{5,4,3,2,1,0:T(8,128)} fusion(f32[2,2,2,2,288,128]{5,4,3,2,1,0:T(8,128)} %bitcast.16, s32[]{:T(128)S(6)} %select_n.178, f32[2,2,2,2,288,128]{5,4,3,2,1,0:T(8,128)} %bitcast.29), kind=kLoop, calls=%fused_computation.2 | loop fusion | flops 294912 | bytes 3538948 | tf_op jit(solution)/shard_map/add | solution.py:505
  37.0 1.2 collective-permute-start.9
  38.2 3.3 %dynamic-slice_add_fusion.1 = f32[1,2,2,2,288,128]{5,4,3,2,1,0:T(8,128)} fusion(f32[2,2,2,2,288,128]{5,4,3,2,1,0:T(8,128)S(1)} %bitcast.25, s32[]{:T(128)S(6)} %select_n.176, f32[2,2,2,2,288,128]{5,4,3,2,1,0:T(8,128)} %bitcast.27), kind=kLoop, calls=%fused_computation.4 | loop fusion | flops 294912 | bytes 3538948 | tf_op jit(solution)/shard_map/add | solution.py:505
  41.4 0.2 collective-permute-start.2
  41.7 35.2 %collective-permute-done.9 = f32[2,1,2,2,288,128]{5,4,3,2,1,0:T(8,128)S(1)} collective-permute-done((f32[2,1,2,2,288,128]{5,4,3,2,1,0:T(8,128)}, f32[2,1,2,2,288,128]{5,4,3,2,1,0:T(8,128)S(1)}, u32[]{:S(2)}, u32[]{:S(2)}) %collective-permute-start.9) | collective-permute-done | bytes 1179680 | tf_op jit(solution)/shard_map/ppermute | solution.py:496
  76.9 2.0 add_add_fusion
  78.9 0.3 collective-permute-start.10
  79.2 0.7 copy-done.2
  80.0 1.5 add_add_fusion.1
  81.5 0.1 collective-permute-start.3
  81.6 6.3 %all-to-all-start.1 = ((s32[32,1,128]{2,1,0:T(1,128)}), s32[32,1,128]{2,1,0:T(1,128)S(1)}, u32[]{:S(2)}, u32[]{:S(2)}) async-start(s32[32,1,128]{2,1,0:T(1,128)} %bitcast.40), calls=%async_computation.1 | async-start | bytes 32768 | tf_op jit(solution)/shard_map/all_to_all | solution.py:536
  88.0 5.7 %collective-permute-done.10 = f32[1,1,2,2,288,128]{5,4,3,2,1,0:T(8,128)} collective-permute-done((f32[1,1,2,2,288,128]{5,4,3,2,1,0:T(8,128)S(1)}, f32[1,1,2,2,288,128]{5,4,3,2,1,0:T(8,128)}, u32[]{:S(2)}, u32[]{:S(2)}) %collective-permute-start.10) | collective-permute-done | bytes 589856 | tf_op jit(solution)/shard_map/ppermute | solution.py:496
  93.7 1.1 dynamic-slice_add_fusion.2
  94.9 0.1 collective-permute-start.11
  94.9 1.4 collective-permute-done.3
  96.3 1.1 dynamic-slice_add_fusion.3
  97.5 0.1 collective-permute-start.4
  97.6 4.6 %collective-permute-done.11 = f32[1,1,1,2,288,128]{5,4,3,2,1,0:T(8,128)S(1)} collective-permute-done((f32[1,1,1,2,288,128]{5,4,3,2,1,0:T(8,128)S(1)}, f32[1,1,1,2,288,128]{5,4,3,2,1,0:T(8,128)S(1)}, u32[]{:S(2)}, u32[]{:S(2)}) %collective-permute-start.11) | collective-permute-done | bytes 294944 | tf_op jit(solution)/shard_map/ppermute | solution.py:496
  102.3 0.6 collective-permute-start.12
  102.9 7.2 %collective-permute-done.4 = f32[1,1,1,2,288,128]{5,4,3,2,1,0:T(8,128)S(1)} collective-permute-done((f32[1,1,1,2,288,128]{5,4,3,2,1,0:T(8,128)S(1)}, f32[1,1,1,2,288,128]{5,4,3,2,1,0:T(8,128)S(1)}, u32[]{:S(2)}, u32[]{:S(2)}) %collective-permute-start.4) | collective-permute-done | bytes 294944 | tf_op jit(solution)/shard_map/ppermute | solution.py:496
  110.2 0.1 collective-permute-start.5
  110.4 9.0 %collective-permute-done.5 = f32[1,1,1,1,288,128]{5,4,3,2,1,0:T(8,128)S(1)} collective-permute-done((f32[1,1,1,1,288,128]{5,4,3,2,1,0:T(8,128)S(1)}, f32[1,1,1,1,288,128]{5,4,3,2,1,0:T(8,128)S(1)}, u32[]{:S(2)}, u32[]{:S(2)}) %collective-permute-start.5) | collective-permute-done | bytes 147488 | tf_op jit(solution)/shard_map/ppermute | solution.py:496
  119.6 0.1 slice_reduce_fusion
  119.7 0.6 dynamic_slice.64
  121.0 2.4 collective-permute-start.14
  123.4 10.5 %collective-permute-done.6 = f32[1,1,1,1,288,128]{5,4,3,2,1,0:T(8,128)S(1)} collective-permute-done((f32[1,1,1,1,288,128]{5,4,3,2,1,0:T(8,128)S(1)}, f32[1,1,1,1,288,128]{5,4,3,2,1,0:T(8,128)S(1)}, u32[]{:S(2)}, u32[]{:S(2)}) %collective-permute-start.6) | collective-permute-done | bytes 147488 | tf_op jit(solution)/shard_map/ppermute | solution.py:496
  134.1 6.2 %collective-permute-done.14 = f32[1,2,1,1,288,128]{5,4,3,2,1,0:T(8,128)S(1)} collective-permute-done((f32[1,2,1,1,288,128]{5,4,3,2,1,0:T(8,128)S(1)}, f32[1,2,1,1,288,128]{5,4,3,2,1,0:T(8,128)S(1)}, u32[]{:S(2)}, u32[]{:S(2)}) %collective-permute-start.14) | collective-permute-done | bytes 294944 | tf_op jit(solution)/shard_map/ppermute | solution.py:496
  140.3 6.4 %collective-permute-done.7 = f32[1,1,1,2,288,128]{5,4,3,2,1,0:T(8,128)S(1)} collective-permute-done((f32[1,1,1,2,288,128]{5,4,3,2,1,0:T(8,128)S(1)}, f32[1,1,1,2,288,128]{5,4,3,2,1,0:T(8,128)S(1)}, u32[]{:S(2)}, u32[]{:S(2)}) %collective-permute-start.7) | collective-permute-done | bytes 294944 | tf_op jit(solution)/shard_map/ppermute | solution.py:496
  146.8 0.5 collective-permute-start.15
  147.3 6.6 %all-to-all-start.2 = ((f32[32,16,1024]{2,1,0:T(8,128)}), f32[32,16,1024]{2,1,0:T(8,128)S(1)}, u32[]{:S(2)}, u32[]{:S(2)}) async-start(f32[32,16,1024]{2,1,0:T(8,128)} %bitcast.9), calls=%async_computation.2 | async-start | bytes 4194304 | tf_op jit(solution)/shard_map/all_to_all | solution.py:536
  153.9 9.8 %collective-permute-done.15 = f32[1,1,2,2,288,128]{5,4,3,2,1,0:T(8,128)} collective-permute-done((f32[1,1,2,2,288,128]{5,4,3,2,1,0:T(8,128)S(1)}, f32[1,1,2,2,288,128]{5,4,3,2,1,0:T(8,128)}, u32[]{:S(2)}, u32[]{:S(2)}) %collective-permute-start.15) | collective-permute-done | bytes 589856 | tf_op jit(solution)/shard_map/ppermute | solution.py:496
  163.7 2.4 maximum_select_fusion
  166.0 2.2 collective-permute-done.16
  168.3 2.4 maximum_select_fusion.1
  170.6 35.2 %chol.1.refs_3_ = f32[6144,128]{1,0:T(8,128)} custom-call(f32[1]{0:T(128)S(6)} %div.3.refs_0_, f32[2304,128]{1,0:T(8,128)} %bitcast.34, f32[2304,128]{1,0:T(8,128)} %bitcast.35), custom_call_target="tpu_custom_call" | custom-call | flops 42949672960 | bytes 4718592 | tf_op jit(solution)/shard_map/chol/pallas_call | solution.py:334
  205.8 5.7 %collective-permute-start.17 = (f32[6144,128]{1,0:T(8,128)}, f32[6144,128]{1,0:T(8,128)}, u32[]{:S(2)}, u32[]{:S(2)}) collective-permute-start(f32[6144,128]{1,0:T(8,128)} %chol.1.refs_3_), channel_id=1, source_target_pairs={{0,1},{1,0},{2,3},{3,2},{4,5},{5,4},{6,7},{7,6},{8,9},{9,8},{10,11... | collective-permute-start | bytes 9437192 | tf_op jit(solution)/shard_map/ppermute | solution.py:496
  211.5 5.6 %collective-permute-done.17.refs_4_ = f32[6144,128]{1,0:T(8,128)} collective-permute-done((f32[6144,128]{1,0:T(8,128)}, f32[6144,128]{1,0:T(8,128)}, u32[]{:S(2)}, u32[]{:S(2)}) %collective-permute-start.17) | collective-permute-done | bytes 3145760 | tf_op jit(solution)/shard_map/ppermute | solution.py:496
  217.2 1.3 copy-done.3
  218.5 23.8 %whiten.1 = (f32[32,32,1024]{2,1,0:T(8,128)}, f32[2,1024,1024]{2,1,0:T(8,128)}) custom-call(s32[1]{0:T(128)} %bitcast.refs_0_, f32[2,1024]{1,0:T(2,128)} %refs_1_.3, s32[32,128]{1,0:T(8,128)} %bitcast.39, f32[6144,128]{1,0:T(8,128)} %chol.1.refs_3_, f32[6144,128]{1,0:T(8,128)} %collective-permute-done.17.refs_4_, f32[32,16,1024]{2,1,0:T(8,128)} %all-to-all-done.refs_5_, ...), custom_call_target="tpu_custom_call" | custom-call | flops 12884901888 | bytes 16777216 | tf_op jit(solution)/shard_map/whiten/pallas_call | solution.py:471
  (42 shorter events, 0.8 us)
Async XLA Ops:
  0.6 9.6 %collective-permute-start = (f32[2,1024]{1,0:T(2,128)}, f32[2,1024]{1,0:T(2,128)S(1)}, u32[]{:S(2)}, u32[]{:S(2)}) collective-permute-start(f32[2,1024]{1,0:T(2,128)} %refs_1_.3), channel_id=1, source_target_pairs={{0,16},{16,0},{1,17},{17,1},{2,18},{18,2},{3,19},{19,3},{4,20},{20... | collective-permute-start | bytes 24584 | tf_op jit(solution)/shard_map/ppermute | solution.py:551
  1.5 8.7 %copy-start.5 = (f32[2,1024]{1,0:T(2,128)S(1)}, f32[2,1024]{1,0:T(2,128)}, u32[]{:S(2)}) copy-start(f32[2,1024]{1,0:T(2,128)} %refs_1_.3) | copy-start | bytes 24580
  19.0 15.2 %collective-permute-start.8 = (f32[2,2304,128]{2,1,0:T(8,128)}, f32[2,2304,128]{2,1,0:T(8,128)}, u32[]{:S(2)}, u32[]{:S(2)}) collective-permute-start(f32[2,2304,128]{2,1,0:T(8,128)} %get-tuple-element.28), channel_id=1, source_target_pairs={{0,1},{1,0},{2,3},{3,2},{4,5},{5,4},{6,7},{7,6},{8,9},{9,8},{10,11... | collective-permute-start | bytes 7077896 | tf_op jit(solution)/shard_map/ppermute | solution.py:496
  19.9 18.2 %collective-permute-start.1 = (f32[2,2304,128]{2,1,0:T(8,128)}, f32[2,2304,128]{2,1,0:T(8,128)S(1)}, u32[]{:S(2)}, u32[]{:S(2)}) collective-permute-start(f32[2,2304,128]{2,1,0:T(8,128)} %get-tuple-element.26), channel_id=1, source_target_pairs={{0,1},{1,0},{2,3},{3,2},{4,5},{5,4},{6,7},{7,6},{8,9},{9,8},{10,11... | collective-permute-start | bytes 7077896 | tf_op jit(solution)/shard_map/ppermute | solution.py:496
  19.9 61.7 %all-to-all-start = ((f32[32,16,1024]{2,1,0:T(8,128)}), f32[32,16,1024]{2,1,0:T(8,128)}, u32[]{:S(2)}, u32[]{:S(2)}) async-start(f32[32,16,1024]{2,1,0:T(8,128)} %bitcast.31), calls=%async_computation | async-start | bytes 4194304 | tf_op jit(solution)/shard_map/all_to_all | solution.py:536
  37.0 39.9 %collective-permute-start.9 = (f32[2,1,2,2,288,128]{5,4,3,2,1,0:T(8,128)}, f32[2,1,2,2,288,128]{5,4,3,2,1,0:T(8,128)S(1)}, u32[]{:S(2)}, u32[]{:S(2)}) collective-permute-start(f32[2,1,2,2,288,128]{5,4,3,2,1,0:T(8,128)} %dynamic-slice_add_fusion), channel_id=1, source_target_pairs={{0,2},{1,3},{2,0},{3,1},{4,6},{5,7},{6,4},{7,5},{8,10},{9,11},{10,... | collective-permute-start | bytes 3538952 | tf_op jit(solution)/shard_map/ppermute | solution.py:496
  38.2 3.3 %copy-start = (f32[2,2304,128]{2,1,0:T(8,128)}, f32[2,2304,128]{2,1,0:T(8,128)S(1)}, u32[]{:S(2)}) copy-start(f32[2,2304,128]{2,1,0:T(8,128)S(1)} %collective-permute-done.1) | copy-start | bytes 7077892
  41.4 37.8 %collective-permute-start.2 = (f32[1,2,2,2,288,128]{5,4,3,2,1,0:T(8,128)}, f32[1,2,2,2,288,128]{5,4,3,2,1,0:T(8,128)}, u32[]{:S(2)}, u32[]{:S(2)}) collective-permute-start(f32[1,2,2,2,288,128]{5,4,3,2,1,0:T(8,128)} %dynamic-slice_add_fusion.1), channel_id=1, source_target_pairs={{0,16},{16,0},{1,17},{17,1},{2,18},{18,2},{3,19},{19,3},{4,20},{20... | collective-permute-start | bytes 3538952 | tf_op jit(solution)/shard_map/ppermute | solution.py:496
  76.9 2.4 copy-start.1
  76.9 3.1 %copy-start.2 = (f32[2,2304,128]{2,1,0:T(8,128)S(1)}, f32[2,2304,128]{2,1,0:T(8,128)}, u32[]{:S(2)}) copy-start(f32[2,2304,128]{2,1,0:T(8,128)} %get-tuple-element.25) | copy-start | bytes 7077892
  78.9 14.8 %collective-permute-start.10 = (f32[1,1,2,2,288,128]{5,4,3,2,1,0:T(8,128)S(1)}, f32[1,1,2,2,288,128]{5,4,3,2,1,0:T(8,128)}, u32[]{:S(2)}, u32[]{:S(2)}) collective-permute-start(f32[1,1,2,2,288,128]{5,4,3,2,1,0:T(8,128)S(1)} %constant_dynamic-slice_fusion.1), channel_id=1, source_target_pairs={{0,16},{16,0},{1,17},{17,1},{2,18},{18,2},{3,19},{19,3},{4,20},{20... | collective-permute-start | bytes 1769480 | tf_op jit(solution)/shard_map/ppermute | solution.py:496
  81.5 14.8 %collective-permute-start.3 = (f32[1,1,2,2,288,128]{5,4,3,2,1,0:T(8,128)S(1)}, f32[1,1,2,2,288,128]{5,4,3,2,1,0:T(8,128)}, u32[]{:S(2)}, u32[]{:S(2)}) collective-permute-start(f32[1,1,2,2,288,128]{5,4,3,2,1,0:T(8,128)S(1)} %constant_dynamic-slice_fusion.4), channel_id=1, source_target_pairs={{0,2},{1,3},{2,0},{3,1},{4,6},{5,7},{6,4},{7,5},{8,10},{9,11},{10,... | collective-permute-start | bytes 1769480 | tf_op jit(solution)/shard_map/ppermute | solution.py:496
  81.6 37.9 %all-to-all-start.1 = ((s32[32,1,128]{2,1,0:T(1,128)}), s32[32,1,128]{2,1,0:T(1,128)S(1)}, u32[]{:S(2)}, u32[]{:S(2)}) async-start(s32[32,1,128]{2,1,0:T(1,128)} %bitcast.40), calls=%async_computation.1 | async-start | bytes 32768 | tf_op jit(solution)/shard_map/all_to_all | solution.py:536
  94.9 7.4 %collective-permute-start.11 = (f32[1,1,1,2,288,128]{5,4,3,2,1,0:T(8,128)S(1)}, f32[1,1,1,2,288,128]{5,4,3,2,1,0:T(8,128)S(1)}, u32[]{:S(2)}, u32[]{:S(2)}) collective-permute-start(f32[1,1,1,2,288,128]{5,4,3,2,1,0:T(8,128)S(1)} %constant_dynamic-slice_fusion), channel_id=1, source_target_pairs={{0,4},{1,5},{2,6},{3,7},{4,0},{5,1},{6,2},{7,3},{8,12},{9,13},{10,... | collective-permute-start | bytes 884744 | tf_op jit(solution)/shard_map/ppermute | solution.py:496
  97.5 12.7 %collective-permute-start.4 = (f32[1,1,1,2,288,128]{5,4,3,2,1,0:T(8,128)S(1)}, f32[1,1,1,2,288,128]{5,4,3,2,1,0:T(8,128)S(1)}, u32[]{:S(2)}, u32[]{:S(2)}) collective-permute-start(f32[1,1,1,2,288,128]{5,4,3,2,1,0:T(8,128)S(1)} %constant_dynamic-slice_fusion.3), channel_id=1, source_target_pairs={{0,4},{1,5},{2,6},{3,7},{4,0},{5,1},{6,2},{7,3},{8,12},{9,13},{10,... | collective-permute-start | bytes 884744 | tf_op jit(solution)/shard_map/ppermute | solution.py:496
  102.3 8.0 %collective-permute-start.12 = (f32[1,1,1,1,288,128]{5,4,3,2,1,0:T(8,128)S(1)}, f32[1,1,1,1,288,128]{5,4,3,2,1,0:T(8,128)S(1)}, u32[]{:S(2)}, u32[]{:S(2)}) collective-permute-start(f32[1,1,1,1,288,128]{5,4,3,2,1,0:T(8,128)S(1)} %constant_dynamic-slice_fusion.5), channel_id=1, source_target_pairs={{0,8},{1,9},{2,10},{3,11},{4,12},{5,13},{6,14},{7,15},{8,0},{9,1},... | collective-permute-start | bytes 442376 | tf_op jit(solution)/shard_map/ppermute | solution.py:496
  110.2 9.2 %collective-permute-start.5 = (f32[1,1,1,1,288,128]{5,4,3,2,1,0:T(8,128)S(1)}, f32[1,1,1,1,288,128]{5,4,3,2,1,0:T(8,128)S(1)}, u32[]{:S(2)}, u32[]{:S(2)}) collective-permute-start(f32[1,1,1,1,288,128]{5,4,3,2,1,0:T(8,128)S(1)} %constant_dynamic-slice_fusion.2), channel_id=1, source_target_pairs={{0,8},{1,9},{2,10},{3,11},{4,12},{5,13},{6,14},{7,15},{8,0},{9,1},... | collective-permute-start | bytes 442376 | tf_op jit(solution)/shard_map/ppermute | solution.py:496
  110.3 10.6 %collective-permute-start.13 = (f32[1,1,1,1,288,128]{5,4,3,2,1,0:T(8,128)S(1)}, f32[1,1,1,1,288,128]{5,4,3,2,1,0:T(8,128)S(1)}, u32[]{:S(2)}, u32[]{:S(2)}) collective-permute-start(f32[1,1,1,1,288,128]{5,4,3,2,1,0:T(8,128)S(1)} %dynamic-slice_add_fusion.6), channel_id=1, source_target_pairs={{0,2},{1,3},{2,0},{3,1},{4,6},{5,7},{6,4},{7,5},{8,10},{9,11},{10,... | collective-permute-start | bytes 442376 | tf_op jit(solution)/shard_map/ppermute | solution.py:496
  119.5 14.4 %collective-permute-start.6 = (f32[1,1,1,1,288,128]{5,4,3,2,1,0:T(8,128)S(1)}, f32[1,1,1,1,288,128]{5,4,3,2,1,0:T(8,128)S(1)}, u32[]{:S(2)}, u32[]{:S(2)}) collective-permute-start(f32[1,1,1,1,288,128]{5,4,3,2,1,0:T(8,128)S(1)} %dynamic-slice_add_fusion.7), channel_id=1, source_target_pairs={{0,8},{1,9},{2,10},{3,11},{4,12},{5,13},{6,14},{7,15},{8,0},{9,1},... | collective-permute-start | bytes 442376 | tf_op jit(solution)/shard_map/ppermute | solution.py:496
  119.6 14.5 %copy-start.4 = (s32[32,1,128]{2,1,0:T(1,128)}, s32[32,1,128]{2,1,0:T(1,128)S(1)}, u32[]{:S(2)}) copy-start(s32[32,1,128]{2,1,0:T(1,128)S(1)} %all-to-all-done.1) | copy-start | bytes 49156
  121.0 19.3 %collective-permute-start.14 = (f32[1,2,1,1,288,128]{5,4,3,2,1,0:T(8,128)S(1)}, f32[1,2,1,1,288,128]{5,4,3,2,1,0:T(8,128)S(1)}, u32[]{:S(2)}, u32[]{:S(2)}) collective-permute-start(f32[1,2,1,1,288,128]{5,4,3,2,1,0:T(8,128)S(1)} %maximum_select_fusion.7), channel_id=1, source_target_pairs={{0,8},{1,9},{2,10},{3,11},{4,12},{5,13},{6,14},{7,15},{8,0},{9,1},... | collective-permute-start | bytes 884744 | tf_op jit(solution)/shard_map/ppermute | solution.py:496
  133.9 12.8 %collective-permute-start.7 = (f32[1,1,1,2,288,128]{5,4,3,2,1,0:T(8,128)S(1)}, f32[1,1,1,2,288,128]{5,4,3,2,1,0:T(8,128)S(1)}, u32[]{:S(2)}, u32[]{:S(2)}) collective-permute-start(f32[1,1,1,2,288,128]{5,4,3,2,1,0:T(8,128)S(1)} %maximum_select_fusion.5), channel_id=1, source_target_pairs={{0,4},{1,5},{2,6},{3,7},{4,0},{5,1},{6,2},{7,3},{8,12},{9,13},{10,... | collective-permute-start | bytes 884744 | tf_op jit(solution)/shard_map/ppermute | solution.py:496
  146.8 16.9 %collective-permute-start.15 = (f32[1,1,2,2,288,128]{5,4,3,2,1,0:T(8,128)S(1)}, f32[1,1,2,2,288,128]{5,4,3,2,1,0:T(8,128)}, u32[]{:S(2)}, u32[]{:S(2)}) collective-permute-start(f32[1,1,2,2,288,128]{5,4,3,2,1,0:T(8,128)S(1)} %maximum_select_fusion.2), channel_id=1, source_target_pairs={{0,2},{1,3},{2,0},{3,1},{4,6},{5,7},{6,4},{7,5},{8,10},{9,11},{10,... | collective-permute-start | bytes 1769480 | tf_op jit(solution)/shard_map/ppermute | solution.py:496
  147.3 21.0 %collective-permute-start.16 = (f32[1,2,1,2,288,128]{5,4,3,2,1,0:T(8,128)S(1)}, f32[1,2,1,2,288,128]{5,4,3,2,1,0:T(8,128)}, u32[]{:S(2)}, u32[]{:S(2)}) collective-permute-start(f32[1,2,1,2,288,128]{5,4,3,2,1,0:T(8,128)S(1)} %maximum_select_fusion.3), channel_id=1, source_target_pairs={{0,4},{1,5},{2,6},{3,7},{4,0},{5,1},{6,2},{7,3},{8,12},{9,13},{10,... | collective-permute-start | bytes 1769480 | tf_op jit(solution)/shard_map/ppermute | solution.py:496
  147.3 69.9 %all-to-all-start.2 = ((f32[32,16,1024]{2,1,0:T(8,128)}), f32[32,16,1024]{2,1,0:T(8,128)S(1)}, u32[]{:S(2)}, u32[]{:S(2)}) async-start(f32[32,16,1024]{2,1,0:T(8,128)} %bitcast.9), calls=%async_computation.2 | async-start | bytes 4194304 | tf_op jit(solution)/shard_map/all_to_all | solution.py:536
  205.8 11.4 %collective-permute-start.17 = (f32[6144,128]{1,0:T(8,128)}, f32[6144,128]{1,0:T(8,128)}, u32[]{:S(2)}, u32[]{:S(2)}) collective-permute-start(f32[6144,128]{1,0:T(8,128)} %chol.1.refs_3_), channel_id=1, source_target_pairs={{0,1},{1,0},{2,3},{3,2},{4,5},{5,4},{6,7},{7,6},{8,9},{9,8},{10,11... | collective-permute-start | bytes 9437192 | tf_op jit(solution)/shard_map/ppermute | solution.py:496
  217.2 1.3 copy-start.3

commit v5 on v4

--- a/solution.py
+++ b/solution.py
@@ -195,6 +195,7 @@
             pltpu.VMEM((n, 3 * rows), bf16),
             pltpu.VMEM((3 * rows, n), bf16),
         ],
+        compiler_params=pltpu.CompilerParams(vmem_limit_bytes=24 << 20),
         cost_estimate=pl.CostEstimate(
             flops=3 * n_group * rows * n * n, bytes_accessed=4 * (rows * n + 2 * n_group * size * BL), transcendentals=0
         ),
@@ -309,17 +310,16 @@
                     out_ref[q : q + BL, :] = -dot3(t_ref[...], x)
                 th, tl = split(t_ref[...])
                 tcat = jnp.concatenate([th, tl, th, tl], axis=1)
-                for i in range(c, n, BL):
-                    ah, al = split(w_ref[i : i + BL, c : c + BL])
-                    x = dot_nt(jnp.concatenate([ah, ah, al, al], axis=1), tcat)
-                    if i == c:
-                        x = jnp.where(row >= col, x, 0.0)
-                    p = place[(i // BL, kk)]
-                    out_ref[p * BL : (p + 1) * BL, :] = x
-                    if i > c:
-                        xh, xl = split(x)
-                        h1_ref[i : i + BL, :] = jnp.concatenate([xh, xh, xl, xl], axis=1)
-                        h2_ref[i : i + BL, :] = jnp.concatenate([xh, xl, xh, xl], axis=1)
+                ah, al = split(w_ref[c:n, c : c + BL])
+                x = dot_nt(jnp.concatenate([ah, ah, al, al], axis=1), tcat)
+                p = place[(kk, kk)] * BL
+                out_ref[p : p + BL, :] = jnp.where(row >= col, x[:BL], 0.0)
+                if kk + 1 < nb:
+                    x = x[BL:]
+                    out_ref[p + BL : p + n - c, :] = x
+                    xh, xl = split(x)
+                    h1_ref[c + BL : n, :] = jnp.concatenate([xh, xh, xl, xl], axis=1)
+                    h2_ref[c + BL : n, :] = jnp.concatenate([xh, xl, xh, xl], axis=1)
                 j = c + BL
                 while j < n:
                     wide = BL if (j // BL) % 2 == 1 else 2 * BL
@@ -353,10 +353,65 @@
     )(scale, pa, pb)
 
 
+def tall(x):
+    hi, lo = split(x)
+    return jnp.concatenate([hi, hi, lo], axis=0)
+
+
+def flat(x):
+    hi, lo = split(x)
+    return jnp.concatenate([hi, lo, hi], axis=1)
+
+
+def invert_body(n, p_ref, out_ref, l_ref, x_ref):
+    order = blocks(n)
+    nb = n // BL
+    wide = 2 * BL
+    for p, (i, j) in enumerate(order):
+        if i // 2 != j // 2:
+            l_ref[i * BL : (i + 1) * BL, j * BL : (j + 1) * BL] = p_ref[p * BL : (p + 1) * BL, :]
+    x_ref[...] = jnp.zeros_like(x_ref)
+    for k in range(nb):
+        o = k * BL
+        p = (len(order) + k) * BL
+        x_ref[o : o + BL, o : o + BL] = p_ref[p : p + BL, :]
+        if k % 2:
+            p = (len(order) + nb + k // 2) * BL
+            x_ref[o : o + BL, o - BL : o] = p_ref[p : p + BL, :]
+    size = wide
+    while size < n:
+        for o in range(0, n, 2 * size):
+            m = o + size
+            e = m + size
+            y = dot_nn(flat(l_ref[m:e, o:m]), tall(x_ref[o:m, o:m]))
+            x_ref[m:e, o:m] = -dot_nn(flat(x_ref[m:e, m:e]), tall(y))
+        size *= 2
+    at = 0
+    for i in range(0, n, wide):
+        for j in range(0, i + wide, wide):
+            out_ref[at : at + wide, :] = x_ref[i : i + wide, j : j + wide]
+            at += wide
+
+
+def invert(pack, n):
+    m = n // (2 * BL)
+    size = m * (m + 1) // 2 * 2 * BL
+    vmem = pl.BlockSpec(memory_space=pltpu.VMEM)
+    return pl.pallas_call(
+        lambda *refs: invert_body(n, *refs),
+        in_specs=[vmem],
+        out_specs=vmem,
+        out_shape=jax.ShapeDtypeStruct((size, 2 * BL), f32),
+        scratch_shapes=[pltpu.VMEM((n, n), f32), pltpu.VMEM((n, n), f32)],
+        cost_estimate=pl.CostEstimate(flops=2 * n * n * n, bytes_accessed=4 * n * n, transcendentals=0),
+        name="invert",
+    )(pack)
+
+
 def whiten_body(n, chunks, *refs):
-    mine_ref, cent_ref, info_ref, own_hbm, other_hbm = refs[:5]
-    res_hbm = refs[5 : 5 + chunks]
-    out_ref, fac_ref, p_ref, r_ref, z_ref, o_ref, l_ref, t_ref, w_ref, sem = refs[5 + chunks :]
+    mine_ref, cent_ref, info_ref, own_hbm, other_hbm, own_inv, other_inv = refs[:7]
+    res_hbm = refs[7 : 7 + chunks]
+    out_ref, fac_ref, p_ref, x_ref, r_ref, z_ref, o_ref, a_ref, b_ref, sem = refs[7 + chunks :]
     order = blocks(n)
     place = {b: p for p, b in enumerate(order)}
     nb = n // BL
@@ -372,9 +427,10 @@
         one.start()
         return one
 
-    packs = [copy(own_hbm, p_ref.at[0])]
     moved = [copy(res_hbm[q], r_ref.at[q]) for q in range(chunks)]
-    packs.append(copy(other_hbm, p_ref.at[1]))
+    inverses = [copy(src, x_ref.at[slot]) for slot, src in enumerate((own_inv, other_inv))]
+    size = len(order) * BL
+    packs = [copy(src.at[pl.ds(0, size), :], p_ref.at[slot]) for slot, src in enumerate((own_hbm, other_hbm))]
     z_ref[...] = jnp.zeros_like(z_ref)
 
     low = part.bit_length() - 1
@@ -383,85 +439,64 @@
     spread = dot_nn(pick, info_ref[...].astype(f32).astype(bf16))
     k = lax.broadcasted_iota(jnp.int32, (rows, BL), 0) & (part - 1)
     lane = lax.broadcasted_iota(jnp.int32, (rows, BL), 1)
-    tags = [jnp.sum(jnp.where(lane == k + q * part, spread, 0.0), axis=1, keepdims=True) for q in range(chunks)]
-
+
+    for q in range(chunks):
+        moved[q].wait()
+        tag = jnp.sum(jnp.where(lane == k + q * part, spread, 0.0), axis=1, keepdims=True)
+        on = [tag == (which + 1).astype(f32) for which in (mine, 1 - mine)]
+        for c in range(0, n, wide):
+            x = r_ref[q, :, :, c : c + wide].reshape(rows, wide)
+            x = x - jnp.where(on[0], cent_ref[pl.ds(mine, 1), c : c + wide], cent_ref[pl.ds(1 - mine, 1), c : c + wide])
+            for slot in range(2):
+                hi, lo = split(jnp.where(on[slot], x, 0.0))
+                for at, y in enumerate((hi, lo, hi)):
+                    a_ref[slot, q * rows : (q + 1) * rows, 3 * c + at * wide : 3 * c + (at + 1) * wide] = y
+    for one in inverses:
+        one.wait()
     done = []
-    for slot, dst in enumerate((mine, 1 - mine)):
-        packs[slot].wait()
-        for j in range(nb):
-            p = place[(j, j)] * BL
-            done.append(
-                copy(
-                    p_ref.at[slot, pl.ds(p, n - j * BL), :],
-                    fac_ref.at[dst, pl.ds(j * BL, n - j * BL), pl.ds(j * BL, BL)],
-                )
-            )
-            if j + 1 < nb:
-                rest = n - (j + 1) * BL
-                done.append(
-                    copy(
-                        z_ref.at[:, pl.ds(0, rest)],
-                        fac_ref.at[dst, pl.ds(j * BL, BL), pl.ds((j + 1) * BL, rest)],
-                    )
-                )
-        for p, (i, j) in enumerate(order):
-            if i // 2 == j // 2:
-                continue
-            hi, lo = split(p_ref[slot, p * BL : (p + 1) * BL, :])
-            c = (j // 2) * 3 * wide + (j % 2) * BL
-            for at, x in enumerate((hi, hi, lo)):
-                l_ref[slot, i * BL : (i + 1) * BL, c + at * wide : c + at * wide + BL] = x
-        for k in range(nb):
-            p = (len(order) + k) * BL
-            c = (k % 2) * BL
-            hi, lo = split(p_ref[slot, p : p + BL, :])
-            if k % 2:
-                p = (len(order) + nb + k // 2) * BL
-                hi2, lo2 = split(p_ref[slot, p : p + BL, :])
-            else:
-                hi2 = lo2 = jnp.zeros((BL, BL), bf16)
-            for at, (x, y) in enumerate(((hi, hi2), (hi, hi2), (lo, lo2))):
-                t_ref[slot, k * BL : (k + 1) * BL, at * wide + c : at * wide + c + BL] = x
-                t_ref[slot, k * BL : (k + 1) * BL, at * wide + BL - c : at * wide + wide - c] = y
-
-    for one in moved:
-        one.wait()
+    at = 0
     for c in range(0, n, wide):
         for slot in range(2):
-            which = mine if slot == 0 else 1 - mine
-            prod = None
-            if c:
-                prod = dot_nt(w_ref[slot, :, : 3 * c], l_ref[slot, c : c + wide, : 3 * c])
-            accs = []
-            for q in range(chunks):
-                x = r_ref[q, :, :, c : c + wide].reshape(rows, wide)
-                x = jnp.where(tags[q] == (which + 1).astype(f32), x - cent_ref[pl.ds(which, 1), c : c + wide], 0.0)
-                if prod is not None:
-                    x = x - prod[q * rows : (q + 1) * rows]
-                accs.append(x)
-            ah, al = split(jnp.concatenate(accs, axis=0) if chunks > 1 else accs[0])
-            x = dot_nt(jnp.concatenate([ah, al, ah], axis=1), t_ref[slot, c : c + wide, :])
-            if c + wide < n:
-                hi, lo = split(x)
-                for at, y in enumerate((hi, lo, hi)):
-                    w_ref[slot, :, 3 * c + at * wide : 3 * c + (at + 1) * wide] = y
-            for q in range(chunks):
-                y = x[q * rows : (q + 1) * rows].reshape(sources, part, wide)
-                if slot:
-                    y = y + o_ref[q, :, :, c : c + wide]
-                o_ref[q, :, :, c : c + wide] = y
+            for j in range(0, c + wide, wide):
+                hi, lo = split(x_ref[slot, at + j : at + j + wide, :])
+                for t, y in enumerate((hi, hi, lo)):
+                    b_ref[slot, c : c + wide, 3 * j + t * wide : 3 * j + (t + 1) * wide] = y
+        at += c + wide
+        x = sum(
+            dot_nt(a_ref[slot, :, : 3 * (c + wide)], b_ref[slot, c : c + wide, : 3 * (c + wide)]) for slot in range(2)
+        )
         for q in range(chunks):
+            o_ref[q, :, :, c : c + wide] = x[q * rows : (q + 1) * rows].reshape(sources, part, wide)
             done.append(
                 copy(
                     o_ref.at[q, :, :, pl.ds(c, wide)],
                     out_ref.at[:, pl.ds(q * part, part), pl.ds(c, wide)],
                 )
             )
+        if c == 0:
+            for slot, dst in enumerate((mine, 1 - mine)):
+                packs[slot].wait()
+                for j in range(nb):
+                    p = place[(j, j)] * BL
+                    done.append(
+                        copy(
+                            p_ref.at[slot, pl.ds(p, n - j * BL), :],
+                            fac_ref.at[dst, pl.ds(j * BL, n - j * BL), pl.ds(j * BL, BL)],
+                        )
+                    )
+                    if j + 1 < nb:
+                        rest = n - (j + 1) * BL
+                        done.append(
+                            copy(
+                                z_ref.at[:, pl.ds(0, rest)],
+                                fac_ref.at[dst, pl.ds(j * BL, BL), pl.ds((j + 1) * BL, rest)],
+                            )
+                        )
     for one in done:
         one.wait()
 
 
-def whiten(res, info, own, other, mine, centroids):
+def whiten(res, info, own, other, own_inv, other_inv, mine, centroids):
     chunks = len(res)
     sources, part, n = res[0].shape
     rows = chunks * sources * part
@@ -470,25 +505,27 @@
     hbm = pl.BlockSpec(memory_space=pltpu.HBM)
     return pl.pallas_call(
         lambda *refs: whiten_body(n, chunks, *refs),
-        in_specs=[pl.BlockSpec(memory_space=pltpu.SMEM), vmem, vmem] + [hbm] * (2 + chunks),
+        in_specs=[pl.BlockSpec(memory_space=pltpu.SMEM), vmem, vmem]
+        + [pl.BlockSpec(memory_space=pl.ANY)] * (4 + chunks),
         out_specs=[hbm, hbm],
         out_shape=[
             jax.ShapeDtypeStruct((sources, chunks * part, n), f32),
             jax.ShapeDtypeStruct((2, n, n), f32),
         ],
         scratch_shapes=[
-            pltpu.VMEM((2,) + own.shape, f32),
+            pltpu.VMEM((2, len(blocks(n)) * BL, BL), f32),
+            pltpu.VMEM((2,) + own_inv.shape, f32),
             pltpu.VMEM((chunks, sources, part, n), f32),
             pltpu.VMEM((BL, n - BL), f32),
             pltpu.VMEM((chunks, sources, part, n), f32),
-            pltpu.VMEM((2, n, 3 * (n - 2 * BL)), bf16),
-            pltpu.VMEM((2, n, 6 * BL), bf16),
-            pltpu.VMEM((2, rows, 3 * (n - 2 * BL)), bf16),
-            pltpu.SemaphoreType.DMA((2 + chunks + 2 * (2 * nb - 1) + chunks * (nb // 2),)),
-        ],
+            pltpu.VMEM((2, rows, 3 * n), bf16),
+            pltpu.VMEM((2, n, 3 * n), bf16),
+            pltpu.SemaphoreType.DMA((4 + chunks + 2 * (2 * nb - 1) + chunks * (nb // 2),)),
+        ],
+        compiler_params=pltpu.CompilerParams(vmem_limit_bytes=50 << 20),
         cost_estimate=pl.CostEstimate(flops=12 * rows * n * n, bytes_accessed=16 * n * n, transcendentals=0),
         name="whiten",
-    )(mine, centroids, info, own, other, *res)
+    )(mine, centroids, info, own, other, own_inv, other_inv, *res)
 
 
 def flip(x, axis, bit):
@@ -512,7 +549,7 @@
     return jnp.where(low, jnp.concatenate([x, got], dim), jnp.concatenate([got, x], dim))
 
 
-def sum_and_share(parts, n_group, n_member, before_last):
+def sum_and_share(parts, n_group, n_member):
     gbits = n_group.bit_length() - 1
     mbits = n_member.bit_length() - 1
     rows = parts[0][0].shape[1]
@@ -526,8 +563,6 @@
         parts = [halve(parts[c], *plans[c][step]) for c in range(2)]
     parts = [sum(terms) for terms in parts]
     for step in range(mbits - 1):
-        if step == mbits - 2:
-            parts = before_last(parts)
         parts = [double(parts[c], *gathers[c][step]) for c in range(2)]
     return [p.reshape(rows, BL) for p in parts]
 
@@ -570,22 +605,19 @@
     parts = [(k, flip(x, "member", 0)) for k, x in zip(kept, away)]
     info, first = lax.optimization_barrier((info.reshape(devices, 1, BL), first))
     info = to_owners(info)[:, 0]
+    pa, pb = sum_and_share(parts, n_group, n_member)
     counts = jnp.sum(info[:, capacity : capacity + lists], axis=0).astype(f32)
     count = lax.dynamic_index_in_dim(counts, core, 0, keepdims=True)
     scale = 1.0 / jnp.maximum(count, 1.0)
     arrived = [first]
-
-    def before_last(parts):
-        nonlocal scale
-        for later in outgoing[1:]:
-            later, scale, *parts = lax.optimization_barrier((later, scale, *parts))
-            arrived.append(to_owners(later))
-        return parts
-
-    pa, pb = sum_and_share(parts, n_group, n_member, before_last)
+    for later in outgoing[1:]:
+        later, scale, pa, pb = lax.optimization_barrier((later, scale, pa, pb))
+        arrived.append(to_owners(later))
     own = chol(pa, pb, scale, width)
     other = flip(own, "member", 0)
-    result, factors = whiten(arrived, info, own, other, core.reshape(1), centroids)
+    own_inv = invert(own, width)
+    other_inv = flip(own_inv, "member", 0)
+    result, factors = whiten(arrived, info, own, other, own_inv, other_inv, core.reshape(1), centroids)
     return (result.reshape(devices * capacity, width), factors)
 
 

time: 243 us -> 242 us (level)
  the two profiles are of different devices: /device:TPU:29 before, /device:TPU:0 now
where the time goes in v5:
time: 242 us; the launch traced here: 241 us
  waiting for transfers between devices  89.4 us (37%)
  Pallas kernels  83.1 us (34%)
  starting transfers between devices  44.2 us (18%)
  other arithmetic  13.4 us (6%)
  local copies, waits for them, and re-layouts  9.46 us (4%)
    ppermute x18, waiting for transfers between devices, flip(): return lax.ppermute(x, axis, [(i, i ^ 1 << bit) for i in range(size)])  78.8 us
    pallas_call x1, Pallas kernels, chol(): pl.pallas_call(lambda *refs: chol_body(n, *refs), in_specs=[pl.BlockSpec(...  36.2 us
    ppermute x18, starting transfers between devices, flip(): return lax.ppermute(x, axis, [(i, i ^ 1 << bit) for i in range(size)])  27.4 us
    pallas_call x1, Pallas kernels, whiten(): pl.pallas_call(lambda *refs: whiten_body(n, chunks, *refs), in_specs=[pl....  20.3 us
    all_to_all x3, starting transfers between devices, to_owners(): lax.all_to_all(x, ('group', 'member'), split_axis=0, concat_axis=0, tiled...  13.7 us
    pallas_call x2, Pallas kernels, gram(): pl.pallas_call(lambda *refs: gram_body(rel, *refs), grid=(n_group,), in_s...  11.9 us
    all_to_all x3, waiting for transfers between devices, to_owners(): lax.all_to_all(x, ('group', 'member'), split_axis=0, concat_axis=0, tiled...  10.6 us
    pallas_call x1, Pallas kernels, route(): pl.pallas_call(lambda *refs: route_body(sizes, *refs), in_specs=[pl.Block...  8.72 us
  transfers between devices with their start and end apart: 22, of which 12 were waited for; matrix products, arithmetic and copies ran while one was open for 6% of the time, Pallas kernels for 23%

profile of v5, /device:TPU:0, one launch (start us, length us, event | category | flops | bytes accessed | tf_op | source)
XLA Modules:
  0.0 241.3 jit_solution(3575077847049387560)
XLA Ops:
  0.6 3.1 %collective-permute-start = (f32[2,1024]{1,0:T(2,128)}, f32[2,1024]{1,0:T(2,128)S(1)}, u32[]{:S(2)}, u32[]{:S(2)}) collective-permute-start(f32[2,1024]{1,0:T(2,128)} %refs_1_.3), channel_id=1, source_target_pairs={{0,16},{16,0},{1,17},{17,1},{2,18},{18,2},{3,19},{19,3},{4,20},{20... | collective-permute-start | bytes 24584 | tf_op jit(solution)/shard_map/ppermute | solution.py:586
  3.7 0.6 pad_add_fusion.refs_0_
  4.3 8.7 %route.1 = (f32[512,1024]{1,0:T(8,128)}, f32[512,1024]{1,0:T(8,128)}, f32[512,1024]{1,0:T(8,128)}, s32[32,128]{1,0:T(8,128)}, s32[8,512]{1,0:T(8,128)}) custom-call(s32[2]{0:T(128)} %pad_add_fusion.refs_0_, f32[512,1024]{1,0:T(8,128)} %refs_1_.2, s32[1,512]{1,0:T(1,128)} %bitcast.38, s32[1,512]{1,0:T(1,128)} %bitcast.39, s32[1,512]{1,0:T(1,128)} %bitcast.40, ...), custom_call_target="tpu_custom_call" | custom-call | flops 3221225472 | bytes 4194304 | tf_op jit(solution)/shard_map/route/pallas_call | solution.py:127
  13.2 1.6 copy-done.2
  14.8 0.7 copy-done.4
  15.5 6.5 %gram.3 = (f32[2,2304,128]{2,1,0:T(8,128)}, f32[2,2304,128]{2,1,0:T(8,128)}) custom-call(f32[512,1024]{1,0:T(8,128)S(1)} %copy-done.2, s32[8,512]{1,0:T(8,128)S(1)} %copy-done.4, f32[8,1024]{1,0:T(8,128)S(1)} %maximum_maximum_fusion.refs_2_), custom_call_target="tpu_custom_call" | custom-call | flops 3221225472 | bytes 6815744 | tf_op jit(solution)/shard_map/gram/pallas_call | solution.py:184
  22.5 1.6 copy-done.3
  24.1 5.5 %gram.2 = (f32[2,2304,128]{2,1,0:T(8,128)S(1)}, f32[2,2304,128]{2,1,0:T(8,128)S(1)}) custom-call(f32[512,1024]{1,0:T(8,128)S(1)} %copy-done.3, s32[8,512]{1,0:T(8,128)S(1)} %copy-done.5, f32[8,1024]{1,0:T(8,128)S(1)} %maximum_maximum_fusion.refs_2_), custom_call_target="tpu_custom_call" | custom-call | flops 3221225472 | bytes 6815744 | tf_op jit(solution)/shard_map/gram/pallas_call | solution.py:184
  29.6 2.3 dynamic-slice_add_fusion.1
  32.0 2.5 %dynamic-slice_add_fusion = f32[2,1,2,2,288,128]{5,4,3,2,1,0:T(8,128)} fusion(f32[2,2,2,2,288,128]{5,4,3,2,1,0:T(8,128)} %bitcast.17, s32[]{:T(128)S(6)} %select_n.195, f32[2,2,2,2,288,128]{5,4,3,2,1,0:T(8,128)S(1)} %bitcast.25), kind=kLoop, calls=%fused_computation.2 | loop fusion | flops 294912 | bytes 3538948 | tf_op jit(solution)/shard_map/add | solution.py:542
  34.5 2.0 collective-permute-start.10
  36.5 5.0 %all-to-all-start = ((f32[32,16,1024]{2,1,0:T(8,128)}), f32[32,16,1024]{2,1,0:T(8,128)}, u32[]{:S(2)}, u32[]{:S(2)}) async-start(f32[32,16,1024]{2,1,0:T(8,128)} %bitcast.31), calls=%async_computation | async-start | bytes 4194304 | tf_op jit(solution)/shard_map/all_to_all | solution.py:571
  41.5 30.6 %collective-permute-done.2 = f32[1,2,2,2,288,128]{5,4,3,2,1,0:T(8,128)} collective-permute-done((f32[1,2,2,2,288,128]{5,4,3,2,1,0:T(8,128)S(1)}, f32[1,2,2,2,288,128]{5,4,3,2,1,0:T(8,128)}, u32[]{:S(2)}, u32[]{:S(2)}) %collective-permute-start.2) | collective-permute-done | bytes 1179680 | tf_op jit(solution)/shard_map/ppermute | solution.py:533
  72.2 2.2 add_add_fusion.1
  74.3 0.9 constant_dynamic-slice_fusion.4
  75.2 1.6 collective-permute-start.3
  77.0 1.9 add_add_fusion
  79.0 1.0 copy-done.6
  80.0 2.1 collective-permute-start.11
  82.1 15.8 %collective-permute-done.3 = f32[1,1,2,2,288,128]{5,4,3,2,1,0:T(8,128)} collective-permute-done((f32[1,1,2,2,288,128]{5,4,3,2,1,0:T(8,128)}, f32[1,1,2,2,288,128]{5,4,3,2,1,0:T(8,128)}, u32[]{:S(2)}, u32[]{:S(2)}) %collective-permute-start.3) | collective-permute-done | bytes 589856 | tf_op jit(solution)/shard_map/ppermute | solution.py:533
  97.9 1.2 dynamic-slice_add_fusion.3
  99.1 1.8 collective-permute-start.4
  101.4 7.7 %collective-permute-done.4 = f32[1,1,1,2,288,128]{5,4,3,2,1,0:T(8,128)S(1)} collective-permute-done((f32[1,1,1,2,288,128]{5,4,3,2,1,0:T(8,128)S(1)}, f32[1,1,1,2,288,128]{5,4,3,2,1,0:T(8,128)S(1)}, u32[]{:S(2)}, u32[]{:S(2)}) %collective-permute-start.4) | collective-permute-done | bytes 294944 | tf_op jit(solution)/shard_map/ppermute | solution.py:533
  109.1 3.3 %collective-permute-start.5 = (f32[1,1,1,1,288,128]{5,4,3,2,1,0:T(8,128)S(1)}, f32[1,1,1,1,288,128]{5,4,3,2,1,0:T(8,128)S(1)}, u32[]{:S(2)}, u32[]{:S(2)}) collective-permute-start(f32[1,1,1,1,288,128]{5,4,3,2,1,0:T(8,128)S(1)} %constant_dynamic-slice_fusion.2), channel_id=1, source_target_pairs={{0,8},{1,9},{2,10},{3,11},{4,12},{5,13},{6,14},{7,15},{8,0},{9,1},... | collective-permute-start | bytes 442376 | tf_op jit(solution)/shard_map/ppermute | solution.py:533
  112.4 3.9 %collective-permute-done.12 = f32[1,1,1,2,288,128]{5,4,3,2,1,0:T(8,128)S(1)} collective-permute-done((f32[1,1,1,2,288,128]{5,4,3,2,1,0:T(8,128)S(1)}, f32[1,1,1,2,288,128]{5,4,3,2,1,0:T(8,128)S(1)}, u32[]{:S(2)}, u32[]{:S(2)}) %collective-permute-start.12) | collective-permute-done | bytes 294944 | tf_op jit(solution)/shard_map/ppermute | solution.py:533
  116.3 1.3 collective-permute-start.13
  117.7 2.2 collective-permute-start.6
  119.9 6.6 %collective-permute-done.13 = f32[1,1,1,1,288,128]{5,4,3,2,1,0:T(8,128)S(1)} collective-permute-done((f32[1,1,1,1,288,128]{5,4,3,2,1,0:T(8,128)S(1)}, f32[1,1,1,1,288,128]{5,4,3,2,1,0:T(8,128)S(1)}, u32[]{:S(2)}, u32[]{:S(2)}) %collective-permute-start.13) | collective-permute-done | bytes 147488 | tf_op jit(solution)/shard_map/ppermute | solution.py:533
  126.6 2.8 %collective-permute-start.14 = (f32[1,1,1,1,288,128]{5,4,3,2,1,0:T(8,128)S(1)}, f32[1,1,1,1,288,128]{5,4,3,2,1,0:T(8,128)S(1)}, u32[]{:S(2)}, u32[]{:S(2)}) collective-permute-start(f32[1,1,1,1,288,128]{5,4,3,2,1,0:T(8,128)S(1)} %dynamic-slice_add_fusion.6), channel_id=1, source_target_pairs={{0,2},{1,3},{2,0},{3,1},{4,6},{5,7},{6,4},{7,5},{8,10},{9,11},{10,... | collective-permute-start | bytes 442376 | tf_op jit(solution)/shard_map/ppermute | solution.py:533
  129.6 3.5 %collective-permute-start.7 = (f32[1,1,1,2,288,128]{5,4,3,2,1,0:T(8,128)S(1)}, f32[1,1,1,2,288,128]{5,4,3,2,1,0:T(8,128)S(1)}, u32[]{:S(2)}, u32[]{:S(2)}) collective-permute-start(f32[1,1,1,2,288,128]{5,4,3,2,1,0:T(8,128)S(1)} %maximum_select_fusion.5), channel_id=1, source_target_pairs={{0,4},{1,5},{2,6},{3,7},{4,0},{5,1},{6,2},{7,3},{8,12},{9,13},{10,... | collective-permute-start | bytes 884744 | tf_op jit(solution)/shard_map/ppermute | solution.py:533
  133.2 3.0 %collective-permute-start.15 = (f32[1,2,1,1,288,128]{5,4,3,2,1,0:T(8,128)S(1)}, f32[1,2,1,1,288,128]{5,4,3,2,1,0:T(8,128)S(1)}, u32[]{:S(2)}, u32[]{:S(2)}) collective-permute-start(f32[1,2,1,1,288,128]{5,4,3,2,1,0:T(8,128)S(1)} %maximum_select_fusion.7), channel_id=1, source_target_pairs={{0,8},{1,9},{2,10},{3,11},{4,12},{5,13},{6,14},{7,15},{8,0},{9,1},... | collective-permute-start | bytes 884744 | tf_op jit(solution)/shard_map/ppermute | solution.py:533
  136.2 8.1 %collective-permute-done.7 = f32[1,1,1,2,288,128]{5,4,3,2,1,0:T(8,128)S(1)} collective-permute-done((f32[1,1,1,2,288,128]{5,4,3,2,1,0:T(8,128)S(1)}, f32[1,1,1,2,288,128]{5,4,3,2,1,0:T(8,128)S(1)}, u32[]{:S(2)}, u32[]{:S(2)}) %collective-permute-start.7) | collective-permute-done | bytes 294944 | tf_op jit(solution)/shard_map/ppermute | solution.py:533
  144.3 1.6 collective-permute-start.8
  146.0 0.8 collective-permute-done.15
  146.9 0.6 collective-permute-start.16
  147.5 4.8 %all-to-all-start.1 = ((s32[32,1,128]{2,1,0:T(1,128)}), s32[32,1,128]{2,1,0:T(1,128)S(1)}, u32[]{:S(2)}, u32[]{:S(2)}) async-start(s32[32,1,128]{2,1,0:T(1,128)} %bitcast.7), calls=%async_computation.1 | async-start | bytes 32768 | tf_op jit(solution)/shard_map/all_to_all | solution.py:571
  152.3 9.9 %all-to-all-done.1 = s32[32,1,128]{2,1,0:T(1,128)S(1)} async-done(((s32[32,1,128]{2,1,0:T(1,128)}), s32[32,1,128]{2,1,0:T(1,128)S(1)}, u32[]{:S(2)}, u32[]{:S(2)}) %all-to-all-start.1) | async-done | bytes 16416 | tf_op jit(solution)/shard_map/all_to_all | solution.py:571
  162.3 0.6 dynamic_slice.64
  163.6 1.1 maximum_select_fusion
  164.7 1.1 maximum_select_fusion.1
  165.8 3.9 %all-to-all-start.2 = ((f32[32,16,1024]{2,1,0:T(8,128)}), f32[32,16,1024]{2,1,0:T(8,128)S(1)}, u32[]{:S(2)}, u32[]{:S(2)}) async-start(f32[32,16,1024]{2,1,0:T(8,128)} %bitcast.9), calls=%async_computation.2 | async-start | bytes 4194304 | tf_op jit(solution)/shard_map/all_to_all | solution.py:571
  169.8 36.2 %chol.1.refs_0_.refs_3_ = f32[6144,128]{1,0:T(8,128)} custom-call(f32[1]{0:T(128)S(6)} %div.3.refs_0_, f32[2304,128]{1,0:T(8,128)} %bitcast.34, f32[2304,128]{1,0:T(8,128)} %bitcast.35), custom_call_target="tpu_custom_call" | custom-call | flops 42949672960 | bytes 4718592 | tf_op jit(solution)/shard_map/chol/pallas_call | solution.py:334
  206.2 6.0 %invert.1.refs_5_ = f32[2560,256]{1,0:T(8,128)} custom-call(f32[6144,128]{1,0:T(8,128)} %chol.1.refs_0_.refs_3_), custom_call_target="tpu_custom_call" | custom-call | flops 2147483648 | bytes 4194304 | tf_op jit(solution)/shard_map/invert/pallas_call | solution.py:400
  212.4 4.9 %collective-permute-done.18.refs_6_ = f32[2560,256]{1,0:T(8,128)S(1)} collective-permute-done((f32[2560,256]{1,0:T(8,128)}, f32[2560,256]{1,0:T(8,128)S(1)}, u32[]{:S(2)}, u32[]{:S(2)}) %collective-permute-start.18) | collective-permute-done | bytes 2621472 | tf_op jit(solution)/shard_map/ppermute | solution.py:533
  217.3 1.5 copy-done.9
  218.8 0.7 all-to-all-done.2.refs_8_
  219.5 1.4 copy-done.8
  220.8 20.3 %whiten.1 = (f32[32,32,1024]{2,1,0:T(8,128)}, f32[2,1024,1024]{2,1,0:T(8,128)}) custom-call(s32[1]{0:T(128)} %bitcast.refs_0_, f32[2,1024]{1,0:T(2,128)S(1)} %copy-done.1, s32[32,128]{1,0:T(8,128)S(1)} %bitcast.30, f32[6144,128]{1,0:T(8,128)} %chol.1.refs_0_.refs_3_, f32[6144,128]{1,0:T(8,128)} %collective-permute-done.17.refs_4_, ...), custom_call_target="tpu_custom_call" | custom-call | flops 12884901888 | bytes 16777216 | tf_op jit(solution)/shard_map/whiten/pallas_call | solution.py:506
  (53 shorter events, 2.7 us)
Async XLA Ops:
  0.6 12.5 %collective-permute-start = (f32[2,1024]{1,0:T(2,128)}, f32[2,1024]{1,0:T(2,128)S(1)}, u32[]{:S(2)}, u32[]{:S(2)}) collective-permute-start(f32[2,1024]{1,0:T(2,128)} %refs_1_.3), channel_id=1, source_target_pairs={{0,16},{16,0},{1,17},{17,1},{2,18},{18,2},{3,19},{19,3},{4,20},{20... | collective-permute-start | bytes 24584 | tf_op jit(solution)/shard_map/ppermute | solution.py:586
  4.3 8.8 %copy-start.1 = (f32[2,1024]{1,0:T(2,128)S(1)}, f32[2,1024]{1,0:T(2,128)}, u32[]{:S(2)}) copy-start(f32[2,1024]{1,0:T(2,128)} %refs_1_.3) | copy-start | bytes 24580
  13.2 1.6 copy-start.2
  14.8 0.7 copy-start.4
  15.5 7.0 %copy-start.5 = (s32[8,512]{1,0:T(8,128)S(1)}, s32[8,512]{1,0:T(8,128)}, u32[]{:S(2)}) copy-start(s32[8,512]{1,0:T(8,128)} %get-tuple-element.24.refs_1_) | copy-start | bytes 49156
  22.0 7.6 %collective-permute-start.1 = (f32[2,2304,128]{2,1,0:T(8,128)}, f32[2,2304,128]{2,1,0:T(8,128)}, u32[]{:S(2)}, u32[]{:S(2)}) collective-permute-start(f32[2,2304,128]{2,1,0:T(8,128)} %get-tuple-element.26), channel_id=1, source_target_pairs={{0,1},{1,0},{2,3},{3,2},{4,5},{5,4},{6,7},{7,6},{8,9},{9,8},{10,11... | collective-permute-start | bytes 7077896 | tf_op jit(solution)/shard_map/ppermute | solution.py:533
  22.0 10.0 %collective-permute-start.9 = (f32[2,2304,128]{2,1,0:T(8,128)}, f32[2,2304,128]{2,1,0:T(8,128)}, u32[]{:S(2)}, u32[]{:S(2)}) collective-permute-start(f32[2,2304,128]{2,1,0:T(8,128)} %get-tuple-element.28), channel_id=1, source_target_pairs={{0,1},{1,0},{2,3},{3,2},{4,5},{5,4},{6,7},{7,6},{8,9},{9,8},{10,11... | collective-permute-start | bytes 7077896 | tf_op jit(solution)/shard_map/ppermute | solution.py:533
  22.5 1.6 copy-start.3
  29.5 2.4 copy-start
  31.9 40.2 %collective-permute-start.2 = (f32[1,2,2,2,288,128]{5,4,3,2,1,0:T(8,128)S(1)}, f32[1,2,2,2,288,128]{5,4,3,2,1,0:T(8,128)}, u32[]{:S(2)}, u32[]{:S(2)}) collective-permute-start(f32[1,2,2,2,288,128]{5,4,3,2,1,0:T(8,128)S(1)} %dynamic-slice_add_fusion.1), channel_id=1, source_target_pairs={{0,16},{16,0},{1,17},{17,1},{2,18},{18,2},{3,19},{19,3},{4,20},{20... | collective-permute-start | bytes 3538952 | tf_op jit(solution)/shard_map/ppermute | solution.py:533
  34.5 42.5 %collective-permute-start.10 = (f32[2,1,2,2,288,128]{5,4,3,2,1,0:T(8,128)}, f32[2,1,2,2,288,128]{5,4,3,2,1,0:T(8,128)}, u32[]{:S(2)}, u32[]{:S(2)}) collective-permute-start(f32[2,1,2,2,288,128]{5,4,3,2,1,0:T(8,128)} %dynamic-slice_add_fusion), channel_id=1, source_target_pairs={{0,2},{1,3},{2,0},{3,1},{4,6},{5,7},{6,4},{7,5},{8,10},{9,11},{10,... | collective-permute-start | bytes 3538952 | tf_op jit(solution)/shard_map/ppermute | solution.py:533
  36.5 111.0 %all-to-all-start = ((f32[32,16,1024]{2,1,0:T(8,128)}), f32[32,16,1024]{2,1,0:T(8,128)}, u32[]{:S(2)}, u32[]{:S(2)}) async-start(f32[32,16,1024]{2,1,0:T(8,128)} %bitcast.31), calls=%async_computation | async-start | bytes 4194304 | tf_op jit(solution)/shard_map/all_to_all | solution.py:571
  75.2 22.7 %collective-permute-start.3 = (f32[1,1,2,2,288,128]{5,4,3,2,1,0:T(8,128)}, f32[1,1,2,2,288,128]{5,4,3,2,1,0:T(8,128)}, u32[]{:S(2)}, u32[]{:S(2)}) collective-permute-start(f32[1,1,2,2,288,128]{5,4,3,2,1,0:T(8,128)} %constant_dynamic-slice_fusion.4), channel_id=1, source_target_pairs={{0,2},{1,3},{2,0},{3,1},{4,6},{5,7},{6,4},{7,5},{8,10},{9,11},{10,... | collective-permute-start | bytes 1769480 | tf_op jit(solution)/shard_map/ppermute | solution.py:533
  78.9 1.0 copy-start.6
  80.0 20.8 %collective-permute-start.11 = (f32[1,1,2,2,288,128]{5,4,3,2,1,0:T(8,128)S(1)}, f32[1,1,2,2,288,128]{5,4,3,2,1,0:T(8,128)S(1)}, u32[]{:S(2)}, u32[]{:S(2)}) collective-permute-start(f32[1,1,2,2,288,128]{5,4,3,2,1,0:T(8,128)S(1)} %constant_dynamic-slice_fusion.1), channel_id=1, source_target_pairs={{0,16},{16,0},{1,17},{17,1},{2,18},{18,2},{3,19},{19,3},{4,20},{20... | collective-permute-start | bytes 1769480 | tf_op jit(solution)/shard_map/ppermute | solution.py:533
  82.1 18.8 %copy-start.7 = (f32[2,1,2,2,288,128]{5,4,3,2,1,0:T(8,128)S(1)}, f32[2,1,2,2,288,128]{5,4,3,2,1,0:T(8,128)}, u32[]{:S(2)}) copy-start(f32[2,1,2,2,288,128]{5,4,3,2,1,0:T(8,128)} %copy-done.6) | copy-start | bytes 3538948
  99.1 9.9 %collective-permute-start.4 = (f32[1,1,1,2,288,128]{5,4,3,2,1,0:T(8,128)S(1)}, f32[1,1,1,2,288,128]{5,4,3,2,1,0:T(8,128)S(1)}, u32[]{:S(2)}, u32[]{:S(2)}) collective-permute-start(f32[1,1,1,2,288,128]{5,4,3,2,1,0:T(8,128)S(1)} %constant_dynamic-slice_fusion.3), channel_id=1, source_target_pairs={{0,4},{1,5},{2,6},{3,7},{4,0},{5,1},{6,2},{7,3},{8,12},{9,13},{10,... | collective-permute-start | bytes 884744 | tf_op jit(solution)/shard_map/ppermute | solution.py:533
  101.0 15.3 %collective-permute-start.12 = (f32[1,1,1,2,288,128]{5,4,3,2,1,0:T(8,128)S(1)}, f32[1,1,1,2,288,128]{5,4,3,2,1,0:T(8,128)S(1)}, u32[]{:S(2)}, u32[]{:S(2)}) collective-permute-start(f32[1,1,1,2,288,128]{5,4,3,2,1,0:T(8,128)S(1)} %constant_dynamic-slice_fusion), channel_id=1, source_target_pairs={{0,4},{1,5},{2,6},{3,7},{4,0},{5,1},{6,2},{7,3},{8,12},{9,13},{10,... | collective-permute-start | bytes 884744 | tf_op jit(solution)/shard_map/ppermute | solution.py:533
  109.1 8.6 %collective-permute-start.5 = (f32[1,1,1,1,288,128]{5,4,3,2,1,0:T(8,128)S(1)}, f32[1,1,1,1,288,128]{5,4,3,2,1,0:T(8,128)S(1)}, u32[]{:S(2)}, u32[]{:S(2)}) collective-permute-start(f32[1,1,1,1,288,128]{5,4,3,2,1,0:T(8,128)S(1)} %constant_dynamic-slice_fusion.2), channel_id=1, source_target_pairs={{0,8},{1,9},{2,10},{3,11},{4,12},{5,13},{6,14},{7,15},{8,0},{9,1},... | collective-permute-start | bytes 442376 | tf_op jit(solution)/shard_map/ppermute | solution.py:533
  116.3 10.2 %collective-permute-start.13 = (f32[1,1,1,1,288,128]{5,4,3,2,1,0:T(8,128)S(1)}, f32[1,1,1,1,288,128]{5,4,3,2,1,0:T(8,128)S(1)}, u32[]{:S(2)}, u32[]{:S(2)}) collective-permute-start(f32[1,1,1,1,288,128]{5,4,3,2,1,0:T(8,128)S(1)} %constant_dynamic-slice_fusion.5), channel_id=1, source_target_pairs={{0,8},{1,9},{2,10},{3,11},{4,12},{5,13},{6,14},{7,15},{8,0},{9,1},... | collective-permute-start | bytes 442376 | tf_op jit(solution)/shard_map/ppermute | solution.py:533
  117.7 11.9 %collective-permute-start.6 = (f32[1,1,1,1,288,128]{5,4,3,2,1,0:T(8,128)S(1)}, f32[1,1,1,1,288,128]{5,4,3,2,1,0:T(8,128)S(1)}, u32[]{:S(2)}, u32[]{:S(2)}) collective-permute-start(f32[1,1,1,1,288,128]{5,4,3,2,1,0:T(8,128)S(1)} %dynamic-slice_add_fusion.7), channel_id=1, source_target_pairs={{0,8},{1,9},{2,10},{3,11},{4,12},{5,13},{6,14},{7,15},{8,0},{9,1},... | collective-permute-start | bytes 442376 | tf_op jit(solution)/shard_map/ppermute | solution.py:533
  126.6 6.6 %collective-permute-start.14 = (f32[1,1,1,1,288,128]{5,4,3,2,1,0:T(8,128)S(1)}, f32[1,1,1,1,288,128]{5,4,3,2,1,0:T(8,128)S(1)}, u32[]{:S(2)}, u32[]{:S(2)}) collective-permute-start(f32[1,1,1,1,288,128]{5,4,3,2,1,0:T(8,128)S(1)} %dynamic-slice_add_fusion.6), channel_id=1, source_target_pairs={{0,2},{1,3},{2,0},{3,1},{4,6},{5,7},{6,4},{7,5},{8,10},{9,11},{10,... | collective-permute-start | bytes 442376 | tf_op jit(solution)/shard_map/ppermute | solution.py:533
  129.6 14.7 %collective-permute-start.7 = (f32[1,1,1,2,288,128]{5,4,3,2,1,0:T(8,128)S(1)}, f32[1,1,1,2,288,128]{5,4,3,2,1,0:T(8,128)S(1)}, u32[]{:S(2)}, u32[]{:S(2)}) collective-permute-start(f32[1,1,1,2,288,128]{5,4,3,2,1,0:T(8,128)S(1)} %maximum_select_fusion.5), channel_id=1, source_target_pairs={{0,4},{1,5},{2,6},{3,7},{4,0},{5,1},{6,2},{7,3},{8,12},{9,13},{10,... | collective-permute-start | bytes 884744 | tf_op jit(solution)/shard_map/ppermute | solution.py:533
  133.2 13.6 %collective-permute-start.15 = (f32[1,2,1,1,288,128]{5,4,3,2,1,0:T(8,128)S(1)}, f32[1,2,1,1,288,128]{5,4,3,2,1,0:T(8,128)S(1)}, u32[]{:S(2)}, u32[]{:S(2)}) collective-permute-start(f32[1,2,1,1,288,128]{5,4,3,2,1,0:T(8,128)S(1)} %maximum_select_fusion.7), channel_id=1, source_target_pairs={{0,8},{1,9},{2,10},{3,11},{4,12},{5,13},{6,14},{7,15},{8,0},{9,1},... | collective-permute-start | bytes 884744 | tf_op jit(solution)/shard_map/ppermute | solution.py:533
  144.3 19.3 %collective-permute-start.8 = (f32[1,1,2,2,288,128]{5,4,3,2,1,0:T(8,128)S(1)}, f32[1,1,2,2,288,128]{5,4,3,2,1,0:T(8,128)S(1)}, u32[]{:S(2)}, u32[]{:S(2)}) collective-permute-start(f32[1,1,2,2,288,128]{5,4,3,2,1,0:T(8,128)S(1)} %maximum_select_fusion.2), channel_id=1, source_target_pairs={{0,2},{1,3},{2,0},{3,1},{4,6},{5,7},{6,4},{7,5},{8,10},{9,11},{10,... | collective-permute-start | bytes 1769480 | tf_op jit(solution)/shard_map/ppermute | solution.py:533
  146.9 17.9 %collective-permute-start.16 = (f32[1,2,1,2,288,128]{5,4,3,2,1,0:T(8,128)S(1)}, f32[1,2,1,2,288,128]{5,4,3,2,1,0:T(8,128)S(1)}, u32[]{:S(2)}, u32[]{:S(2)}) collective-permute-start(f32[1,2,1,2,288,128]{5,4,3,2,1,0:T(8,128)S(1)} %maximum_select_fusion.3), channel_id=1, source_target_pairs={{0,4},{1,5},{2,6},{3,7},{4,0},{5,1},{6,2},{7,3},{8,12},{9,13},{10,... | collective-permute-start | bytes 1769480 | tf_op jit(solution)/shard_map/ppermute | solution.py:533
  147.5 14.7 %all-to-all-start.1 = ((s32[32,1,128]{2,1,0:T(1,128)}), s32[32,1,128]{2,1,0:T(1,128)S(1)}, u32[]{:S(2)}, u32[]{:S(2)}) async-start(s32[32,1,128]{2,1,0:T(1,128)} %bitcast.7), calls=%async_computation.1 | async-start | bytes 32768 | tf_op jit(solution)/shard_map/all_to_all | solution.py:571
  165.8 53.6 %all-to-all-start.2 = ((f32[32,16,1024]{2,1,0:T(8,128)}), f32[32,16,1024]{2,1,0:T(8,128)S(1)}, u32[]{:S(2)}, u32[]{:S(2)}) async-start(f32[32,16,1024]{2,1,0:T(8,128)} %bitcast.9), calls=%async_computation.2 | async-start | bytes 4194304 | tf_op jit(solution)/shard_map/all_to_all | solution.py:571
  205.9 12.8 %collective-permute-start.17 = (f32[6144,128]{1,0:T(8,128)}, f32[6144,128]{1,0:T(8,128)}, u32[]{:S(2)}, u32[]{:S(2)}) collective-permute-start(f32[6144,128]{1,0:T(8,128)} %chol.1.refs_0_.refs_3_), channel_id=1, source_target_pairs={{0,1},{1,0},{2,3},{3,2},{4,5},{5,4},{6,7},{7,6},{8,9},{9,8},{10,11... | collective-permute-start | bytes 9437192 | tf_op jit(solution)/shard_map/ppermute | solution.py:533
  212.2 5.1 %collective-permute-start.18 = (f32[2560,256]{1,0:T(8,128)}, f32[2560,256]{1,0:T(8,128)S(1)}, u32[]{:S(2)}, u32[]{:S(2)}) collective-permute-start(f32[2560,256]{1,0:T(8,128)} %invert.1.refs_5_), channel_id=1, source_target_pairs={{0,1},{1,0},{2,3},{3,2},{4,5},{5,4},{6,7},{7,6},{8,9},{9,8},{10,11... | collective-permute-start | bytes 7864328 | tf_op jit(solution)/shard_map/ppermute | solution.py:533
  217.3 1.5 copy-start.9
  219.4 1.4 copy-start.8
